TPU v7x, 32 devices: a whole 2x2x4 slice. The times are simulated.
32 devices in a mesh: dp: 16 (over z, y, x), tensor: 2 (over core).
Axes of the slice: x: 2, y: 2, z: 4, core: 2. Of those that a mesh axis runs over, the one named last changes fastest.
Arguments:
- inputs: bfloat16 [8192, 2048], P('dp'), may hold values from -6 to 6
- gamma_first: bfloat16 [2048], replicated, may hold values from 0.099609375 to 1.8984375
- beta_first: bfloat16 [2048], replicated, may hold values from -4 to 4
- heads_weight: bfloat16 [2048, 3, 2048], P('dp', None, 'tensor'), may hold values from -0.125 to 0.125
- output_weight: bfloat16 [2048, 2048], P('dp', 'tensor'), may hold values from -0.5 to 0.5
- output_bias: bfloat16 [2048], replicated, may hold values from -4 to 4
- gamma_second: bfloat16 [2048], replicated, may hold values from 0.099609375 to 1.8984375
- beta_second: bfloat16 [2048], replicated, may hold values from -4 to 4
- expand_weight: bfloat16 [2048, 8192], P('dp', 'tensor'), may hold values from -0.125 to 0.125
- expand_bias: bfloat16 [8192], P('tensor'), may hold values from -6 to 6
- reduce_weight: bfloat16 [2048, 8192], P('dp', 'tensor'), may hold values from -0.0625 to 0.0625
- reduce_bias: bfloat16 [2048], replicated, may hold values from -4 to 4
- group_sizes: int32 [32], P('dp'), may hold values from 4 to 16, as said below
- prefix_lengths: int32 [32], P('dp'), may hold values from 32 to 128, as said below
- solution_lengths: int32 [32, 16], P('dp'), may hold values from 1 to 221, as said below
- cotangent: bfloat16 [8192, 2048], P('dp'), may hold values from -6 to 6
Outputs:
- outputs: bfloat16 [8192, 2048], P('dp')
- input_gradient: bfloat16 [8192, 2048], P('dp')
- gamma_first_gradient: float32 [2048], P('dp')
- beta_first_gradient: float32 [2048], P('dp')
- heads_weight_gradient: float32 [2048, 3, 2048], P('dp', None, 'tensor')
- output_weight_gradient: float32 [2048, 2048], P('dp', 'tensor')
- output_bias_gradient: float32 [2048], P('dp')
- gamma_second_gradient: float32 [2048], P('dp')
- beta_second_gradient: float32 [2048], P('dp')
- expand_weight_gradient: float32 [2048, 8192], P('dp', 'tensor')
- expand_bias_gradient: float32 [2, 4096], P('tensor', 'dp')
- reduce_weight_gradient: float32 [2048, 8192], P('dp', 'tensor')
- reduce_bias_gradient: float32 [2048], P('dp')
Inputs may be any that keep to these rules, and one draw needn't show every extreme that they name: Each group has group_sizes solutions. `prefix_lengths`: A group's prefix and its first group_sizes solutions together take at most 256 token slots. `solution_lengths`: only a group's first group_sizes entries are used. The groups of a block fill at most 512 slots, and on at least one block exactly 512.
All inputs are finite; a program needn't handle non-finite values.
Results may differ from a plain program's by a relative error of at most 0.017.
Values may be sent and summed in bfloat16 or wider, within the bound.
No kernel may reach another device: no remote copies, remote signals or barrier semaphores. Data moves between devices by JAX's collectives and lax.ppermute only.
A program may use at most 384 MiB of HBM per device.

v0:
```python
import jax
import jax.numpy as jnp
from jax import lax
from jax.sharding import PartitionSpec as P

HEAD = 128


def layout(group_sizes, prefix_lengths, solution_lengths, row_count):
    entries = solution_lengths.shape[1]
    position = jnp.arange(entries, dtype=jnp.int32)
    counted = jnp.where(position[None, :] < group_sizes[:, None], solution_lengths, 0)
    pieces = jnp.concatenate([prefix_lengths[:, None], counted], axis=1).reshape(-1)
    bounds = jnp.cumsum(pieces)
    slot_index = jnp.arange(row_count, dtype=jnp.int32)
    piece_index = jnp.sum((slot_index[:, None] >= bounds[None, :]).astype(jnp.int32), axis=1)
    live_rows = piece_index < pieces.shape[0]
    group_index = piece_index // (entries + 1)
    opening = piece_index % (entries + 1) == 0
    same_group = (
        (group_index[:, None] == group_index[None, :]) & live_rows[:, None] & live_rows[None, :]
    )
    causal = slot_index[None, :] <= slot_index[:, None]
    visible = opening[None, :] | (piece_index[:, None] == piece_index[None, :])
    allowed = (slot_index[:, None] == slot_index[None, :]) | same_group & causal & visible
    return (allowed, live_rows)


def normalize(values, gain_vector, shift_vector):
    center = values - jnp.mean(values, axis=-1, keepdims=True)
    spread = jnp.mean(center * center, axis=-1, keepdims=True)
    return center * lax.rsqrt(spread + 1e-05) * gain_vector + shift_vector


def smooth(values):
    return jax.nn.gelu(values, approximate=True)


def body(
    inputs,
    gamma_first,
    beta_first,
    heads_weight,
    output_weight,
    output_bias,
    gamma_second,
    beta_second,
    expand_weight,
    expand_bias,
    reduce_weight,
    reduce_bias,
    group_sizes,
    prefix_lengths,
    solution_lengths,
    cotangent,
):
    row_count = inputs.shape[0]
    local_width = output_weight.shape[1]
    local_heads = local_width // HEAD
    score_scale = HEAD ** (-0.5)
    across = (((1,), (1,)), ((), ()))
    token_dims = (((0,), (0,)), ((), ()))
    allowed, live_rows = layout(group_sizes, prefix_lengths, solution_lengths, row_count)
    live_mask = live_rows.astype(jnp.float32)[:, None]
    gain_first = gamma_first.astype(jnp.float32)
    shift_first = beta_first.astype(jnp.float32)
    gain_second = gamma_second.astype(jnp.float32)
    shift_second = beta_second.astype(jnp.float32)
    residual = inputs.astype(jnp.float32)
    first_low = normalize(residual, gain_first, shift_first).astype(jnp.bfloat16)
    heads_full, output_full = (
        lax.all_gather(heads_weight, "dp", axis=0, tiled=True),
        lax.all_gather(output_weight, "dp", axis=0, tiled=True),
    )
    projected = jnp.einsum(
        "td,dch->tch", first_low, heads_full, preferred_element_type=jnp.float32
    ).astype(jnp.bfloat16)
    queries = projected[:, 0].reshape(row_count, local_heads, HEAD)
    keyset = projected[:, 1].reshape(row_count, local_heads, HEAD)
    valueset = projected[:, 2].reshape(row_count, local_heads, HEAD)

    def masked_scores():
        raw_scores = (
            jnp.einsum("qhe,khe->hqk", queries, keyset, preferred_element_type=jnp.float32)
            * score_scale
        )
        return jnp.where(allowed[None], raw_scores, -1e30)

    scores = masked_scores()
    row_peak = jnp.max(scores, axis=-1, keepdims=True)
    exponent = jnp.exp(scores - row_peak)
    row_total = jnp.sum(exponent, axis=-1, keepdims=True)
    soft_weights = exponent / row_total
    log_total = row_peak + jnp.log(row_total)
    soft_low = soft_weights.astype(jnp.bfloat16)
    mixed_heads = (
        jnp.einsum("hqk,khe->qhe", soft_low, valueset, preferred_element_type=jnp.float32)
        .reshape(row_count, local_width)
        .astype(jnp.bfloat16)
    )
    attended = lax.psum(
        lax.dot_general(mixed_heads, output_full, across, preferred_element_type=jnp.float32),
        "tensor",
    )
    middle = residual + attended + output_bias.astype(jnp.float32)
    second_low = normalize(middle, gain_second, shift_second).astype(jnp.bfloat16)
    columns = second_low
    hidden_sum = jnp.dot(
        columns,
        lax.all_gather(expand_weight, "dp", axis=0, tiled=True),
        preferred_element_type=jnp.float32,
    ) + expand_bias.astype(jnp.float32)
    hidden_low = smooth(hidden_sum).astype(jnp.bfloat16)
    branch = lax.psum(
        lax.dot_general(
            hidden_low,
            lax.all_gather(reduce_weight, "dp", axis=0, tiled=True),
            across,
            preferred_element_type=jnp.float32,
        ).astype(jnp.bfloat16),
        "tensor",
    ).astype(jnp.float32)
    outputs = (live_mask * (middle + branch + reduce_bias.astype(jnp.float32))).astype(jnp.bfloat16)
    upstream = live_mask * cotangent.astype(jnp.float32)
    reduce_bias_gradient = jnp.sum(upstream, axis=0)
    upstream_low = upstream.astype(jnp.bfloat16)
    columns = upstream_low
    hidden_tangent = jnp.dot(
        columns,
        lax.all_gather(reduce_weight, "dp", axis=0, tiled=True),
        preferred_element_type=jnp.float32,
    )
    _, smooth_pullback = jax.vjp(smooth, hidden_sum)
    sum_tangent = smooth_pullback(hidden_tangent)[0]
    expand_bias_gradient = jnp.sum(sum_tangent, axis=0)[None, :]
    sum_low = sum_tangent.astype(jnp.bfloat16)
    second_tangent = lax.psum(
        lax.dot_general(
            sum_low,
            lax.all_gather(expand_weight, "dp", axis=0, tiled=True),
            across,
            preferred_element_type=jnp.float32,
        ).astype(jnp.bfloat16),
        "tensor",
    ).astype(jnp.float32)
    feed_totals = lax.psum_scatter(
        jnp.stack(
            [
                lax.dot_general(
                    second_low, sum_low, token_dims, preferred_element_type=jnp.float32
                ),
                lax.dot_general(
                    upstream_low, hidden_low, token_dims, preferred_element_type=jnp.float32
                ),
            ],
            axis=1,
        ),
        "dp",
        scatter_dimension=0,
        tiled=True,
    )
    expand_share = feed_totals[:, 0]
    reduce_share = feed_totals[:, 1]
    _, second_pullback = jax.vjp(normalize, middle, gain_second, shift_second)
    middle_part, gamma_second_gradient, beta_second_gradient = second_pullback(second_tangent)
    middle_tangent = upstream + middle_part
    output_bias_gradient = jnp.sum(middle_tangent, axis=0)
    middle_low = middle_tangent.astype(jnp.bfloat16)
    mixed_tangent = (
        jnp.dot(middle_low, output_full, preferred_element_type=jnp.float32)
        .astype(jnp.bfloat16)
        .reshape(row_count, local_heads, HEAD)
    )
    soft_again = jnp.exp(masked_scores() - log_total)
    soft_again_low = soft_again.astype(jnp.bfloat16)
    value_tangent = jnp.einsum(
        "hqk,qhe->khe", soft_again_low, mixed_tangent, preferred_element_type=jnp.float32
    )
    weight_tangent = jnp.einsum(
        "qhe,khe->hqk", mixed_tangent, valueset, preferred_element_type=jnp.float32
    )
    score_tangent = (
        soft_again * (weight_tangent - jnp.sum(soft_again * weight_tangent, axis=-1, keepdims=True))
    ).astype(jnp.bfloat16)
    query_tangent = (
        jnp.einsum("hqk,khe->qhe", score_tangent, keyset, preferred_element_type=jnp.float32)
        * score_scale
    )
    key_tangent = (
        jnp.einsum("hqk,qhe->khe", score_tangent, queries, preferred_element_type=jnp.float32)
        * score_scale
    )
    projected_tangent = (
        jnp.stack([query_tangent, key_tangent, value_tangent], axis=1)
        .reshape(row_count, 3, local_width)
        .astype(jnp.bfloat16)
    )
    first_tangent = lax.psum(
        jnp.einsum(
            "tch,dch->td", projected_tangent, heads_full, preferred_element_type=jnp.float32
        ).astype(jnp.bfloat16),
        "tensor",
    ).astype(jnp.float32)
    heads_term = jnp.einsum(
        "tc,tkh->ckh", first_low, projected_tangent, preferred_element_type=jnp.float32
    )
    output_term = lax.dot_general(
        middle_low, mixed_heads, token_dims, preferred_element_type=jnp.float32
    )
    head_totals = lax.psum_scatter(
        jnp.concatenate([heads_term, output_term[:, None, :]], axis=1),
        "dp",
        scatter_dimension=0,
        tiled=True,
    )
    _, first_pullback = jax.vjp(normalize, residual, gain_first, shift_first)
    input_part, gamma_first_gradient, beta_first_gradient = first_pullback(first_tangent)
    input_gradient = (middle_tangent + input_part).astype(jnp.bfloat16)
    vectors = (
        lax.psum_scatter(gamma_first_gradient, "dp", scatter_dimension=0, tiled=True),
        lax.psum_scatter(beta_first_gradient, "dp", scatter_dimension=0, tiled=True),
        lax.psum_scatter(output_bias_gradient, "dp", scatter_dimension=0, tiled=True),
        lax.psum_scatter(gamma_second_gradient, "dp", scatter_dimension=0, tiled=True),
        lax.psum_scatter(beta_second_gradient, "dp", scatter_dimension=0, tiled=True),
        lax.psum_scatter(reduce_bias_gradient, "dp", scatter_dimension=0, tiled=True),
        lax.psum_scatter(expand_bias_gradient, "dp", scatter_dimension=1, tiled=True),
    )
    return (
        outputs,
        input_gradient,
        vectors[0],
        vectors[1],
        head_totals[:, :3],
        head_totals[:, 3],
        vectors[2],
        vectors[3],
        vectors[4],
        expand_share,
        vectors[6],
        reduce_share,
        vectors[5],
    )


def solution(mesh):
    placed = (
        P("dp", None),
        P(),
        P(),
        P("dp", None, "tensor"),
        P("dp", "tensor"),
        P(),
        P(),
        P(),
        P("dp", "tensor"),
        P("tensor"),
        P("dp", "tensor"),
        P(),
        P("dp"),
        P("dp"),
        P("dp", None),
        P("dp", None),
    )
    return jax.shard_map(
        body,
        mesh=mesh,
        in_specs=placed,
        out_specs=(
            P("dp", None),
            P("dp", None),
            P("dp"),
            P("dp"),
            P("dp", None, "tensor"),
            P("dp", "tensor"),
            P("dp"),
            P("dp"),
            P("dp"),
            P("dp", "tensor"),
            P("tensor", "dp"),
            P("dp", "tensor"),
            P("dp"),
        ),
        check_vma=False,
    )
```

profile of v0, /device:TPU:0, one launch (start us, length us, event | category | flops | bytes accessed | tf_op | source)
XLA Modules:
  0.0 2898.8 jit_solution(15388383072456782599)
XLA Ops:
  12.0 1.9 convert_reduce_fusion.2
  16.1 149.3 %all-gather.5.cloned.1.call-done = bf16[2048,3,1024]{2,0,1:T(8,128)(2,1)} async-done(((bf16[128,3,1024]{2,0,1:T(8,128)(2,1)}), bf16[2048,3,1024]{2,0,1:T(8,128)(2,1)}) %all-gather.5.cloned.1.call-update) | async-done | bytes 12582928 | tf_op jit(solution)/shard_map/all_gather | solution.py:72
  165.4 9.7 convolution_convert_fusion.2
  175.2 1.7 slice_bitcast_fusion.2
  178.1 1.5 copy.110
  179.7 2.7 copy.109
  182.3 2.9 fusion.66
  186.4 2.2 copy-done
  188.7 2.6 fusion.34
  191.3 51.2 %all-gather.7.cloned.1.call-done = bf16[2048,1024]{1,0:T(8,128)(2,1)} async-done(((bf16[128,1024]{1,0:T(8,128)(2,1)}), bf16[2048,1024]{1,0:T(8,128)(2,1)}) %all-gather.7.cloned.1.call-update) | async-done | bytes 4194320 | tf_op jit(solution)/shard_map/all_gather | solution.py:73
  242.5 6.8 fusion.68
  251.0 25.5 all-reduce.12.cloned.1.call-done
  276.5 2.8 fusion.64
  279.3 2.0 copy-done.1
  281.9 190.4 %all-gather.9.cloned.1.call-done = bf16[2048,4096]{1,0:T(8,128)(2,1)} async-done(((bf16[128,4096]{1,0:T(8,128)(2,1)}), bf16[2048,4096]{1,0:T(8,128)(2,1)}) %all-gather.9.cloned.1.call-update) | async-done | bytes 16777232 | tf_op jit(solution)/shard_map/all_gather | solution.py:110
  472.3 15.8 fusion.61
  488.1 177.0 %all-gather.11.cloned.1.call-done = bf16[2048,4096]{1,0:T(8,128)(2,1)} async-done(((bf16[128,4096]{1,0:T(8,128)(2,1)}), bf16[2048,4096]{1,0:T(8,128)(2,1)}) %all-gather.11.cloned.1.call-update) | async-done | bytes 16777232 | tf_op jit(solution)/shard_map/all_gather | solution.py:117
  665.1 18.5 fusion.67
  683.7 1.9 copy-done.44
  685.6 13.4 convolution_convert_fusion
  699.1 2.0 copy.107
  701.2 18.9 convolution_convert_fusion.1
  720.1 4.6 convert_reduce_fusion.1
  724.8 2.6 fusion.22
  727.4 2.8 fusion.62
  730.2 2.0 copy-done.8
  732.2 2.3 convolution_convert_fusion.3
  735.1 5.1 fusion.35
  740.2 5.0 multiply_reduce_fusion
  745.2 2.6 multiply_convert_fusion
  753.3 11.4 bitcast_convert_fusion
  764.8 5.1 convolution_bitcast_fusion.2
  770.0 12.0 fusion.38
  782.0 20.2 pad_maximum_fusion.1
  802.9 20.3 convolution_bitcast_fusion.1
  823.2 20.2 convolution_bitcast_fusion
  843.4 44.4 %pad_maximum_fusion = f32[2048,2,4096]{2,0,1:T(8,128)} fusion(f32[2048,1,4096]{2,0,1:T(8,128)} %convolution_bitcast_fusion, f32[2048,1,4096]{2,0,1:T(8,128)} %convolution_bitcast_fusion.1), kind=kLoop, calls=%fused_computation | loop fusion | flops 16777216 | bytes 134217728 | tf_op jit(solution)/shard_map/stack | solution.py:147
  889.8 1.6 copy.108
  891.3 2.9 convert_reduce_fusion
  894.3 2.4 fusion.23
  896.7 77.7 %all-reduce.6 = (f32[2048]{0:T(1024)S(1)}, f32[2048]{0:T(1024)S(1)}, f32[2048]{0:T(1024)S(1)}, f32[2048]{0:T(1024)S(1)}, f32[2048]{0:T(1024)S(1)}, /*index=5*/f32[2048]{0:T(1024)S(1)}) all-reduce(f32[2048]{0:T(1024)S(1)} %get-tuple-element.15, f32[2048]{0:T(1024)S(1)} %get-tuple-element.19, ...), channel_id=2, replica_groups=mesh['dp'=16,'tensor'=2] {'dp'}, use_global_device_ids=true, to_apply=%region_18.19.clone | all-reduce | flops 12288 | bytes 98304
  978.0 4.9 multiply_convert_fusion.2
  982.9 2.8 add_convert_fusion
  985.7 535.8 %reduce-scatter.6.cloned.1.call-done = f32[128,4,1024]{2,0,1:T(8,128)} async-done(((f32[2048,4,1024]{2,0,1:T(8,128)}), f32[128,4,1024]{2,0,1:T(8,128)}) %reduce-scatter.6.cloned.1.call-update) | async-done | bytes 2097168 | tf_op jit(solution)/shard_map/reduce_scatter | solution.py:210
  1521.5 2.7 slice.31
  1524.3 1.9 slice_bitcast_fusion.3
  1526.1 1360.9 %reduce-scatter.8.cloned.1.call-done = f32[128,2,4096]{2,0,1:T(8,128)} async-done(((f32[2048,2,4096]{2,0,1:T(8,128)}), f32[128,2,4096]{2,0,1:T(8,128)}) %reduce-scatter.8.cloned.1.call-update) | async-done | bytes 4194320 | tf_op jit(solution)/shard_map/reduce_scatter | solution.py:146
  2887.1 4.7 slice_bitcast_fusion
  (157 shorter events, 23.3 us)
Async XLA Ops:
  7.2 6.8 copy-start.3
  7.2 158.2 %all-gather.5.cloned.1.call-start = ((), (), s32[]{:S(2)}) async-start(), calls=%async_computation.3 | async-start | bytes 13369344 | tf_op jit(solution)/shard_map/all_gather | solution.py:72
  7.9 234.5 %all-gather.7.cloned.1.call-start = ((), (), s32[]{:S(2)}) async-start(), calls=%async_computation.4 | async-start | bytes 4456448 | tf_op jit(solution)/shard_map/all_gather | solution.py:73
  8.7 267.8 %all-reduce.12.cloned.1.call-start = ((), (), s32[]{:S(2)}) async-start(), calls=%async_computation.5 | async-start | bytes 8388608 | tf_op jit(solution)/shard_map/psum | solution.py:101
  10.2 165.0 %copy-start.21 = (f32[2048]{0:T(1024)}, f32[2048]{0:T(1024)S(1)}, u32[]{:S(2)}) copy-start(f32[2048]{0:T(1024)S(1)} %convert_element_type.107) | copy-start | bytes 24580
  10.8 164.3 %copy-start.34 = (f32[2048]{0:T(1024)}, f32[2048]{0:T(1024)S(1)}, u32[]{:S(2)}) copy-start(f32[2048]{0:T(1024)S(1)} %convert_element_type.108) | copy-start | bytes 24580
  14.0 161.1 %copy-start.23 = (f32[512]{0:T(512)}, f32[512]{0:T(512)S(1)}, u32[]{:S(2)}) copy-start(f32[512]{0:T(512)S(1)} %broadcast_multiply_fusion.1) | copy-start | bytes 6148
  14.7 160.4 %copy-start.29 = (f32[512]{0:T(512)}, f32[512]{0:T(512)S(1)}, u32[]{:S(2)}) copy-start(f32[512]{0:T(512)S(1)} %fusion.56) | copy-start | bytes 6148
  179.6 5.6 copy-start.10
  185.2 3.4 copy-start
  185.2 3.4 copy-start.13
  249.3 223.0 %all-gather.9.cloned.1.call-start = ((), (), s32[]{:S(2)}) async-start(), calls=%async_computation.6 | async-start | bytes 17825792 | tf_op jit(solution)/shard_map/all_gather | solution.py:110
  249.9 415.3 %all-gather.11.cloned.1.call-start = ((), (), s32[]{:S(2)}) async-start(), calls=%async_computation.7 | async-start | bytes 17825792 | tf_op jit(solution)/shard_map/all_gather | solution.py:117
  250.5 469.6 %all-reduce.14.cloned.1.call-start = ((), (), s32[]{:S(2)}) async-start(), calls=%async_computation.8 | async-start | bytes 4194304 | tf_op jit(solution)/shard_map/psum | solution.py:137
  250.9 221.4 %copy-start.36 = (f32[2048]{0:T(1024)}, f32[2048]{0:T(1024)S(1)}, u32[]{:S(2)}) copy-start(f32[2048]{0:T(1024)S(1)} %convert_element_type.117) | copy-start | bytes 24580
  279.3 2.1 copy-start.1
  281.9 383.2 %copy-start.14 = (bf16[512,2048]{1,0:T(8,128)(2,1)S(1)}, bf16[512,2048]{1,0:T(8,128)(2,1)}, u32[]{:S(2)}) copy-start(bf16[512,2048]{1,0:T(8,128)(2,1)} %param.31) | copy-start | bytes 6291460
  683.7 1.9 copy-start.44
  699.1 190.7 %reduce-scatter.10.cloned.1.call-start = ((), (), s32[]{:S(2)}) async-start(), calls=%async_computation.11 | async-start | bytes 2228224
  701.1 190.2 %all-reduce.16.cloned.1.call-start = ((), (), s32[]{:S(2)}) async-start(), calls=%async_computation.12 | async-start | bytes 8388608 | tf_op jit(solution)/shard_map/psum | solution.py:114
  720.1 4.6 copy-start.2
  720.1 4.7 copy-start.7
  727.4 4.8 copy-start.42
  730.2 2.0 copy-start.8
  735.0 10.2 slice-start
  740.2 5.0 slice-start.1
  745.2 2.6 copy-start.12
  751.4 1.9 copy-start.16
  753.3 11.4 copy-start.19
  764.7 5.2 copy-start.4
  764.7 5.2 copy-start.17
  764.7 5.2 copy-start.22
  764.7 5.2 copy-start.24
  764.7 5.2 copy-start.30
  764.8 5.2 copy-start.35
  764.8 756.8 %reduce-scatter.6.cloned.1.call-start = ((), (), s32[]{:S(2)}) async-start(), calls=%async_computation.9 | async-start | bytes 35651584 | tf_op jit(solution)/shard_map/reduce_scatter | solution.py:210
  764.8 5.2 copy-start.18
  764.8 5.2 copy-start.20
  802.3 2084.8 %reduce-scatter.8.cloned.1.call-start = ((), (), s32[]{:S(2)}) async-start(), calls=%async_computation.10 | async-start | bytes 71303168 | tf_op jit(solution)/shard_map/reduce_scatter | solution.py:146
  802.9 20.3 copy-start.15
  887.8 6.4 copy-start.32
  891.3 3.0 copy-start.5
  891.3 5.4 copy-start.25
  891.3 5.4 copy-start.26
  891.3 5.4 copy-start.27
  891.3 5.4 copy-start.28
  978.0 5.0 copy-start.6
  978.0 5.0 copy-start.9
  (9 other events, 10.7 us)
Sparse Core Ops, SparseCore 0:
  10.8 154.5 all-gather.4
  168.1 74.2 all-gather.6
  249.4 27.0 all-reduce.11
  279.5 192.7 all-gather.8
  475.3 189.7 all-gather.10
  699.2 19.4 all-reduce.13
  721.5 81.5 reduce-scatter.9
  806.2 25.5 all-reduce.15
  834.3 687.2 reduce-scatter.5
  1523.9 1363.1 reduce-scatter.7
where the time goes:
time: 2910 us; the launch traced here: 2900 us
  waiting for transfers between devices  2490 us (86%)
  matrix products  172 us (6%)
  other arithmetic  101 us (3%)
  blocking collectives  77.7 us (3%)
  local copies, waits for them, and re-layouts  38.8 us (1%)
    reduce_scatter x1, waiting for transfers between devices, body(): lax.psum_scatter(jnp.stack([lax.dot_general(second_low, sum_low, token_di...  1360 us
    reduce_scatter x1, waiting for transfers between devices, body(): lax.psum_scatter(jnp.concatenate([heads_term, output_term[:, None, :]], a...  536 us
    all_gather x1, waiting for transfers between devices, body(): lax.all_gather(expand_weight, 'dp', axis=0, tiled=True)  190 us
    all_gather x1, waiting for transfers between devices, body(): lax.all_gather(reduce_weight, 'dp', axis=0, tiled=True)  177 us
    all_gather x1, waiting for transfers between devices, body(): lax.all_gather(heads_weight, 'dp', axis=0, tiled=True)  149 us
    unnamed x1, blocking collectives  77.7 us
  transfers between devices with their start and end apart: 10, of which 7 were waited for; matrix products, arithmetic and copies ran while one was open for 9% of the time, Pallas kernels for 0%

commit v1 on v0

v1 whole, which is shorter than its diff:
```python
import functools

import jax
import jax.numpy as jnp
from jax import lax
from jax.experimental import pallas as pl
from jax.experimental.pallas import tpu as pltpu
from jax.sharding import Mesh
from jax.sharding import PartitionSpec as P

HEAD = 128
WINDOW = 256
CHUNK = 128
SCALE = HEAD**-0.5
ALL = ("z", "y", "x", "c")
BF = jnp.bfloat16
F32 = jnp.float32
ACROSS = (((1,), (1,)), ((), ()))
ROWS = (((0,), (0,)), ((), ()))
PLAIN = (((1,), (0,)), ((), ()))


def dot(a, b, dims=PLAIN):
    return lax.dot_general(a, b, dims, preferred_element_type=F32)


def add_dots(pairs, dims=PLAIN):
    total = None
    for a, b in pairs:
        part = dot(a, b, dims)
        total = part if total is None else total + part
    return total


def pairs_of(depth, route):
    def flat(z, y, x, c):
        return ((z * 2 + y) * 2 + x) * 2 + c

    found = []
    for z in range(depth):
        for y in range(2):
            for x in range(2):
                for c in range(2):
                    goal = route(y, x, c)
                    if goal is not None:
                        found.append((flat(z, y, x, c), flat(z, *goal)))
    return found


def bounds_of(group_sizes, prefix_lengths, solution_lengths, row_count):
    entries = solution_lengths.shape[1]
    position = jnp.arange(entries, dtype=jnp.int32)
    counted = jnp.where(position[None, :] < group_sizes[:, None], solution_lengths, 0)
    pieces = jnp.concatenate([prefix_lengths[:, None], counted], axis=1)
    flat = pieces.reshape(-1)
    count = flat.shape[0]
    index = jnp.arange(count, dtype=jnp.int32)
    ends = jnp.sum(jnp.where(index[None, :] <= index[:, None], flat[None, :], 0), axis=1)
    slot = jnp.arange(row_count, dtype=jnp.int32)
    passed = slot[:, None] >= ends[None, :]
    piece_start = jnp.max(jnp.where(passed, ends[None, :], 0), axis=1)
    group_end = ends.reshape(pieces.shape)[:, -1]
    over = slot[:, None] >= group_end[None, :]
    group_start = jnp.max(jnp.where(over, group_end[None, :], 0), axis=1)
    group_index = jnp.sum(over.astype(jnp.int32), axis=1)
    member = group_index[:, None] == jnp.arange(pieces.shape[0], dtype=jnp.int32)[None, :]
    prefix_end = group_start + jnp.sum(jnp.where(member, prefix_lengths[None, :], 0), axis=1)
    live = slot < ends[-1]
    piece_start = jnp.where(live, piece_start, slot)
    group_start = jnp.where(live, group_start, slot)
    prefix_end = jnp.where(live, prefix_end, slot)
    return jnp.stack([group_start, prefix_end, piece_start], axis=1), live


def key_range(i):
    return max(0, i * CHUNK - WINDOW), (i + 1) * CHUNK


def allowed_tile(info, i, lo, hi):
    rows = info[i * CHUNK : (i + 1) * CHUNK, :]
    start, stop, piece = rows[:, 0:1], rows[:, 1:2], rows[:, 2:3]
    s = lax.broadcasted_iota(jnp.int32, (CHUNK, hi - lo), 0) + i * CHUNK
    t = lax.broadcasted_iota(jnp.int32, (CHUNK, hi - lo), 1) + lo
    return (t <= s) & ((t >= piece) | ((t >= start) & (t < stop)))


def attend_kernel(info_ref, p0_ref, p1_ref, o0_ref, o1_ref):
    block, width = p0_ref.shape
    width = width // 3
    info = info_ref[...]
    for i in range(block // CHUNK):
        lo, hi = key_range(i)
        allowed = allowed_tile(info, i, lo, hi)
        rows = slice(i * CHUNK, (i + 1) * CHUNK)
        for p_ref, o_ref in ((p0_ref, o0_ref), (p1_ref, o1_ref)):
            for h in range(width // HEAD):
                q = p_ref[rows, h * HEAD : (h + 1) * HEAD]
                k = p_ref[lo:hi, width + h * HEAD : width + (h + 1) * HEAD]
                v = p_ref[lo:hi, 2 * width + h * HEAD : 2 * width + (h + 1) * HEAD]
                scores = jnp.where(allowed, dot(q, k, ACROSS) * SCALE, -1e30)
                e = jnp.exp(scores - jnp.max(scores, axis=-1, keepdims=True))
                soft = e / jnp.sum(e, axis=-1, keepdims=True)
                o_ref[rows, h * HEAD : (h + 1) * HEAD] = dot(soft.astype(BF), v).astype(BF)


def attend_back_kernel(info_ref, p0_ref, p1_ref, g0_ref, g1_ref, d0_ref, d1_ref, dk_ref, dv_ref):
    block, width = p0_ref.shape
    width = width // 3
    info = info_ref[...]
    masks = []
    for i in range(block // CHUNK):
        lo, hi = key_range(i)
        masks.append(allowed_tile(info, i, lo, hi))
    for p_ref, g_ref, d_ref in ((p0_ref, g0_ref, d0_ref), (p1_ref, g1_ref, d1_ref)):
        for h in range(width // HEAD):
            dk_ref[...] = jnp.zeros_like(dk_ref)
            dv_ref[...] = jnp.zeros_like(dv_ref)
            qs = slice(h * HEAD, (h + 1) * HEAD)
            ks = slice(width + h * HEAD, width + (h + 1) * HEAD)
            vs = slice(2 * width + h * HEAD, 2 * width + (h + 1) * HEAD)
            for i in range(block // CHUNK):
                lo, hi = key_range(i)
                rows = slice(i * CHUNK, (i + 1) * CHUNK)
                q = p_ref[rows, qs]
                k = p_ref[lo:hi, ks]
                v = p_ref[lo:hi, vs]
                g = g_ref[rows, qs]
                scores = jnp.where(masks[i], dot(q, k, ACROSS) * SCALE, -1e30)
                e = jnp.exp(scores - jnp.max(scores, axis=-1, keepdims=True))
                soft = e / jnp.sum(e, axis=-1, keepdims=True)
                back = dot(g, v, ACROSS)
                low = (soft * (back - jnp.sum(soft * back, axis=-1, keepdims=True))).astype(BF)
                d_ref[rows, qs] = (dot(low, k) * SCALE).astype(BF)
                dk_ref[lo:hi, :] += dot(low, q, ROWS)
                dv_ref[lo:hi, :] += dot(soft.astype(BF), g, ROWS)
            d_ref[:, ks] = (dk_ref[...] * SCALE).astype(BF)
            d_ref[:, vs] = dv_ref[...].astype(BF)


def attend(info, p0, p1, block):
    rows, width = p0.shape
    spec = lambda n: pl.BlockSpec((block, n), lambda b: (b, 0))
    out = jax.ShapeDtypeStruct((rows, width // 3), BF)
    return pl.pallas_call(
        attend_kernel,
        grid=(rows // block,),
        in_specs=[spec(info.shape[1]), spec(width), spec(width)],
        out_specs=[spec(width // 3)] * 2,
        out_shape=[out, out],
        compiler_params=pltpu.CompilerParams(vmem_limit_bytes=32 << 20),
        cost_estimate=pl.CostEstimate(
            flops=4 * rows * block * width, bytes_accessed=4 * rows * width * 2, transcendentals=rows * block * 4
        ),
        name="attend",
    )(info, p0, p1)


def attend_back(info, p0, p1, g0, g1, block):
    rows, width = p0.shape
    spec = lambda n: pl.BlockSpec((block, n), lambda b: (b, 0))
    out = jax.ShapeDtypeStruct((rows, width), BF)
    return pl.pallas_call(
        attend_back_kernel,
        grid=(rows // block,),
        in_specs=[spec(info.shape[1]), spec(width), spec(width), spec(width // 3), spec(width // 3)],
        out_specs=[spec(width)] * 2,
        out_shape=[out, out],
        scratch_shapes=[pltpu.VMEM((block, HEAD), F32)] * 2,
        compiler_params=pltpu.CompilerParams(vmem_limit_bytes=32 << 20),
        cost_estimate=pl.CostEstimate(
            flops=10 * rows * block * width, bytes_accessed=8 * rows * width * 2, transcendentals=rows * block * 4
        ),
        name="attend_back",
    )(info, p0, p1, g0, g1)


def normalize(values, gain_vector, shift_vector):
    center = values - jnp.mean(values, axis=-1, keepdims=True)
    spread = jnp.mean(center * center, axis=-1, keepdims=True)
    return center * lax.rsqrt(spread + 1e-05) * gain_vector + shift_vector


def smooth(values):
    return jax.nn.gelu(values, approximate=True)


def body(
    depth,
    inputs,
    gamma_first,
    beta_first,
    heads_weight,
    output_weight,
    output_bias,
    gamma_second,
    beta_second,
    expand_weight,
    expand_bias,
    reduce_weight,
    reduce_bias,
    group_sizes,
    prefix_lengths,
    solution_lengths,
    cotangent,
):
    block, model = inputs.shape
    zi, yi, xi, ci = (lax.axis_index(a) for a in ALL)
    plane = yi * 2 + xi
    own = xi == ci
    send = lambda v, route: lax.ppermute(v, ALL, pairs_of(depth, route))
    wide = lambda v: v.astype(F32)

    def near_of(v):
        return send(v, lambda y, x, c: (y, x, c) if c == x else (y, 1 - x, 1 - c))

    def far_of(v):
        return send(v, lambda y, x, c: (1 - y, x, c) if c == x else (1 - y, 1 - x, 1 - c))

    def spread(v):
        half = v.shape[0] // 2
        over_y = send(v, lambda y, x, c: (1 - y, x, c) if c == x else None)
        over_x = send(v, lambda y, x, c: (y, 1 - x, c) if c == x else None)
        near = jnp.where(own, v, over_x)
        first_half = send(over_x[:half], lambda y, x, c: (1 - y, x, c) if c != x else None)
        second_half = send(over_y[half:], lambda y, x, c: (y, 1 - x, c) if c == x else None)
        far = jnp.where(own, over_y, jnp.concatenate([first_half, second_half], axis=0))
        return jnp.concatenate([near, far], axis=0)

    def collect(v):
        near, far = v[:block], v[block:]
        half = block // 2
        a = send(far[:half], lambda y, x, c: (1 - y, x, c) if c != x else None)
        b = send(far[half:], lambda y, x, c: (y, 1 - x, c) if c != x else None)
        send_x = jnp.concatenate([(wide(near[:half]) + wide(a)).astype(BF), near[half:]], axis=0)
        send_y = jnp.concatenate([far[:half], (wide(far[half:]) + wide(b)).astype(BF)], axis=0)
        from_x = send(send_x, lambda y, x, c: (y, 1 - x, c) if c != x else None)
        from_y = send(send_y, lambda y, x, c: (1 - y, x, c) if c == x else None)
        return wide(near) + wide(from_x) + wide(from_y)

    def from_owner(v):
        return jnp.where(own, v, send(v, lambda y, x, c: (y, x, 1 - c) if c == x else None))

    def shuffle(v):
        take = lambda k: lax.dynamic_index_in_dim(v, plane ^ k, 0, keepdims=False)
        mine = take(0)
        by_x = send(take(1), lambda y, x, c: (y, 1 - x, c))
        by_y = send(take(2), lambda y, x, c: (1 - y, x, c))
        by_both = send(take(3), lambda y, x, c: (1 - y, 1 - x, c))
        even, low = xi == 0, yi == 0
        a0, a1 = jnp.where(even, mine, by_x), jnp.where(even, by_x, mine)
        b0, b1 = jnp.where(even, by_y, by_both), jnp.where(even, by_both, by_y)
        return [
            jnp.where(low, a0, b0),
            jnp.where(low, a1, b1),
            jnp.where(low, b0, a0),
            jnp.where(low, b1, a1),
        ]

    def gather(v):
        full = lax.all_gather(v, ("c", "z"), axis=0, tiled=True)
        return full.reshape(2, full.shape[0] // 2, full.shape[1])

    def scatter(v):
        return lax.psum_scatter(v.reshape(-1, v.shape[-1]), ("c", "z"), scatter_dimension=0, tiled=True)

    shard, _, local = heads_weight.shape
    part = local // 4
    inner = expand_weight.shape[1] // 4
    heads_in = heads_weight.reshape(shard, 3, 4, part).transpose(2, 0, 1, 3).reshape(4, shard, 3 * part)
    heads_all = gather(jnp.concatenate(shuffle(heads_in), axis=0))
    out_in = output_weight.reshape(shard, 4, part).transpose(1, 0, 2)
    expand_in = expand_weight.reshape(shard, 4, inner).transpose(1, 0, 2)
    reduce_in = reduce_weight.reshape(shard, 4, inner).transpose(1, 0, 2)
    rest = shuffle(jnp.concatenate([out_in, expand_in, reduce_in], axis=2))
    out_all = gather(jnp.concatenate([r[:, :part] for r in rest], axis=0))
    expand_all = gather(jnp.concatenate([r[:, part : part + inner] for r in rest], axis=0))
    reduce_all = gather(jnp.concatenate([r[:, part + inner :] for r in rest], axis=0))
    bias_mine = lax.dynamic_slice_in_dim(expand_bias, plane * inner, inner).reshape(1, inner)
    bias_other = send(bias_mine, lambda y, x, c: (y, x, 1 - c))
    bias = [wide(jnp.where(ci == k, bias_mine, bias_other)) for k in range(2)]

    info, live = bounds_of(group_sizes, prefix_lengths, solution_lengths, block)
    info = jnp.pad(info, ((0, 0), (0, 5)))
    live_mask = wide(live)[:, None]
    info_two = jnp.concatenate([near_of(info), far_of(info)], axis=0)
    gain_first, shift_first = wide(gamma_first), wide(beta_first)
    gain_second, shift_second = wide(gamma_second), wide(beta_second)
    residual = wide(inputs)
    first_own = normalize(residual, gain_first, shift_first).astype(BF)
    first = jnp.concatenate([near_of(first_own), far_of(first_own)], axis=0)
    upstream = live_mask * wide(cotangent)
    upstream_own = upstream.astype(BF)
    upstream_low = jnp.concatenate([near_of(upstream_own), far_of(upstream_own)], axis=0)
    reduce_bias_gradient = jnp.sum(upstream, axis=0)

    projected = [dot(first, heads_all[k]).astype(BF) for k in range(2)]
    mixed = attend(info_two, projected[0], projected[1], block)
    attended = collect(add_dots([(mixed[k], out_all[k]) for k in range(2)], ACROSS).astype(BF))
    middle = residual + attended + wide(output_bias)
    second_own = normalize(middle, gain_second, shift_second).astype(BF)
    second = spread(second_own)
    hidden = [dot(second, expand_all[k]) + bias[k] for k in range(2)]
    activated = [smooth(h).astype(BF) for h in hidden]
    reduce_terms = jnp.stack([dot(upstream_low, activated[k], ROWS).astype(BF) for k in range(2)])
    reduce_part = scatter(reduce_terms)

    hidden_back = [dot(upstream_low, reduce_all[k]) for k in range(2)]
    sum_back = [jax.vjp(smooth, hidden[k])[1](hidden_back[k])[0] for k in range(2)]
    sum_low = [s.astype(BF) for s in sum_back]
    expand_bias_gradient = jnp.stack([jnp.sum(s, axis=0) for s in sum_back])
    second_back = collect(add_dots([(sum_low[k], expand_all[k]) for k in range(2)], ACROSS).astype(BF))
    expand_terms = jnp.stack([dot(second, sum_low[k], ROWS).astype(BF) for k in range(2)])
    expand_part = scatter(expand_terms)
    branch = collect(add_dots([(activated[k], reduce_all[k]) for k in range(2)], ACROSS).astype(BF))
    outputs = from_owner((live_mask * (middle + branch + wide(reduce_bias))).astype(BF))

    _, second_pullback = jax.vjp(normalize, middle, gain_second, shift_second)
    middle_part, gamma_second_gradient, beta_second_gradient = second_pullback(second_back)
    middle_back = upstream + middle_part
    output_bias_gradient = jnp.sum(middle_back, axis=0)
    middle_low = spread(middle_back.astype(BF))

    mixed_back = [dot(middle_low, out_all[k]).astype(BF) for k in range(2)]
    projected_back = attend_back(info_two, projected[0], projected[1], mixed_back[0], mixed_back[1], block)
    heads_terms = jnp.stack(
        [
            jnp.concatenate(
                [dot(first, projected_back[k], ROWS).astype(BF), dot(middle_low, mixed[k], ROWS).astype(BF)], axis=1
            )
            for k in range(2)
        ]
    )
    heads_part = scatter(heads_terms)
    first_back = collect(add_dots([(projected_back[k], heads_all[k]) for k in range(2)], ACROSS).astype(BF))
    _, first_pullback = jax.vjp(normalize, residual, gain_first, shift_first)
    input_part, gamma_first_gradient, beta_first_gradient = first_pullback(first_back)
    input_gradient = from_owner((middle_back + input_part).astype(BF))

    rows_out = lambda v: v.reshape(4, shard, v.shape[-1])
    reduce_gradient = wide(jnp.concatenate(shuffle(rows_out(reduce_part)), axis=1))
    expand_gradient = wide(jnp.concatenate(shuffle(rows_out(expand_part)), axis=1))
    heads_out = shuffle(rows_out(heads_part))
    heads_gradient = wide(jnp.stack([h[:, : 3 * part].reshape(shard, 3, part) for h in heads_out], axis=2))
    heads_gradient = heads_gradient.reshape(shard, 3, local)
    output_gradient = wide(jnp.concatenate([h[:, 3 * part :] for h in heads_out], axis=1))

    vectors = jnp.stack(
        [
            gamma_first_gradient,
            beta_first_gradient,
            output_bias_gradient,
            gamma_second_gradient,
            beta_second_gradient,
            reduce_bias_gradient,
        ]
    )
    vectors = jnp.where(own, vectors, 0.0)
    placed = lax.dynamic_update_slice(jnp.zeros((2, 4 * inner), F32), expand_bias_gradient, (0, plane * inner))
    sums = jnp.concatenate([vectors.reshape(-1), placed.reshape(-1)]).reshape(-1, 128)
    for route in (
        lambda y, x, c: (y, x, 1 - c),
        lambda y, x, c: (y, 1 - x, c),
        lambda y, x, c: (1 - y, x, c),
    ):
        sums = sums + send(sums, route)
    step = 1
    while step < depth:
        sums = sums + lax.ppermute(sums, "z", [(i, i ^ step) for i in range(depth)])
        step *= 2
    flat = sums.reshape(-1)
    index = zi * 4 + plane
    vectors = lax.dynamic_slice_in_dim(flat[: 6 * model].reshape(6, model), index * shard, shard, axis=1)
    placed = flat[6 * model :].reshape(2, 4 * inner)
    count = 4 * inner // (4 * depth)
    expand_bias_gradient = lax.dynamic_slice(placed, (ci, index * count), (1, count))
    return (
        outputs,
        input_gradient,
        vectors[0],
        vectors[1],
        heads_gradient,
        output_gradient,
        vectors[2],
        vectors[3],
        vectors[4],
        expand_gradient,
        expand_bias_gradient,
        reduce_gradient,
        vectors[5],
    )


def solution(mesh):
    depth = mesh.shape["dp"] // 4
    fine = Mesh(mesh.devices.reshape(depth, 2, 2, 2), ALL)
    dp = ("z", "y", "x")
    placed = (
        P(dp, None),
        P(),
        P(),
        P(dp, None, "c"),
        P(dp, "c"),
        P(),
        P(),
        P(),
        P(dp, "c"),
        P("c"),
        P(dp, "c"),
        P(),
        P(dp),
        P(dp),
        P(dp, None),
        P(dp, None),
    )
    return jax.shard_map(
        functools.partial(body, depth),
        mesh=fine,
        in_specs=placed,
        out_specs=(
            P(dp, None),
            P(dp, None),
            P(dp),
            P(dp),
            P(dp, None, "c"),
            P(dp, "c"),
            P(dp),
            P(dp),
            P(dp),
            P(dp, "c"),
            P("c", dp),
            P(dp, "c"),
            P(dp),
        ),
        check_vma=False,
    )
```

time: 2910 us -> 908 us (0.31)
  waiting for transfers between devices: 2490 us -> 450 us
  starting transfers between devices: 0.74 us -> 114 us
  blocking collectives: 77.7 us -> 0 us
    reduce_scatter x2 -> x3, waiting for transfers between devices: 1900 us -> 116 us  [scatter(): lax.psum_scatter(v.reshape(-1, v.shape[-1]), ('c', 'z'), scatter_dimensio...]
    all_gather x4, waiting for transfers between devices: 568 us -> 0.02 us  [gather(): full = lax.all_gather(v, ('c', 'z'), axis=0, tiled=True)]
    ppermute x0 -> x53, waiting for transfers between devices: none -> 335 us  [the longest x51 319 us: body(): send = lambda v, route: lax.ppermute(v, ALL, pairs_of(depth, route))]
    ppermute x0 -> x53, starting transfers between devices: none -> 113 us  [the longest x51 110 us: body(): send = lambda v, route: lax.ppermute(v, ALL, pairs_of(depth, route))]
    unnamed x1 -> x0, blocking collectives: 77.7 us -> none
    dot_general x18 -> x24, matrix products: 172 us -> 147 us  [dot(): return lax.dot_general(a, b, dims, preferred_element_type=F32)]
  transfers between devices with their start and end apart: 10 -> 60, of which waited for: 7 -> 31; matrix products, arithmetic and copies ran while one was open for 9% -> 31% of each run, Pallas kernels for 0% -> 3%
where the time goes in v1:
time: 908 us; the launch traced here: 899 us
  waiting for transfers between devices  450 us (50%)
  matrix products  147 us (16%)
  starting transfers between devices  114 us (13%)
  other arithmetic  82.2 us (9%)
  local copies, waits for them, and re-layouts  63 us (7%)
  Pallas kernels  26.4 us (3%)
  between operations  16.4 us (2%)
    ppermute x51, waiting for transfers between devices, body(): send = lambda v, route: lax.ppermute(v, ALL, pairs_of(depth, route))  319 us
    dot_general x24, matrix products, dot(): return lax.dot_general(a, b, dims, preferred_element_type=F32)  147 us
    reduce_scatter x3, waiting for transfers between devices, scatter(): lax.psum_scatter(v.reshape(-1, v.shape[-1]), ('c', 'z'), scatter_dimensio...  116 us
    ppermute x51, starting transfers between devices, body(): send = lambda v, route: lax.ppermute(v, ALL, pairs_of(depth, route))  110 us
    unnamed x181, local copies, waits for them, and re-layouts  26.4 us
  transfers between devices with their start and end apart: 60, of which 31 were waited for; matrix products, arithmetic and copies ran while one was open for 31% of the time, Pallas kernels for 3%

profile of v1, /device:TPU:0, one launch (start us, length us, event | category | flops | bytes accessed | tf_op | source)
XLA Modules:
  0.0 899.2 jit_solution(10961826484962447467)
XLA Ops:
  17.7 4.8 collective-permute-done.5
  31.9 11.1 %collective-permute-done.7 = bf16[128,2304]{1,0:T(8,128)(2,1)S(1)} collective-permute-done((bf16[128,2304]{1,0:T(8,128)(2,1)S(1)}, bf16[128,2304]{1,0:T(8,128)(2,1)S(1)}, u32[]{:S(2)}, u32[]{:S(2)}) %collective-permute-start.7) | collective-permute-done | bytes 589856 | tf_op jit(solution)/shard_map/ppermute | solution.py:210
  43.1 11.8 %collective-permute-done.8 = bf16[128,2304]{1,0:T(8,128)(2,1)S(1)} collective-permute-done((bf16[128,2304]{1,0:T(8,128)(2,1)S(1)}, bf16[128,2304]{1,0:T(8,128)(2,1)S(1)}, u32[]{:S(2)}, u32[]{:S(2)}) %collective-permute-start.8) | collective-permute-done | bytes 589856 | tf_op jit(solution)/shard_map/ppermute | solution.py:210
  66.6 17.2 %collective-permute-start.2 = (bf16[512,2048]{1,0:T(8,128)(2,1)}, bf16[512,2048]{1,0:T(8,128)(2,1)}, u32[]{:S(2)}, u32[]{:S(2)}) collective-permute-start(bf16[512,2048]{1,0:T(8,128)(2,1)} %fusion.7), channel_id=1, source_target_pairs={{0,0},{1,2},{2,1},{3,3},{4,4},{5,6},{6,5},{7,7},{8,8},{9,10},{10,9... | collective-permute-start | bytes 6291464 | tf_op jit(solution)/shard_map/ppermute | solution.py:210
  89.2 43.7 %collective-permute-done.1 = s32[512,8]{0,1:T(8,128)S(1)} collective-permute-done((s32[512,8]{0,1:T(8,128)S(1)}, s32[512,8]{0,1:T(8,128)S(1)}, u32[]{:S(2)}, u32[]{:S(2)}) %collective-permute-start.1) | collective-permute-done | bytes 16416 | tf_op jit(solution)/shard_map/ppermute | solution.py:210
  137.8 6.8 fusion.54.p1_ref
  144.6 6.2 fusion.51.p0_ref
  150.8 9.9 %attend.1 = (bf16[1024,256]{1,0:T(8,128)(2,1)S(1)}, bf16[1024,256]{1,0:T(8,128)(2,1)S(1)}) custom-call(s32[1024,8]{1,0:T(8,128)S(1)} %copy.117.info_ref, bf16[1024,768]{1,0:T(8,128)(2,1)S(1)} %fusion.51.p0_ref, bf16[1024,768]{1,0:T(8,128)(2,1)S(1)} %fusion.54.p1_ref), custom_call_target="tpu_custom_call" | custom-call | flops 1610612736 | bytes 6291456 | tf_op jit(solution)/shard_map/attend/pallas_call | solution.py:144
  174.1 14.0 %collective-permute-done.12 = bf16[256,2048]{1,0:T(8,128)(2,1)} collective-permute-done((bf16[256,2048]{1,0:T(8,128)(2,1)}, bf16[256,2048]{1,0:T(8,128)(2,1)}, u32[]{:S(2)}, u32[]{:S(2)}) %collective-permute-start.12) | collective-permute-done | bytes 1048608 | tf_op jit(solution)/shard_map/ppermute | solution.py:210
  196.4 23.3 %collective-permute-done.11 = bf16[512,2048]{1,0:T(8,128)(2,1)S(1)} collective-permute-done((bf16[512,2048]{1,0:T(8,128)(2,1)S(1)}, bf16[512,2048]{1,0:T(8,128)(2,1)S(1)}, u32[]{:S(2)}, u32[]{:S(2)}) %collective-permute-start.11) | collective-permute-done | bytes 2097184 | tf_op jit(solution)/shard_map/ppermute | solution.py:210
  232.6 17.2 %collective-permute-start.24 = (bf16[512,2048]{1,0:T(8,128)(2,1)}, bf16[512,2048]{1,0:T(8,128)(2,1)}, u32[]{:S(2)}, u32[]{:S(2)}) collective-permute-start(bf16[512,2048]{1,0:T(8,128)(2,1)} %fusion.25), channel_id=1, source_target_pairs={{0,0},{1,2},{2,1},{3,3},{4,4},{5,6},{6,5},{7,7},{8,8},{9,10},{10,9... | collective-permute-start | bytes 6291464 | tf_op jit(solution)/shard_map/ppermute | solution.py:210
  253.1 18.3 %collective-permute-done.14 = bf16[512,2048]{1,0:T(8,128)(2,1)} collective-permute-done((bf16[512,2048]{1,0:T(8,128)(2,1)}, bf16[512,2048]{1,0:T(8,128)(2,1)}, u32[]{:S(2)}, u32[]{:S(2)}) %collective-permute-start.14) | collective-permute-done | bytes 2097184 | tf_op jit(solution)/shard_map/ppermute | solution.py:210
  273.6 6.5 collective-permute-start.17
  283.3 29.5 %collective-permute-done.25 = bf16[512,2048]{1,0:T(8,128)(2,1)} collective-permute-done((bf16[512,2048]{1,0:T(8,128)(2,1)}, bf16[512,2048]{1,0:T(8,128)(2,1)}, u32[]{:S(2)}, u32[]{:S(2)}) %collective-permute-start.25) | collective-permute-done | bytes 2097184 | tf_op jit(solution)/shard_map/ppermute | solution.py:210
  320.6 8.1 fusion.30
  328.7 4.5 fusion.38
  333.3 10.2 %convert_bitcast_fusion = bf16[1,2048,1024]{2,1,0:T(8,128)(2,1)} fusion(bf16[1024,2048]{1,0:T(8,128)(2,1)} %constant_dynamic-update-slice_fusion.2, f32[1024,1024]{1,0:T(8,128)S(1)} %fusion.30, f32[1024]{0:T(1024)S(1)} %bitcast.205), kind=kOutput, calls=%fused_computation.44 | convolution fusion | flops 4307550208 | bytes 12587008 | tf_op jit(solution)/shard_map/dot_general | solution.py:24
  343.5 8.8 convert_bitcast_fusion.1
  352.3 7.6 pad_maximum_fusion.2
  360.0 11.5 %fusion.90 = (f32[1024]{0:T(1024)}, bf16[1024,1024]{1,0:T(8,128)(2,1)S(1)}) fusion(f32[1024,1024]{1,0:T(8,128)} %copy-done.73, f32[1024]{0:T(1024)S(1)} %bitcast.209, bf16[1024,2048]{1,0:T(8,128)(2,1)} %constant_dynamic-update-slice_fusion.2, bf16[4096,1024]{1,0:T(8,128)(2,1)} %all-gather.11.cloned.1.call-done), kind=kOutput, calls=%fused_computation.255 | convolution fusion | flops 4318034944 | bytes 14688256 | tf_op jit(solution)/shard_map/dot_general | solution.py:24
  371.4 9.9 %fusion.36 = f32[1024,2048]{1,0:T(8,128)} fusion(bf16[4096,1024]{1,0:T(8,128)(2,1)} %all-gather.9.cloned.1.call-done, bf16[1024,1024]{1,0:T(8,128)(2,1)S(1)} %get-tuple-element.171), kind=kOutput, calls=%fused_computation.72 | convolution fusion | flops 4294967296 | bytes 14680064 | tf_op jit(solution)/shard_map/dot_general | solution.py:24
  381.4 11.1 %fusion.89 = (f32[1024]{0:T(1024)}, bf16[1024,1024]{1,0:T(8,128)(2,1)}) fusion(f32[1024,1024]{1,0:T(8,128)S(1)} %copy-done.75, f32[1024]{0:T(1024)S(1)} %bitcast.206, bf16[1024,2048]{1,0:T(8,128)(2,1)} %constant_dynamic-update-slice_fusion.2, bf16[4096,1024]{1,0:T(8,128)(2,1)S(1)} %copy-done.71), kind=kOutput, calls=%fused_computation.254 | convolution fusion | flops 4318034944 | bytes 14688256 | tf_op jit(solution)/shard_map/dot_general | solution.py:24
  392.5 7.8 add_convert_fusion.1
  405.3 6.6 convert_bitcast_fusion.2
  411.9 6.2 convert_bitcast_fusion.3
  418.1 7.6 pad_maximum_fusion.1
  425.7 8.4 fusion.34
  434.2 8.6 add_convert_fusion.2
  452.1 11.0 %collective-permute-done.21 = bf16[256,2048]{1,0:T(8,128)(2,1)S(1)} collective-permute-done((bf16[256,2048]{1,0:T(8,128)(2,1)S(1)}, bf16[256,2048]{1,0:T(8,128)(2,1)S(1)}, u32[]{:S(2)}, u32[]{:S(2)}) %collective-permute-start.21) | collective-permute-done | bytes 1048608 | tf_op jit(solution)/shard_map/ppermute | solution.py:210
  469.4 16.1 %collective-permute-done.27 = bf16[512,2048]{1,0:T(8,128)(2,1)S(1)} collective-permute-done((bf16[512,2048]{1,0:T(8,128)(2,1)S(1)}, bf16[512,2048]{1,0:T(8,128)(2,1)S(1)}, u32[]{:S(2)}, u32[]{:S(2)}) %collective-permute-start.27) | collective-permute-done | bytes 2097184 | tf_op jit(solution)/shard_map/ppermute | solution.py:210
  488.2 19.8 %collective-permute-done.20 = bf16[512,2048]{1,0:T(8,128)(2,1)S(1)} collective-permute-done((bf16[512,2048]{1,0:T(8,128)(2,1)S(1)}, bf16[512,2048]{1,0:T(8,128)(2,1)S(1)}, u32[]{:S(2)}, u32[]{:S(2)}) %collective-permute-start.20) | collective-permute-done | bytes 2097184 | tf_op jit(solution)/shard_map/ppermute | solution.py:210
  519.3 19.9 %collective-permute-done.30 = bf16[512,2048]{1,0:T(8,128)(2,1)S(1)} collective-permute-done((bf16[512,2048]{1,0:T(8,128)(2,1)S(1)}, bf16[512,2048]{1,0:T(8,128)(2,1)S(1)}, u32[]{:S(2)}, u32[]{:S(2)}) %collective-permute-start.30) | collective-permute-done | bytes 2097184 | tf_op jit(solution)/shard_map/ppermute | solution.py:210
  540.0 7.6 collective-permute-done.31
  549.4 12.0 %collective-permute-done.33 = bf16[256,2048]{1,0:T(8,128)(2,1)S(1)} collective-permute-done((bf16[256,2048]{1,0:T(8,128)(2,1)S(1)}, bf16[256,2048]{1,0:T(8,128)(2,1)S(1)}, u32[]{:S(2)}, u32[]{:S(2)}) %collective-permute-start.33) | collective-permute-done | bytes 1048608 | tf_op jit(solution)/shard_map/ppermute | solution.py:210
  565.4 16.4 %attend_back.1 = (bf16[1024,768]{1,0:T(8,128)(2,1)S(1)}, bf16[1024,768]{1,0:T(8,128)(2,1)S(1)}) custom-call(s32[1024,8]{1,0:T(8,128)S(1)} %copy.117.info_ref, bf16[1024,768]{1,0:T(8,128)(2,1)S(1)} %copy-done.7, bf16[1024,768]{1,0:T(8,128)(2,1)S(1)} %copy-done.5, bf16[1024,256]{1,0:T(8,128)(2,1)S(1)} %convolution_convert_fusion.5.g0_ref, ...), custom_call_target="tpu_custom_call" | custom-call | flops 4026531840 | bytes 12582912 | tf_op jit(solution)/shard_map/attend_back/pallas_call | solution.py:162
  583.2 5.9 convolution_convert_fusion.1
  592.8 5.9 convolution_convert_fusion
  601.0 7.5 pad_maximum_fusion
  608.6 12.3 %copy.126 = bf16[2,2048,1024]{2,1,0:T(8,128)(2,1)} copy(bf16[2,2048,1024]{1,2,0:T(8,128)(2,1)} %pad_maximum_fusion) | data formatting | bytes 16777216 | tf_op jit(solution)/shard_map/stack | solution.py:325
  620.9 5.4 fusion.47
  626.3 5.6 add_convert_fusion
  634.3 18.8 %collective-permute-done.36 = bf16[256,2048]{1,0:T(8,128)(2,1)S(1)} collective-permute-done((bf16[256,2048]{1,0:T(8,128)(2,1)S(1)}, bf16[256,2048]{1,0:T(8,128)(2,1)S(1)}, u32[]{:S(2)}, u32[]{:S(2)}) %collective-permute-start.36) | collective-permute-done | bytes 1048608 | tf_op jit(solution)/shard_map/ppermute | solution.py:210
  660.6 21.8 %collective-permute-done.35 = bf16[512,2048]{1,0:T(8,128)(2,1)S(1)} collective-permute-done((bf16[512,2048]{1,0:T(8,128)(2,1)S(1)}, bf16[512,2048]{1,0:T(8,128)(2,1)S(1)}, u32[]{:S(2)}, u32[]{:S(2)}) %collective-permute-start.35) | collective-permute-done | bytes 2097184 | tf_op jit(solution)/shard_map/ppermute | solution.py:210
  697.4 4.7 collective-permute-done.40
  708.4 6.8 collective-permute-done.42
  718.3 9.1 %collective-permute-done.43 = f32[160,128]{1,0:T(8,128)S(1)} collective-permute-done((f32[160,128]{1,0:T(8,128)S(1)}, f32[160,128]{1,0:T(8,128)S(1)}, u32[]{:S(2)}, u32[]{:S(2)}) %collective-permute-start.43) | collective-permute-done | bytes 81952 | tf_op jit(solution)/shard_map/ppermute | solution.py:368
  754.0 115.7 %reduce-scatter.4.cloned.1.call-done = bf16[512,1024]{1,0:T(8,128)(2,1)} async-done(((bf16[4096,1024]{1,0:T(8,128)(2,1)}), bf16[512,1024]{1,0:T(8,128)(2,1)}) %reduce-scatter.4.cloned.1.call-update) | async-done | bytes 1048592 | tf_op jit(solution)/shard_map/reduce_scatter | solution.py:264
  881.3 6.6 collective-permute-done.45
  (429 shorter events, 216.5 us)
Async XLA Ops:
  7.2 130.6 %all-gather.5.cloned.1.call-start = ((), (), s32[]{:S(2)}) async-start(), calls=%async_computation.3 | async-start | bytes 7077888 | tf_op jit(solution)/shard_map/all_gather | solution.py:260
  12.0 10.6 %collective-permute-start.5 = (bf16[128,768]{0,1:T(8,128)(2,1)S(1)}, bf16[128,768]{0,1:T(8,128)(2,1)S(1)}, u32[]{:S(2)}, u32[]{:S(2)}) collective-permute-start(bf16[128,768]{0,1:T(8,128)(2,1)S(1)} %get-tuple-element.149), channel_id=1, source_target_pairs={{0,4},{1,5},{2,6},{3,7},{4,0},{5,1},{6,2},{7,3},{8,12},{9,13},{10,... | collective-permute-start | bytes 589832 | tf_op jit(solution)/shard_map/ppermute | solution.py:210
  23.6 138.3 %all-gather.7.cloned.1.call-start = ((), (), s32[]{:S(2)}) async-start(), calls=%async_computation.4 | async-start | bytes 2359296 | tf_op jit(solution)/shard_map/all_gather | solution.py:260
  26.8 16.3 %collective-permute-start.7 = (bf16[128,2304]{1,0:T(8,128)(2,1)S(1)}, bf16[128,2304]{1,0:T(8,128)(2,1)S(1)}, u32[]{:S(2)}, u32[]{:S(2)}) collective-permute-start(bf16[128,2304]{1,0:T(8,128)(2,1)S(1)} %bitcast.181), channel_id=1, source_target_pairs={{0,2},{1,3},{2,0},{3,1},{4,6},{5,7},{6,4},{7,5},{8,10},{9,11},{10,... | collective-permute-start | bytes 1769480 | tf_op jit(solution)/shard_map/ppermute | solution.py:210
  28.3 26.6 %collective-permute-start.8 = (bf16[128,2304]{1,0:T(8,128)(2,1)S(1)}, bf16[128,2304]{1,0:T(8,128)(2,1)S(1)}, u32[]{:S(2)}, u32[]{:S(2)}) collective-permute-start(bf16[128,2304]{1,0:T(8,128)(2,1)S(1)} %bitcast.182), channel_id=1, source_target_pairs={{0,4},{1,5},{2,6},{3,7},{4,0},{5,1},{6,2},{7,3},{8,12},{9,13},{10,... | collective-permute-start | bytes 1769480 | tf_op jit(solution)/shard_map/ppermute | solution.py:210
  30.3 25.5 %collective-permute-start.9 = (bf16[128,2304]{1,0:T(8,128)(2,1)}, bf16[128,2304]{1,0:T(8,128)(2,1)}, u32[]{:S(2)}, u32[]{:S(2)}) collective-permute-start(bf16[128,2304]{1,0:T(8,128)(2,1)} %bitcast.183), channel_id=1, source_target_pairs={{0,6},{1,7},{2,4},{3,5},{4,2},{5,3},{6,0},{7,1},{8,14},{9,15},{10,... | collective-permute-start | bytes 1769480 | tf_op jit(solution)/shard_map/ppermute | solution.py:210
  59.2 261.4 %all-gather.9.cloned.1.call-start = ((), (), s32[]{:S(2)}) async-start(), calls=%async_computation.5 | async-start | bytes 9437184 | tf_op jit(solution)/shard_map/all_gather | solution.py:260
  63.2 296.7 %all-gather.11.cloned.1.call-start = ((), (), s32[]{:S(2)}) async-start(), calls=%async_computation.6 | async-start | bytes 9437184 | tf_op jit(solution)/shard_map/all_gather | solution.py:260
  66.6 66.5 %collective-permute-start.2 = (bf16[512,2048]{1,0:T(8,128)(2,1)}, bf16[512,2048]{1,0:T(8,128)(2,1)}, u32[]{:S(2)}, u32[]{:S(2)}) collective-permute-start(bf16[512,2048]{1,0:T(8,128)(2,1)} %fusion.7), channel_id=1, source_target_pairs={{0,0},{1,2},{2,1},{3,3},{4,4},{5,6},{6,5},{7,7},{8,8},{9,10},{10,9... | collective-permute-start | bytes 6291464 | tf_op jit(solution)/shard_map/ppermute | solution.py:210
  83.8 52.5 %collective-permute-start.3 = (bf16[512,2048]{1,0:T(8,128)(2,1)}, bf16[512,2048]{1,0:T(8,128)(2,1)S(1)}, u32[]{:S(2)}, u32[]{:S(2)}) collective-permute-start(bf16[512,2048]{1,0:T(8,128)(2,1)} %fusion.7), channel_id=1, source_target_pairs={{0,4},{1,6},{2,5},{3,7},{4,0},{5,2},{6,1},{7,3},{8,12},{9,14},{10,... | collective-permute-start | bytes 6291464 | tf_op jit(solution)/shard_map/ppermute | solution.py:210
  87.6 45.3 %collective-permute-start.1 = (s32[512,8]{0,1:T(8,128)S(1)}, s32[512,8]{0,1:T(8,128)S(1)}, u32[]{:S(2)}, u32[]{:S(2)}) collective-permute-start(s32[512,8]{0,1:T(8,128)S(1)} %pad.4), channel_id=1, source_target_pairs={{0,4},{1,6},{2,5},{3,7},{4,0},{5,2},{6,1},{7,3},{8,12},{9,14},{10,... | collective-permute-start | bytes 49160 | tf_op jit(solution)/shard_map/ppermute | solution.py:210
  171.2 17.0 %collective-permute-start.12 = (bf16[256,2048]{1,0:T(8,128)(2,1)}, bf16[256,2048]{1,0:T(8,128)(2,1)}, u32[]{:S(2)}, u32[]{:S(2)}) collective-permute-start(bf16[256,2048]{1,0:T(8,128)(2,1)} %get-tuple-element.109), channel_id=1, source_target_pairs={{1,3},{2,0},{5,7},{6,4},{9,11},{10,8},{13,15},{14,12},{17,19},{18,... | collective-permute-start | bytes 3145736 | tf_op jit(solution)/shard_map/ppermute | solution.py:210
  173.5 555.2 %reduce-scatter.8.cloned.1.call-start = ((), (), s32[]{:S(2)}) async-start(), calls=%async_computation.9 | async-start | bytes 9437184 | tf_op jit(solution)/shard_map/reduce_scatter | solution.py:264
  191.5 28.2 %collective-permute-start.11 = (bf16[512,2048]{1,0:T(8,128)(2,1)S(1)}, bf16[512,2048]{1,0:T(8,128)(2,1)S(1)}, u32[]{:S(2)}, u32[]{:S(2)}) collective-permute-start(bf16[512,2048]{1,0:T(8,128)(2,1)S(1)} %pad_maximum_fusion.6), channel_id=1, source_target_pairs={{1,3},{2,0},{5,7},{6,4},{9,11},{10,8},{13,15},{14,12},{17,19},{18,... | collective-permute-start | bytes 6291464 | tf_op jit(solution)/shard_map/ppermute | solution.py:210
  193.3 27.9 %collective-permute-start.13 = (bf16[512,2048]{1,0:T(8,128)(2,1)S(1)}, bf16[512,2048]{1,0:T(8,128)(2,1)S(1)}, u32[]{:S(2)}, u32[]{:S(2)}) collective-permute-start(bf16[512,2048]{1,0:T(8,128)(2,1)S(1)} %pad_maximum_fusion.7), channel_id=1, source_target_pairs={{0,4},{3,7},{4,0},{7,3},{8,12},{11,15},{12,8},{15,11},{16,20},{19,... | collective-permute-start | bytes 6291464 | tf_op jit(solution)/shard_map/ppermute | solution.py:210
  225.8 45.6 %collective-permute-start.14 = (bf16[512,2048]{1,0:T(8,128)(2,1)}, bf16[512,2048]{1,0:T(8,128)(2,1)}, u32[]{:S(2)}, u32[]{:S(2)}) collective-permute-start(bf16[512,2048]{1,0:T(8,128)(2,1)} %add_convert_fusion.5), channel_id=1, source_target_pairs={{0,2},{3,1},{4,6},{7,5},{8,10},{11,9},{12,14},{15,13},{16,18},{19,... | collective-permute-start | bytes 6291464 | tf_op jit(solution)/shard_map/ppermute | solution.py:210
  228.4 45.1 %collective-permute-start.15 = (bf16[512,2048]{1,0:T(8,128)(2,1)}, bf16[512,2048]{1,0:T(8,128)(2,1)S(1)}, u32[]{:S(2)}, u32[]{:S(2)}) collective-permute-start(bf16[512,2048]{1,0:T(8,128)(2,1)} %add_convert_fusion.5), channel_id=1, source_target_pairs={{0,4},{3,7},{4,0},{7,3},{8,12},{11,15},{12,8},{15,11},{16,20},{19,... | collective-permute-start | bytes 6291464 | tf_op jit(solution)/shard_map/ppermute | solution.py:210
  232.6 47.5 %collective-permute-start.24 = (bf16[512,2048]{1,0:T(8,128)(2,1)}, bf16[512,2048]{1,0:T(8,128)(2,1)}, u32[]{:S(2)}, u32[]{:S(2)}) collective-permute-start(bf16[512,2048]{1,0:T(8,128)(2,1)} %fusion.25), channel_id=1, source_target_pairs={{0,0},{1,2},{2,1},{3,3},{4,4},{5,6},{6,5},{7,7},{8,8},{9,10},{10,9... | collective-permute-start | bytes 6291464 | tf_op jit(solution)/shard_map/ppermute | solution.py:210
  249.8 63.0 %collective-permute-start.25 = (bf16[512,2048]{1,0:T(8,128)(2,1)}, bf16[512,2048]{1,0:T(8,128)(2,1)}, u32[]{:S(2)}, u32[]{:S(2)}) collective-permute-start(bf16[512,2048]{1,0:T(8,128)(2,1)} %fusion.25), channel_id=1, source_target_pairs={{0,4},{1,6},{2,5},{3,7},{4,0},{5,2},{6,1},{7,3},{8,12},{9,14},{10,... | collective-permute-start | bytes 6291464 | tf_op jit(solution)/shard_map/ppermute | solution.py:210
  272.8 45.7 %collective-permute-start.16 = (bf16[256,2048]{1,0:T(8,128)(2,1)S(1)}, bf16[256,2048]{1,0:T(8,128)(2,1)S(1)}, u32[]{:S(2)}, u32[]{:S(2)}) collective-permute-start(bf16[256,2048]{1,0:T(8,128)(2,1)S(1)} %slice.307), channel_id=1, source_target_pairs={{1,5},{2,6},{5,1},{6,2},{9,13},{10,14},{13,9},{14,10},{17,21},{18,... | collective-permute-start | bytes 3145736 | tf_op jit(solution)/shard_map/ppermute | solution.py:210
  273.6 44.8 %collective-permute-start.17 = (bf16[256,2048]{1,0:T(8,128)(2,1)S(1)}, bf16[256,2048]{1,0:T(8,128)(2,1)S(1)}, u32[]{:S(2)}, u32[]{:S(2)}) collective-permute-start(bf16[256,2048]{1,0:T(8,128)(2,1)S(1)} %slice.308), channel_id=1, source_target_pairs={{0,2},{3,1},{4,6},{7,5},{8,10},{11,9},{12,14},{15,13},{16,18},{19,... | collective-permute-start | bytes 3145736 | tf_op jit(solution)/shard_map/ppermute | solution.py:210
  359.9 377.7 %reduce-scatter.6.cloned.1.call-start = ((), (), s32[]{:S(2)}) async-start(), calls=%async_computation.8 | async-start | bytes 9437184 | tf_op jit(solution)/shard_map/reduce_scatter | solution.py:264
  401.5 44.1 %collective-permute-start.26 = (bf16[256,2048]{1,0:T(8,128)(2,1)S(1)}, bf16[256,2048]{1,0:T(8,128)(2,1)}, u32[]{:S(2)}, u32[]{:S(2)}) collective-permute-start(bf16[256,2048]{1,0:T(8,128)(2,1)S(1)} %get-tuple-element.100), channel_id=1, source_target_pairs={{1,5},{2,6},{5,1},{6,2},{9,13},{10,14},{13,9},{14,10},{17,21},{18,... | collective-permute-start | bytes 3145736 | tf_op jit(solution)/shard_map/ppermute | solution.py:210
  403.2 42.4 %collective-permute-start.28 = (bf16[256,2048]{1,0:T(8,128)(2,1)}, bf16[256,2048]{1,0:T(8,128)(2,1)}, u32[]{:S(2)}, u32[]{:S(2)}) collective-permute-start(bf16[256,2048]{1,0:T(8,128)(2,1)} %get-tuple-element.99), channel_id=1, source_target_pairs={{1,3},{2,0},{5,7},{6,4},{9,11},{10,8},{13,15},{14,12},{17,19},{18,... | collective-permute-start | bytes 3145736 | tf_op jit(solution)/shard_map/ppermute | solution.py:210
  425.7 444.1 %reduce-scatter.4.cloned.1.call-start = ((), (), s32[]{:S(2)}) async-start(), calls=%async_computation.7 | async-start | bytes 9437184 | tf_op jit(solution)/shard_map/reduce_scatter | solution.py:264
  444.1 19.0 %collective-permute-start.21 = (bf16[256,2048]{1,0:T(8,128)(2,1)S(1)}, bf16[256,2048]{1,0:T(8,128)(2,1)S(1)}, u32[]{:S(2)}, u32[]{:S(2)}) collective-permute-start(bf16[256,2048]{1,0:T(8,128)(2,1)S(1)} %get-tuple-element.104), channel_id=1, source_target_pairs={{1,3},{2,0},{5,7},{6,4},{9,11},{10,8},{13,15},{14,12},{17,19},{18,... | collective-permute-start | bytes 3145736 | tf_op jit(solution)/shard_map/ppermute | solution.py:210
  448.1 37.5 %collective-permute-start.27 = (bf16[512,2048]{1,0:T(8,128)(2,1)S(1)}, bf16[512,2048]{1,0:T(8,128)(2,1)S(1)}, u32[]{:S(2)}, u32[]{:S(2)}) collective-permute-start(bf16[512,2048]{1,0:T(8,128)(2,1)S(1)} %pad_maximum_fusion.10), channel_id=1, source_target_pairs={{1,3},{2,0},{5,7},{6,4},{9,11},{10,8},{13,15},{14,12},{17,19},{18,... | collective-permute-start | bytes 6291464 | tf_op jit(solution)/shard_map/ppermute | solution.py:210
  449.5 36.0 %collective-permute-start.29 = (bf16[512,2048]{1,0:T(8,128)(2,1)S(1)}, bf16[512,2048]{1,0:T(8,128)(2,1)S(1)}, u32[]{:S(2)}, u32[]{:S(2)}) collective-permute-start(bf16[512,2048]{1,0:T(8,128)(2,1)S(1)} %pad_maximum_fusion.11), channel_id=1, source_target_pairs={{0,4},{3,7},{4,0},{7,3},{8,12},{11,15},{12,8},{15,11},{16,20},{19,... | collective-permute-start | bytes 6291464 | tf_op jit(solution)/shard_map/ppermute | solution.py:210
  464.0 43.9 %collective-permute-start.20 = (bf16[512,2048]{1,0:T(8,128)(2,1)S(1)}, bf16[512,2048]{1,0:T(8,128)(2,1)S(1)}, u32[]{:S(2)}, u32[]{:S(2)}) collective-permute-start(bf16[512,2048]{1,0:T(8,128)(2,1)S(1)} %pad_maximum_fusion.8), channel_id=1, source_target_pairs={{1,3},{2,0},{5,7},{6,4},{9,11},{10,8},{13,15},{14,12},{17,19},{18,... | collective-permute-start | bytes 6291464 | tf_op jit(solution)/shard_map/ppermute | solution.py:210
  465.9 42.1 %collective-permute-start.22 = (bf16[512,2048]{1,0:T(8,128)(2,1)S(1)}, bf16[512,2048]{1,0:T(8,128)(2,1)S(1)}, u32[]{:S(2)}, u32[]{:S(2)}) collective-permute-start(bf16[512,2048]{1,0:T(8,128)(2,1)S(1)} %pad_maximum_fusion.9), channel_id=1, source_target_pairs={{0,4},{3,7},{4,0},{7,3},{8,12},{11,15},{12,8},{15,11},{16,20},{19,... | collective-permute-start | bytes 6291464 | tf_op jit(solution)/shard_map/ppermute | solution.py:210
  514.3 25.0 %collective-permute-start.30 = (bf16[512,2048]{1,0:T(8,128)(2,1)S(1)}, bf16[512,2048]{1,0:T(8,128)(2,1)S(1)}, u32[]{:S(2)}, u32[]{:S(2)}) collective-permute-start(bf16[512,2048]{1,0:T(8,128)(2,1)S(1)} %fusion.76), channel_id=1, source_target_pairs={{0,2},{3,1},{4,6},{7,5},{8,10},{11,9},{12,14},{15,13},{16,18},{19,... | collective-permute-start | bytes 6291464 | tf_op jit(solution)/shard_map/ppermute | solution.py:210
  515.8 31.8 %collective-permute-start.31 = (bf16[512,2048]{1,0:T(8,128)(2,1)S(1)}, bf16[512,2048]{1,0:T(8,128)(2,1)S(1)}, u32[]{:S(2)}, u32[]{:S(2)}) collective-permute-start(bf16[512,2048]{1,0:T(8,128)(2,1)S(1)} %fusion.76), channel_id=1, source_target_pairs={{0,4},{3,7},{4,0},{7,3},{8,12},{11,15},{12,8},{15,11},{16,20},{19,... | collective-permute-start | bytes 6291464 | tf_op jit(solution)/shard_map/ppermute | solution.py:210
  539.3 10.1 %collective-permute-start.32 = (bf16[256,2048]{1,0:T(8,128)(2,1)S(1)}, bf16[256,2048]{1,0:T(8,128)(2,1)S(1)}, u32[]{:S(2)}, u32[]{:S(2)}) collective-permute-start(bf16[256,2048]{1,0:T(8,128)(2,1)S(1)} %slice.331), channel_id=1, source_target_pairs={{1,5},{2,6},{5,1},{6,2},{9,13},{10,14},{13,9},{14,10},{17,21},{18,... | collective-permute-start | bytes 3145736 | tf_op jit(solution)/shard_map/ppermute | solution.py:210
  547.7 13.6 %collective-permute-start.33 = (bf16[256,2048]{1,0:T(8,128)(2,1)S(1)}, bf16[256,2048]{1,0:T(8,128)(2,1)S(1)}, u32[]{:S(2)}, u32[]{:S(2)}) collective-permute-start(bf16[256,2048]{1,0:T(8,128)(2,1)S(1)} %slice.332), channel_id=1, source_target_pairs={{0,2},{3,1},{4,6},{7,5},{8,10},{11,9},{12,14},{15,13},{16,18},{19,... | collective-permute-start | bytes 3145736 | tf_op jit(solution)/shard_map/ppermute | solution.py:210
  633.0 20.1 %collective-permute-start.36 = (bf16[256,2048]{1,0:T(8,128)(2,1)S(1)}, bf16[256,2048]{1,0:T(8,128)(2,1)S(1)}, u32[]{:S(2)}, u32[]{:S(2)}) collective-permute-start(bf16[256,2048]{1,0:T(8,128)(2,1)S(1)} %get-tuple-element.93), channel_id=1, source_target_pairs={{1,3},{2,0},{5,7},{6,4},{9,11},{10,8},{13,15},{14,12},{17,19},{18,... | collective-permute-start | bytes 3145736 | tf_op jit(solution)/shard_map/ppermute | solution.py:210
  654.2 28.2 %collective-permute-start.35 = (bf16[512,2048]{1,0:T(8,128)(2,1)S(1)}, bf16[512,2048]{1,0:T(8,128)(2,1)S(1)}, u32[]{:S(2)}, u32[]{:S(2)}) collective-permute-start(bf16[512,2048]{1,0:T(8,128)(2,1)S(1)} %pad_maximum_fusion.12), channel_id=1, source_target_pairs={{1,3},{2,0},{5,7},{6,4},{9,11},{10,8},{13,15},{14,12},{17,19},{18,... | collective-permute-start | bytes 6291464 | tf_op jit(solution)/shard_map/ppermute | solution.py:210
  656.0 27.9 %collective-permute-start.37 = (bf16[512,2048]{1,0:T(8,128)(2,1)S(1)}, bf16[512,2048]{1,0:T(8,128)(2,1)S(1)}, u32[]{:S(2)}, u32[]{:S(2)}) collective-permute-start(bf16[512,2048]{1,0:T(8,128)(2,1)S(1)} %pad_maximum_fusion.13), channel_id=1, source_target_pairs={{0,4},{3,7},{4,0},{7,3},{8,12},{11,15},{12,8},{15,11},{16,20},{19,... | collective-permute-start | bytes 6291464 | tf_op jit(solution)/shard_map/ppermute | solution.py:210
  658.0 58.8 %collective-permute-start.23 = (bf16[512,2048]{1,0:T(8,128)(2,1)S(1)}, bf16[512,2048]{1,0:T(8,128)(2,1)}, u32[]{:S(2)}, u32[]{:S(2)}) collective-permute-start(bf16[512,2048]{1,0:T(8,128)(2,1)S(1)} %copy-done.25), channel_id=1, source_target_pairs={{0,1},{3,2},{4,5},{7,6},{8,9},{11,10},{12,13},{15,14},{16,17},{19,... | collective-permute-start | bytes 6291464 | tf_op jit(solution)/shard_map/ppermute | solution.py:210
  692.1 42.1 %collective-permute-start.38 = (bf16[512,2048]{1,0:T(8,128)(2,1)}, bf16[512,2048]{1,0:T(8,128)(2,1)}, u32[]{:S(2)}, u32[]{:S(2)}) collective-permute-start(bf16[512,2048]{1,0:T(8,128)(2,1)} %get-tuple-element.89), channel_id=1, source_target_pairs={{0,1},{3,2},{4,5},{7,6},{8,9},{11,10},{12,13},{15,14},{16,17},{19,... | collective-permute-start | bytes 6291464 | tf_op jit(solution)/shard_map/ppermute | solution.py:210
  715.2 12.2 %collective-permute-start.43 = (f32[160,128]{1,0:T(8,128)S(1)}, f32[160,128]{1,0:T(8,128)S(1)}, u32[]{:S(2)}, u32[]{:S(2)}) collective-permute-start(f32[160,128]{1,0:T(8,128)S(1)} %add.309), channel_id=1, source_target_pairs={{0,16},{8,24},{16,0},{24,8},{1,17},{9,25},{17,1},{25,9},{2,18},{10... | collective-permute-start | bytes 245768 | tf_op jit(solution)/shard_map/ppermute | solution.py:368
  730.2 10.1 %collective-permute-start.50 = (bf16[128,1024]{0,1:T(8,128)(2,1)S(1)}, bf16[128,1024]{0,1:T(8,128)(2,1)S(1)}, u32[]{:S(2)}, u32[]{:S(2)}) collective-permute-start(bf16[128,1024]{0,1:T(8,128)(2,1)S(1)} %bitcast.188), channel_id=1, source_target_pairs={{0,2},{1,3},{2,0},{3,1},{4,6},{5,7},{6,4},{7,5},{8,10},{9,11},{10,... | collective-permute-start | bytes 786440 | tf_op jit(solution)/shard_map/ppermute | solution.py:210
  730.5 15.1 %collective-permute-start.51 = (bf16[128,1024]{0,1:T(8,128)(2,1)S(1)}, bf16[128,1024]{0,1:T(8,128)(2,1)}, u32[]{:S(2)}, u32[]{:S(2)}) collective-permute-start(bf16[128,1024]{0,1:T(8,128)(2,1)S(1)} %bitcast.187), channel_id=1, source_target_pairs={{0,4},{1,5},{2,6},{3,7},{4,0},{5,1},{6,2},{7,3},{8,12},{9,13},{10,... | collective-permute-start | bytes 786440 | tf_op jit(solution)/shard_map/ppermute | solution.py:210
  730.7 14.9 %collective-permute-start.52 = (bf16[128,1024]{0,1:T(8,128)(2,1)S(1)}, bf16[128,1024]{0,1:T(8,128)(2,1)}, u32[]{:S(2)}, u32[]{:S(2)}) collective-permute-start(bf16[128,1024]{0,1:T(8,128)(2,1)S(1)} %bitcast.189), channel_id=1, source_target_pairs={{0,6},{1,7},{2,4},{3,5},{4,2},{5,3},{6,0},{7,1},{8,14},{9,15},{10,... | collective-permute-start | bytes 786440 | tf_op jit(solution)/shard_map/ppermute | solution.py:210
  739.1 10.8 %collective-permute-start.47 = (bf16[128,1024]{0,1:T(8,128)(2,1)S(1)}, bf16[128,1024]{0,1:T(8,128)(2,1)}, u32[]{:S(2)}, u32[]{:S(2)}) collective-permute-start(bf16[128,1024]{0,1:T(8,128)(2,1)S(1)} %bitcast.190), channel_id=1, source_target_pairs={{0,2},{1,3},{2,0},{3,1},{4,6},{5,7},{6,4},{7,5},{8,10},{9,11},{10,... | collective-permute-start | bytes 786440 | tf_op jit(solution)/shard_map/ppermute | solution.py:210
  739.3 13.5 %collective-permute-start.48 = (bf16[128,1024]{0,1:T(8,128)(2,1)S(1)}, bf16[128,1024]{0,1:T(8,128)(2,1)}, u32[]{:S(2)}, u32[]{:S(2)}) collective-permute-start(bf16[128,1024]{0,1:T(8,128)(2,1)S(1)} %bitcast.191), channel_id=1, source_target_pairs={{0,4},{1,5},{2,6},{3,7},{4,0},{5,1},{6,2},{7,3},{8,12},{9,13},{10,... | collective-permute-start | bytes 786440 | tf_op jit(solution)/shard_map/ppermute | solution.py:210
  740.3 12.6 %collective-permute-start.49 = (bf16[128,1024]{0,1:T(8,128)(2,1)S(1)}, bf16[128,1024]{0,1:T(8,128)(2,1)}, u32[]{:S(2)}, u32[]{:S(2)}) collective-permute-start(bf16[128,1024]{0,1:T(8,128)(2,1)S(1)} %bitcast.192), channel_id=1, source_target_pairs={{0,6},{1,7},{2,4},{3,5},{4,2},{5,3},{6,0},{7,1},{8,14},{9,15},{10,... | collective-permute-start | bytes 786440 | tf_op jit(solution)/shard_map/ppermute | solution.py:210
  874.0 13.9 %collective-permute-start.45 = (bf16[128,1024]{0,1:T(8,128)(2,1)}, bf16[128,1024]{0,1:T(8,128)(2,1)}, u32[]{:S(2)}, u32[]{:S(2)}) collective-permute-start(bf16[128,1024]{0,1:T(8,128)(2,1)} %bitcast.41), channel_id=1, source_target_pairs={{0,4},{1,5},{2,6},{3,7},{4,0},{5,1},{6,2},{7,3},{8,12},{9,13},{10,... | collective-permute-start | bytes 786440 | tf_op jit(solution)/shard_map/ppermute | solution.py:210
  875.6 12.3 %collective-permute-start.46 = (bf16[128,1024]{0,1:T(8,128)(2,1)}, bf16[128,1024]{0,1:T(8,128)(2,1)}, u32[]{:S(2)}, u32[]{:S(2)}) collective-permute-start(bf16[128,1024]{0,1:T(8,128)(2,1)} %bitcast.42), channel_id=1, source_target_pairs={{0,6},{1,7},{2,4},{3,5},{4,2},{5,3},{6,0},{7,1},{8,14},{9,15},{10,... | collective-permute-start | bytes 786440 | tf_op jit(solution)/shard_map/ppermute | solution.py:210
  (93 other events, 1239.8 us)
Sparse Core Ops, SparseCore 0:
  23.8 65.0 all-gather.4
  91.0 27.7 all-gather.6
  121.0 81.5 all-gather.8
  204.6 80.5 all-gather.10
  360.0 166.0 reduce-scatter.7
  528.2 167.8 reduce-scatter.5
  698.4 171.2 reduce-scatter.3

commit v2 on v1

v2 whole, which is shorter than its diff:
```python
import functools

import jax
import jax.numpy as jnp
from jax import lax
from jax.experimental import pallas as pl
from jax.experimental.pallas import tpu as pltpu
from jax.sharding import Mesh
from jax.sharding import PartitionSpec as P

HEAD = 128
WINDOW = 256
CHUNK = 128
SCALE = HEAD**-0.5
ALL = ("z", "y", "x", "c")
BF = jnp.bfloat16
F32 = jnp.float32
ACROSS = (((1,), (1,)), ((), ()))
ROWS = (((0,), (0,)), ((), ()))
PLAIN = (((1,), (0,)), ((), ()))


def dot(a, b, dims=PLAIN):
    return lax.dot_general(a, b, dims, preferred_element_type=F32)


def pairs_of(depth, route):
    def flat(z, y, x, c):
        return ((z * 2 + y) * 2 + x) * 2 + c

    found = []
    for z in range(depth):
        for y in range(2):
            for x in range(2):
                for c in range(2):
                    goal = route(y, x, c)
                    if goal is not None:
                        found.append((flat(z, y, x, c), flat(z, *goal)))
    return found


def bounds_of(group_sizes, prefix_lengths, solution_lengths, row_count):
    entries = solution_lengths.shape[1]
    position = jnp.arange(entries, dtype=jnp.int32)
    counted = jnp.where(position[None, :] < group_sizes[:, None], solution_lengths, 0)
    pieces = jnp.concatenate([prefix_lengths[:, None], counted], axis=1)
    flat = pieces.reshape(-1)
    count = flat.shape[0]
    index = jnp.arange(count, dtype=jnp.int32)
    ends = jnp.sum(jnp.where(index[None, :] <= index[:, None], flat[None, :], 0), axis=1)
    slot = jnp.arange(row_count, dtype=jnp.int32)
    passed = slot[:, None] >= ends[None, :]
    piece_start = jnp.max(jnp.where(passed, ends[None, :], 0), axis=1)
    group_end = ends.reshape(pieces.shape)[:, -1]
    over = slot[:, None] >= group_end[None, :]
    group_start = jnp.max(jnp.where(over, group_end[None, :], 0), axis=1)
    group_index = jnp.sum(over.astype(jnp.int32), axis=1)
    member = group_index[:, None] == jnp.arange(pieces.shape[0], dtype=jnp.int32)[None, :]
    prefix_end = group_start + jnp.sum(jnp.where(member, prefix_lengths[None, :], 0), axis=1)
    live = slot < ends[-1]
    piece_start = jnp.where(live, piece_start, slot)
    group_start = jnp.where(live, group_start, slot)
    prefix_end = jnp.where(live, prefix_end, slot)
    return jnp.stack([group_start, prefix_end, piece_start], axis=1), live


def key_range(i):
    return max(0, i * CHUNK - WINDOW), (i + 1) * CHUNK


def allowed_tile(info, i, lo, hi):
    rows = info[i * CHUNK : (i + 1) * CHUNK, :]
    start, stop, piece = rows[:, 0:1], rows[:, 1:2], rows[:, 2:3]
    s = lax.broadcasted_iota(jnp.int32, (CHUNK, hi - lo), 0) + i * CHUNK
    t = lax.broadcasted_iota(jnp.int32, (CHUNK, hi - lo), 1) + lo
    return (t <= s) & ((t >= piece) | ((t >= start) & (t < stop)))


def tiles_of(p_ref, width):
    found = []
    for i in range(p_ref.shape[0] // CHUNK):
        lo, hi = key_range(i)
        rows = slice(i * CHUNK, (i + 1) * CHUNK)
        for h in range(width // HEAD):
            qs, ks, vs = (slice(c * width + h * HEAD, c * width + (h + 1) * HEAD) for c in range(3))
            found.append((i, rows, slice(lo, hi), qs, ks, vs))
    return found


def masks_of(info_ref, block):
    info = info_ref[...]
    return [allowed_tile(info, i, *key_range(i)) for i in range(block // CHUNK)]


def attend_kernel(info_ref, p_ref, o_ref, l_ref):
    block, width = p_ref.shape
    width = width // 3
    masks = masks_of(info_ref, block)
    tiles = tiles_of(p_ref, width)
    raw = [dot(p_ref[rows, qs], p_ref[keys, ks], ACROSS) for _, rows, keys, qs, ks, _ in tiles]
    low = []
    for (i, rows, _, qs, _, _), score in zip(tiles, raw):
        scores = jnp.where(masks[i], score * SCALE, -1e30)
        peak = jnp.max(scores, axis=-1, keepdims=True)
        e = jnp.exp(scores - peak)
        total = jnp.sum(e, axis=-1, keepdims=True)
        low.append((e * (1.0 / total)).astype(BF))
        l_ref[rows, qs] = jnp.broadcast_to(peak + jnp.log(total), (CHUNK, HEAD))
    for (_, rows, keys, qs, _, vs), soft in zip(tiles, low):
        o_ref[rows, qs] = dot(soft, p_ref[keys, vs]).astype(BF)


def attend_back_kernel(info_ref, p_ref, g_ref, l_ref, d_ref, dk_ref, dv_ref):
    block, width = p_ref.shape
    width = width // 3
    masks = masks_of(info_ref, block)
    tiles = tiles_of(p_ref, width)
    dk_ref[...] = jnp.zeros_like(dk_ref)
    dv_ref[...] = jnp.zeros_like(dv_ref)
    raw = [dot(p_ref[rows, qs], p_ref[keys, ks], ACROSS) for _, rows, keys, qs, ks, _ in tiles]
    tangents = [dot(g_ref[rows, qs], p_ref[keys, vs], ACROSS) for _, rows, keys, qs, _, vs in tiles]
    kept = []
    for (i, rows, _, qs, _, _), score, tangent in zip(tiles, raw, tangents):
        scores = jnp.where(masks[i], score * SCALE, -1e30)
        soft = jnp.exp(scores - l_ref[rows, qs.start : qs.start + 1])
        back = soft * tangent
        low = (back - soft * jnp.sum(back, axis=-1, keepdims=True)).astype(BF)
        kept.append((soft.astype(BF), low))
    for (_, rows, keys, qs, ks, _), (soft, low) in zip(tiles, kept):
        d_ref[rows, qs] = (dot(low, p_ref[keys, ks]) * SCALE).astype(BF)
        dk_ref[keys, qs] += dot(low, p_ref[rows, qs], ROWS)
        dv_ref[keys, qs] += dot(soft, g_ref[rows, qs], ROWS)
    d_ref[:, width : 2 * width] = (dk_ref[...] * SCALE).astype(BF)
    d_ref[:, 2 * width :] = dv_ref[...].astype(BF)


def params(mib=48):
    return pltpu.CompilerParams(vmem_limit_bytes=mib << 20)


def cost(flops, moved, exps=0):
    return pl.CostEstimate(flops=flops, bytes_accessed=moved, transcendentals=exps)


def attend(info, projected, block):
    sides, rows, width = projected.shape
    spec = lambda n: pl.BlockSpec((None, block, n), lambda b, c: (c, b, 0))
    return pl.pallas_call(
        attend_kernel,
        grid=(rows // block, sides),
        in_specs=[pl.BlockSpec((block, info.shape[1]), lambda b, c: (b, 0)), spec(width)],
        out_specs=[spec(width // 3)] * 2,
        out_shape=[jax.ShapeDtypeStruct((sides, rows, width // 3), t) for t in (BF, F32)],
        compiler_params=params(),
        cost_estimate=cost(16 * rows * block * width, 8 * rows * width * 2, rows * block * 4),
        name="attend",
    )(info, projected)


def attend_back(info, projected, mixed_back, log_sums, block):
    sides, rows, width = projected.shape
    spec = lambda n: pl.BlockSpec((None, block, n), lambda b, c: (c, b, 0))
    return pl.pallas_call(
        attend_back_kernel,
        grid=(rows // block, sides),
        in_specs=[pl.BlockSpec((block, info.shape[1]), lambda b, c: (b, 0)), spec(width), spec(width // 3), spec(width // 3)],
        out_specs=spec(width),
        out_shape=jax.ShapeDtypeStruct((sides, rows, width), BF),
        scratch_shapes=[pltpu.VMEM((block, width // 3), F32)] * 2,
        compiler_params=params(),
        cost_estimate=cost(40 * rows * block * width, 16 * rows * width * 2, rows * block * 4),
        name="attend_back",
    )(info, projected, mixed_back, log_sums)


def steps(width, step=256):
    return [slice(j, min(j + step, width)) for j in range(0, width, step)]


def project_kernel(a_ref, w_ref, o_ref):
    for s in steps(w_ref.shape[1]):
        o_ref[:, s] = dot(a_ref[...], w_ref[:, s]).astype(BF)


def project(rows, weights, width, column):
    m, k = rows.shape
    sides = weights.shape[0]
    return pl.pallas_call(
        project_kernel,
        grid=(sides,),
        in_specs=[pl.BlockSpec((m, k), lambda c: (0, 0)), pl.BlockSpec((None, k, width), lambda c: (c, 0, column))],
        out_specs=pl.BlockSpec((None, m, width), lambda c: (c, 0, 0)),
        out_shape=jax.ShapeDtypeStruct((sides, m, width), BF),
        compiler_params=params(),
        cost_estimate=cost(2 * sides * m * k * width, 2 * (m * k + sides * k * width + sides * m * width)),
        name="project",
    )(rows, weights)


def expand_kernel(a_ref, w_ref, b_ref, o_ref, d_ref):
    root, cubic = 0.7978845608028654, 0.044715
    for s in steps(w_ref.shape[1]):
        v = dot(a_ref[...], w_ref[:, s]) + b_ref[:, s]
        square = v * v
        t = jnp.tanh(v * (root + root * cubic * square))
        half = 0.5 + 0.5 * t
        o_ref[:, s] = (v * half).astype(BF)
        d_ref[:, s] = half + v * (half * (1.0 - t)) * (root + 3.0 * root * cubic * square)


def expand(rows, weights, bias):
    m, k = rows.shape
    sides, _, n = weights.shape
    tile = min(n, 256)
    out = pl.BlockSpec((None, m, tile), lambda c, j: (c, 0, j))
    return pl.pallas_call(
        expand_kernel,
        grid=(sides, n // tile),
        in_specs=[
            pl.BlockSpec((m, k), lambda c, j: (0, 0)),
            pl.BlockSpec((None, k, tile), lambda c, j: (c, 0, j)),
            pl.BlockSpec((None, 1, tile), lambda c, j: (c, 0, j)),
        ],
        out_specs=[out, out],
        out_shape=[jax.ShapeDtypeStruct((sides, m, n), BF), jax.ShapeDtypeStruct((sides, m, n), F32)],
        compiler_params=params(),
        cost_estimate=cost(2 * sides * m * k * n, 2 * (m * k + sides * k * n) + 6 * sides * m * n, sides * m * n),
        name="expand",
    )(rows, weights, bias)


def expand_back_kernel(a_ref, w_ref, d_ref, o_ref, s_ref):
    for s in steps(w_ref.shape[1]):
        back = dot(a_ref[...], w_ref[:, s]) * d_ref[:, s]
        o_ref[:, s] = back.astype(BF)
        s_ref[:, s] = jnp.sum(back, axis=0, keepdims=True)


def expand_back(rows, weights, slope):
    m, k = rows.shape
    sides, _, n = weights.shape
    tile = min(n, 512)
    out = pl.BlockSpec((None, m, tile), lambda c, j: (c, 0, j))
    return pl.pallas_call(
        expand_back_kernel,
        grid=(sides, n // tile),
        in_specs=[
            pl.BlockSpec((m, k), lambda c, j: (0, 0)),
            pl.BlockSpec((None, k, tile), lambda c, j: (c, 0, j)),
            out,
        ],
        out_specs=[out, pl.BlockSpec((None, 1, tile), lambda c, j: (c, 0, j))],
        out_shape=[jax.ShapeDtypeStruct((sides, m, n), BF), jax.ShapeDtypeStruct((sides, 1, n), F32)],
        compiler_params=params(),
        cost_estimate=cost(2 * sides * m * k * n, 2 * (m * k + sides * k * n) + 6 * sides * m * n),
        name="expand_back",
    )(rows, weights, slope)


def contract_kernel(a_ref, w_ref, top_ref, low_ref):
    half = top_ref.shape[0]
    for s in steps(w_ref.shape[1]):
        total = dot(a_ref[0], w_ref[0, s, :], ACROSS)
        for c in range(1, a_ref.shape[0]):
            total = total + dot(a_ref[c], w_ref[c, s, :], ACROSS)
        top_ref[:, s] = total[:half].astype(BF)
        low_ref[:, s] = total[half:].astype(BF)


def contract(terms, weights, column, side):
    sides, m, n = terms.shape
    d = weights.shape[1]
    m = m // 2
    tile = min(d, 512)
    half = pl.BlockSpec((m // 2, tile), lambda j: (0, j))
    out = jax.ShapeDtypeStruct((m // 2, d), BF)
    return pl.pallas_call(
        contract_kernel,
        grid=(d // tile,),
        in_specs=[
            pl.BlockSpec((sides, m, n), lambda j: (0, side, 0)),
            pl.BlockSpec((sides, tile, n), lambda j: (0, j, column)),
        ],
        out_specs=[half, half],
        out_shape=[out, out],
        compiler_params=params(),
        cost_estimate=cost(2 * sides * m * n * d, 2 * (sides * m * n + sides * n * d + m * d)),
        name="contract",
    )(terms, weights)


def outer_kernel(pairs, adds, pick_ref, *refs):
    o_ref = refs[-1]
    start = 0
    for i in range(pairs):
        a_ref, r_ref = refs[2 * i], refs[2 * i + 1]
        for s in steps(r_ref.shape[1]):
            place = slice(start + s.start, start + s.stop)
            total = dot(a_ref[...], r_ref[:, s], ROWS)
            if adds:
                total = total + refs[2 * pairs][:, place].astype(F32)
            o_ref[:, place] = total.astype(BF)
        start += r_ref.shape[1]


def outer(pick, pairs, depth, extra=None):
    m, d = pairs[0][0].shape
    sides = pick.shape[0]
    total = sum(r.shape[2] for _, r in pairs)
    tile = d // depth
    place = pl.BlockSpec((None, None, tile, total), lambda c, i, s: (i, c, 0, 0))
    specs, args = [], []
    for a, r in pairs:
        specs.append(pl.BlockSpec((m, tile), lambda c, i, s: (0, i)))
        specs.append(pl.BlockSpec((None, m, r.shape[2]), lambda c, i, s: (s[c], 0, 0)))
        args += [a, r]
    if extra is not None:
        specs.append(place)
        args.append(extra)
    return pl.pallas_call(
        functools.partial(outer_kernel, len(pairs), extra is not None),
        grid_spec=pltpu.PrefetchScalarGridSpec(
            num_scalar_prefetch=1, grid=(sides, depth), in_specs=specs, out_specs=place
        ),
        out_shape=jax.ShapeDtypeStruct((depth, sides, tile, total), BF),
        compiler_params=params(),
        cost_estimate=cost(2 * sides * m * d * total, 2 * (m * d + sides * m * total + sides * d * total)),
        name="outer",
    )(pick, *args)


TILE = 128


def whole(v):
    return pl.BlockSpec((TILE, v.shape[1]), lambda i: (i, 0))


def vector(v):
    return pl.BlockSpec(v.shape, lambda i: (0, 0))


def halves(v):
    count = v.shape[0] // TILE
    return (
        pl.BlockSpec((TILE, v.shape[1]), lambda i: (jnp.minimum(i, count - 1), 0)),
        pl.BlockSpec((TILE, v.shape[1]), lambda i: (jnp.maximum(i - count, 0), 0)),
    )


def in_half(count, use):
    for side in range(2):
        pl.when(pl.program_id(0) // count == side)(functools.partial(use, side))


def total_of(terms, side):
    picked = [t[...].astype(F32) for t in terms[3 * side : 3 * side + 3]]
    return picked[0] + picked[1] + picked[2]


def unit(values):
    center = values - jnp.mean(values, axis=-1, keepdims=True)
    factor = lax.rsqrt(jnp.mean(center * center, axis=-1, keepdims=True) + 1e-05)
    return center * factor, factor


def unit_back(tangent, gain, xhat, factor):
    e = tangent * gain
    return factor * (
        e - jnp.mean(e, axis=-1, keepdims=True) - xhat * jnp.mean(e * xhat, axis=-1, keepdims=True)
    )


def add_sums(s_ref, rows):
    sums = jnp.concatenate([jnp.sum(r, axis=0, keepdims=True) for r in rows], axis=0)
    first = pl.program_id(0) == 0

    @pl.when(first)
    def _():
        s_ref[0 : len(rows), :] = sums

    @pl.when(jnp.logical_not(first))
    def _():
        s_ref[0 : len(rows), :] += sums


def first_kernel(count, x_ref, gain_ref, shift_ref, *outs):
    def use(side):
        xhat, _ = unit(x_ref[...].astype(F32))
        outs[side][...] = (xhat * gain_ref[...] + shift_ref[...]).astype(BF)

    in_half(count, use)


def middle_kernel(count, *refs):
    terms, (x_ref, bias_ref, gain_ref, shift_ref, m_ref), outs = refs[:6], refs[6:11], refs[11:]

    def use(side):
        middle = x_ref[...].astype(F32) + total_of(terms, side) + bias_ref[...]
        m_ref[...] = middle
        xhat, _ = unit(middle)
        outs[side][...] = (xhat * gain_ref[...] + shift_ref[...]).astype(BF)

    in_half(count, use)


def output_kernel(count, *refs):
    terms, (m_ref, live_ref, bias_ref, o_ref) = refs[:6], refs[6:]

    def use(side):
        o_ref[...] = (live_ref[:, 0:1] * (m_ref[...] + total_of(terms, side) + bias_ref[...])).astype(BF)

    in_half(count, use)


def middle_back_kernel(count, *refs):
    terms, (m_ref, g_ref, live_ref, gain_ref, b_ref, s_ref), outs = refs[:6], refs[6:12], refs[12:]

    def use(side):
        tangent = total_of(terms, side)
        xhat, factor = unit(m_ref[...])
        upstream = live_ref[:, 0:1] * g_ref[...].astype(F32)
        back = upstream + unit_back(tangent, gain_ref[...], xhat, factor)
        b_ref[...] = back
        outs[side][...] = back.astype(BF)
        add_sums(s_ref, [tangent * xhat, tangent, back, upstream])

    in_half(count, use)


def input_back_kernel(count, *refs):
    terms, (x_ref, b_ref, gain_ref, o_ref, s_ref) = refs[:6], refs[6:]

    def use(side):
        tangent = total_of(terms, side)
        xhat, factor = unit(x_ref[...].astype(F32))
        o_ref[...] = (b_ref[...] + unit_back(tangent, gain_ref[...], xhat, factor)).astype(BF)
        add_sums(s_ref, [tangent * xhat, tangent])

    in_half(count, use)


def over_rows(kernel, terms, rows, vectors, wholes=(), pieces=0, sums=False):
    m = rows[0].shape[0]
    d = rows[0].shape[1]
    half = jax.ShapeDtypeStruct((m // 2, d), BF)
    upper, lower = halves(half)
    specs = [upper] * 3 + [lower] * 3 if terms else []
    specs += [whole(r) for r in rows] + [vector(v) for v in vectors]
    outs = [jax.ShapeDtypeStruct((m, d), t) for t in wholes]
    out_specs = [whole(o) for o in outs]
    if sums:
        outs.append(jax.ShapeDtypeStruct((8, d), F32))
        out_specs.append(vector(outs[-1]))
    outs += [half] * pieces
    out_specs += [upper, lower][:pieces]
    return pl.pallas_call(
        functools.partial(kernel, m // 2 // TILE),
        grid=(m // TILE,),
        in_specs=specs,
        out_specs=out_specs,
        out_shape=outs,
        compiler_params=params(),
        cost_estimate=cost(20 * m * d, 16 * m * d),
        name=kernel.__name__.replace("_kernel", ""),
    )(*terms, *rows, *vectors)


def assemble_kernel(own_ref, *refs):
    pieces, o_ref, sems = refs[:8], refs[8], refs[9]
    rows = pieces[0].shape[0]
    for side in range(2):

        @pl.when(own_ref[0] == 1 - side)
        def _():
            copies = [
                pltpu.make_async_copy(pieces[4 * side + k], o_ref.at[pl.ds(k * rows, rows), :], sems.at[k])
                for k in range(4)
            ]
            for c in copies:
                c.start()
            for c in copies:
                c.wait()


def assemble(own, mine, theirs):
    rows, d = mine[0].shape
    anywhere = pl.BlockSpec(memory_space=pl.ANY)
    return pl.pallas_call(
        assemble_kernel,
        in_specs=[pl.BlockSpec(memory_space=pltpu.SMEM)] + [anywhere] * 8,
        out_specs=pl.BlockSpec(memory_space=pltpu.VMEM),
        out_shape=jax.ShapeDtypeStruct((4 * rows, d), BF),
        scratch_shapes=[pltpu.SemaphoreType.DMA((4,))],
        compiler_params=params(16),
        cost_estimate=cost(0, 16 * rows * d),
        name="assemble",
    )(own, *mine, *theirs)


def place_kernel(plane_ref, *refs):
    for k in range(4):

        @pl.when(pl.program_id(0) == k)
        def _():
            start = 0
            for o_ref in refs[4:]:
                if len(o_ref.shape) == 3:
                    width = o_ref.shape[2]
                    for j in range(o_ref.shape[0]):
                        o_ref[j] = refs[k][:, start : start + width].astype(o_ref.dtype)
                        start += width
                else:
                    width = o_ref.shape[1]
                    o_ref[...] = refs[k][:, start : start + width].astype(o_ref.dtype)
                    start += width


def place(plane, pieces, axis, dtype, split=(1,)):
    m, n = pieces[0].shape
    unit_width = n // sum(split)
    outs, specs = [], []
    for count in split:
        if axis == 0:
            outs.append(jax.ShapeDtypeStruct((4 * m, n), dtype))
            specs.append(pl.BlockSpec((m, n), lambda k, p: (p[0] ^ k, 0)))
        elif count == 1:
            outs.append(jax.ShapeDtypeStruct((m, 4 * unit_width), dtype))
            specs.append(pl.BlockSpec((m, unit_width), lambda k, p: (0, p[0] ^ k)))
        else:
            outs.append(jax.ShapeDtypeStruct((count, m, 4 * unit_width), dtype))
            specs.append(pl.BlockSpec((count, m, unit_width), lambda k, p: (0, 0, p[0] ^ k)))
    return pl.pallas_call(
        place_kernel,
        grid_spec=pltpu.PrefetchScalarGridSpec(
            num_scalar_prefetch=1,
            grid=(4,),
            in_specs=[pl.BlockSpec((m, n), lambda k, p: (0, 0))] * 4,
            out_specs=specs,
        ),
        out_shape=outs,
        compiler_params=params(),
        cost_estimate=cost(0, 16 * m * n),
        name="place",
    )(plane, *pieces)


def part_kernel(plane_ref, v_ref, *outs):
    for k in range(4):

        @pl.when(pl.program_id(0) == k)
        def _():
            outs[k][...] = v_ref[...]


def part_rows(plane, v):
    m, n = v.shape[0] // 4, v.shape[1]
    return pl.pallas_call(
        part_kernel,
        grid_spec=pltpu.PrefetchScalarGridSpec(
            num_scalar_prefetch=1,
            grid=(4,),
            in_specs=[pl.BlockSpec((m, n), lambda k, p: (p[0] ^ k, 0))],
            out_specs=[pl.BlockSpec((m, n), lambda k, p: (0, 0))] * 4,
        ),
        out_shape=[jax.ShapeDtypeStruct((m, n), v.dtype)] * 4,
        compiler_params=params(),
        cost_estimate=cost(0, 16 * m * n),
        name="part_rows",
    )(plane, v)


def after(value, *others):
    return lax.optimization_barrier((value, *others))[0]


def body(
    depth,
    inputs,
    gamma_first,
    beta_first,
    heads_weight,
    output_weight,
    output_bias,
    gamma_second,
    beta_second,
    expand_weight,
    expand_bias,
    reduce_weight,
    reduce_bias,
    group_sizes,
    prefix_lengths,
    solution_lengths,
    cotangent,
):
    block, model = inputs.shape
    zi, yi, xi, ci = (lax.axis_index(a) for a in ALL)
    plane = yi * 2 + xi
    own = xi == ci
    send = lambda v, route: lax.ppermute(v, ALL, pairs_of(depth, route))
    wide = lambda v: v.astype(F32)

    def near_of(v):
        return send(v, lambda y, x, c: (y, x, c) if c == x else (y, 1 - x, 1 - c))

    def far_of(v):
        return send(v, lambda y, x, c: (1 - y, x, c) if c == x else (1 - y, 1 - x, 1 - c))

    flip_y = lambda y, x, c: (1 - y, x, c)
    owners_y = lambda y, x, c: (1 - y, x, c) if c == x else None
    others_y = lambda y, x, c: (1 - y, x, c) if c != x else None
    owners_x = lambda y, x, c: (y, 1 - x, c) if c == x else None
    others_x = lambda y, x, c: (y, 1 - x, c) if c != x else None

    def spread_out(top, low):
        y_low, x_top = send(low, owners_y), send(top, owners_x)
        return top, low, send(top, owners_y), y_low, x_top, send(low, owners_x)

    def spread_on(moved):
        top, low, y_top, y_low, x_top, x_low = moved
        far_low, far_top = send(y_low, owners_x), send(x_top, others_y)
        return assemble(own_flag, (top, low, y_top, y_low), (x_top, x_low, far_top, far_low))

    def collect(far, near):
        far_top, far_low = far
        near_top, near_low = near
        by_y, to_far = send(far_top, flip_y), send(far_low, others_x)
        by_x = send(near_low, others_x)
        from_y = send((wide(far_low) + wide(to_far)).astype(BF), owners_y)
        from_x = send((wide(near_top) + wide(by_y)).astype(BF), others_x)
        return (near_top, from_x, by_y, near_low, by_x, from_y), (to_far, by_y)

    def from_owner(v):
        return jnp.where(own, v, send(v, lambda y, x, c: (y, x, 1 - c) if c == x else None))

    def shuffle(pieces, *first):
        routes = (
            lambda y, x, c: (y, 1 - x, c),
            lambda y, x, c: (1 - y, x, c),
            lambda y, x, c: (1 - y, 1 - x, c),
        )
        pieces = lax.optimization_barrier((*pieces, *first))[:4]
        return [pieces[0]] + [send(pieces[k], routes[k - 1]) for k in (1, 2, 3)]

    def columns(v, k):
        width = v.shape[-1] // 4
        return lax.dynamic_slice_in_dim(v, (plane ^ k) * width, width, axis=-1)

    def gather(pieces):
        full = lax.all_gather(place(plane_flag, pieces, 0, BF)[0], ("c", "z"), axis=0, tiled=True)
        return full.reshape(2, full.shape[0] // 2, full.shape[1])

    def scatter(terms, axes):
        return lax.psum_scatter(terms.reshape(-1, terms.shape[-1]), axes, scatter_dimension=0, tiled=True)

    pick = ci.astype(jnp.int32).reshape(1)
    plane_flag = plane.astype(jnp.int32).reshape(1)
    own_flag = own.astype(jnp.int32).reshape(1)
    row = lambda v: wide(v).reshape(1, -1)
    shard, _, local = heads_weight.shape
    part = local // 4
    inner = expand_weight.shape[1] // 4

    def attention_columns(k):
        heads = columns(heads_weight, k)
        return jnp.concatenate([heads[:, 0], heads[:, 1], heads[:, 2], columns(output_weight, k)], axis=1)

    heads_got = shuffle([attention_columns(k) for k in range(4)])
    heads_all = gather(heads_got)

    info, live = bounds_of(group_sizes, prefix_lengths, solution_lengths, block)
    info = jnp.pad(info, ((0, 0), (0, 5)))
    live_mask = wide(live)[:, None]
    live_wide = jnp.broadcast_to(live_mask, (block, 128))
    info_two = jnp.concatenate([near_of(info), far_of(info)], axis=0)
    first_own = over_rows(first_kernel, (), (inputs,), (row(gamma_first), row(beta_first)), pieces=2)
    first_own = lax.optimization_barrier((*first_own, *heads_got))[:2]
    first = spread_on(spread_out(*first_own))

    expand_got = shuffle([columns(expand_weight, k) for k in range(4)], first)
    expand_all = gather(expand_got)
    reduce_got = shuffle([columns(reduce_weight, k) for k in range(4)], *expand_got)
    reduce_all = gather(reduce_got)
    bias_mine = lax.dynamic_slice_in_dim(expand_bias, plane * inner, inner).reshape(1, 1, inner)
    bias_other = send(bias_mine, lambda y, x, c: (y, x, 1 - c))
    bias = wide(
        jnp.where(ci == 0, jnp.concatenate([bias_mine, bias_other]), jnp.concatenate([bias_other, bias_mine]))
    )
    upstream_own = (live_mask * wide(cotangent)).astype(BF)
    upstream_own = (upstream_own[: block // 2], upstream_own[block // 2 :])
    upstream_moved = spread_out(*lax.optimization_barrier((*upstream_own, *reduce_got))[:2])

    both = jnp.arange(2, dtype=jnp.int32)
    projected = project(first, heads_all, 3 * part, 0)
    mixed, log_sums = attend(info_two, projected, block)
    far = contract(mixed, heads_all, 3, 1)
    mixed_near, *upstream_moved = lax.optimization_barrier((mixed, *upstream_moved, *far))[:7]
    attended, _ = collect(far, contract(mixed_near, heads_all, 3, 0))
    middle, *second_own = over_rows(
        middle_kernel, attended, (inputs,), (row(output_bias), row(gamma_second), row(beta_second)), (F32,), pieces=2
    )
    second = spread_on(spread_out(*second_own))
    upstream_low = spread_on(lax.optimization_barrier((*upstream_moved, second))[:6])
    activated, slope = expand(second, expand_all, bias)
    reduce_terms = outer(both, [(upstream_low, activated)], depth)
    reduce_part = scatter(reduce_terms, ("z", "c"))

    slope, upstream_last, _ = lax.optimization_barrier((slope, upstream_low, reduce_terms))
    sum_low, expand_bias_gradient = expand_back(upstream_last, reduce_all, slope)
    expand_bias_gradient = expand_bias_gradient.reshape(2, inner)
    far, near = contract(sum_low, expand_all, 0, 1), contract(sum_low, expand_all, 0, 0)
    second_back, moved = collect(far, near)
    expand_terms = outer(both, [(second, after(sum_low, *moved, *near))], depth)
    expand_part = scatter(expand_terms, ("z", "c"))
    second_back = lax.optimization_barrier((*second_back, expand_terms))[:6]
    middle_back, sums_second, *middle_own = over_rows(
        middle_back_kernel,
        second_back,
        (middle, cotangent, live_wide),
        (row(gamma_second),),
        (F32,),
        pieces=2,
        sums=True,
    )
    active_last = after(activated, *middle_own)
    far, near = contract(active_last, reduce_all, 0, 1), contract(active_last, reduce_all, 0, 0)
    branch, moved = collect(far, near)
    middle_low = spread_on(spread_out(*middle_own))

    mixed_back = project(after(middle_low, reduce_part, *far, *near), heads_all, part, 3)
    projected_back = attend_back(info_two, projected, after(mixed_back, moved[0]), log_sums, block)
    projected_back = after(projected_back, moved[1])
    heads_terms = outer(both, [(first, projected_back), (middle_low, mixed)], depth)
    heads_part = scatter(after(heads_terms, expand_part), ("z", "c"))
    far = contract(after(projected_back, heads_terms), heads_all, 0, 1)
    reduce_got = shuffle(part_rows(plane_flag, reduce_part))
    projected_near, *rest = lax.optimization_barrier((projected_back, *branch, *reduce_got, *far))
    branch, reduce_got = rest[:6], rest[6:10]
    near = contract(projected_near, heads_all, 0, 0)
    first_back, _ = collect(far, near)
    (outputs,) = over_rows(output_kernel, branch, (middle, live_wide), (row(reduce_bias),), (BF,))
    outputs = from_owner(outputs)
    (reduce_gradient,) = place(plane_flag, reduce_got, 1, F32)
    *first_back, outputs, reduce_gradient = lax.optimization_barrier((*first_back, outputs, reduce_gradient))
    input_gradient, sums_first = over_rows(
        input_back_kernel, first_back, (inputs, middle_back), (row(gamma_first),), (BF,), sums=True
    )
    input_gradient = from_owner(input_gradient)

    expand_got = shuffle(part_rows(plane_flag, expand_part), *first_back)
    (expand_gradient,) = place(plane_flag, expand_got, 1, F32)
    gamma_first_gradient, beta_first_gradient = sums_first[0], sums_first[1]
    gamma_second_gradient, beta_second_gradient = sums_second[0], sums_second[1]
    output_bias_gradient, reduce_bias_gradient = sums_second[2], sums_second[3]

    vectors = jnp.stack(
        [
            gamma_first_gradient,
            beta_first_gradient,
            output_bias_gradient,
            gamma_second_gradient,
            beta_second_gradient,
            reduce_bias_gradient,
        ]
    )
    vectors = jnp.where(own, vectors, 0.0)
    placed = lax.dynamic_update_slice(jnp.zeros((2, 4 * inner), F32), expand_bias_gradient, (0, plane * inner))
    sums = jnp.concatenate([vectors.reshape(-1), placed.reshape(-1)]).reshape(-1, 128)
    for route in (
        lambda y, x, c: (y, x, 1 - c),
        lambda y, x, c: (y, 1 - x, c),
        lambda y, x, c: (1 - y, x, c),
    ):
        sums = sums + send(sums, route)
    sums, expand_gradient = lax.optimization_barrier((sums, expand_gradient))
    step = 1
    while step < depth:
        sums = sums + lax.ppermute(sums, "z", [(i, i ^ step) for i in range(depth)])
        step *= 2
    flat = sums.reshape(-1)
    index = zi * 4 + plane
    vectors = lax.dynamic_slice_in_dim(flat[: 6 * model].reshape(6, model), index * shard, shard, axis=1)
    placed = flat[6 * model :].reshape(2, 4 * inner)
    count = 4 * inner // (4 * depth)
    expand_bias_gradient = lax.dynamic_slice(placed, (ci, index * count), (1, count))
    heads_part, reduce_gradient, expand_gradient, outputs, input_gradient, vectors, expand_bias_gradient = (
        lax.optimization_barrier(
            (heads_part, reduce_gradient, expand_gradient, outputs, input_gradient, vectors, expand_bias_gradient)
        )
    )
    heads_got = shuffle(part_rows(plane_flag, heads_part))
    heads_gradient, output_gradient = place(plane_flag, heads_got, 1, F32, (3, 1))
    heads_gradient = heads_gradient.transpose(1, 0, 2)
    return (
        outputs,
        input_gradient,
        vectors[0],
        vectors[1],
        heads_gradient,
        output_gradient,
        vectors[2],
        vectors[3],
        vectors[4],
        expand_gradient,
        expand_bias_gradient,
        reduce_gradient,
        vectors[5],
    )


def solution(mesh):
    depth = mesh.shape["dp"] // 4
    fine = Mesh(mesh.devices.reshape(depth, 2, 2, 2), ALL)
    dp = ("z", "y", "x")
    placed = (
        P(dp, None),
        P(),
        P(),
        P(dp, None, "c"),
        P(dp, "c"),
        P(),
        P(),
        P(),
        P(dp, "c"),
        P("c"),
        P(dp, "c"),
        P(),
        P(dp),
        P(dp),
        P(dp, None),
        P(dp, None),
    )
    return jax.shard_map(
        functools.partial(body, depth),
        mesh=fine,
        in_specs=placed,
        out_specs=(
            P(dp, None),
            P(dp, None),
            P(dp),
            P(dp),
            P(dp, None, "c"),
            P(dp, "c"),
            P(dp),
            P(dp),
            P(dp),
            P(dp, "c"),
            P("c", dp),
            P(dp, "c"),
            P(dp),
        ),
        check_vma=False,
    )
```

time: 908 us -> 648 us (0.71)
  waiting for transfers between devices: 450 us -> 250 us
  Pallas kernels: 26.4 us -> 206 us
  matrix products: 147 us -> 0 us
  other arithmetic: 82.2 us -> 12.8 us
  local copies, waits for them, and re-layouts: 63 us -> 28.7 us
  starting transfers between devices: 114 us -> 125 us
    pallas_call x2 -> x35, Pallas kernels: 26.4 us -> 206 us  [the longest x8 52.8 us: contract(): pl.pallas_call(contract_kernel, grid=(d // tile,), in_specs=[pl.BlockSpec...]
    dot_general x24 -> x0, matrix products: 147 us -> none  [dot(): return lax.dot_general(a, b, dims, preferred_element_type=F32)]
    reduce_scatter x3, waiting for transfers between devices: 116 us -> 0.01 us  [scatter(): lax.psum_scatter(terms.reshape(-1, terms.shape[-1]), axes, scatter_dimens...]
    ppermute x51 -> x70, waiting for transfers between devices: 319 us -> 243 us  [body(): send = lambda v, route: lax.ppermute(v, ALL, pairs_of(depth, route))]
    another operation x5 -> x0, other arithmetic: 27.3 us -> none  [the longest x3 12.2 us: body(): jnp.stack([jnp.concatenate([dot(first, projected_back[k], ROWS).astype(BF...]
    reduce_sum x9 -> x0, other arithmetic: 17.8 us -> none  [the longest x4 8.7 us: normalize(): center = values - jnp.mean(values, axis=-1, keepdims=True)]
    another operation x2 -> x0, local copies, waits for them, and re-layouts: 12.3 us -> none  [the longest x1 12.3 us: body(): jnp.stack([jnp.concatenate([dot(first, projected_back[k], ROWS).astype(BF...]
    ppermute x51 -> x70, starting transfers between devices: 110 us -> 122 us  [body(): send = lambda v, route: lax.ppermute(v, ALL, pairs_of(depth, route))]
  transfers between devices with their start and end apart: 60 -> 78, of which waited for: 31 -> 42; matrix products, arithmetic and copies ran while one was open for 31% -> 3% of each run, Pallas kernels for 3% -> 32%
where the time goes in v2:
time: 648 us; the launch traced here: 638 us
  waiting for transfers between devices  250 us (39%)
  Pallas kernels  206 us (32%)
  starting transfers between devices  125 us (19%)
  local copies, waits for them, and re-layouts  28.7 us (4%)
  between operations  15.9 us (2%)
  other arithmetic  12.8 us (2%)
    ppermute x70, waiting for transfers between devices, body(): send = lambda v, route: lax.ppermute(v, ALL, pairs_of(depth, route))  243 us
    ppermute x70, starting transfers between devices, body(): send = lambda v, route: lax.ppermute(v, ALL, pairs_of(depth, route))  122 us
    pallas_call x8, Pallas kernels, contract(): pl.pallas_call(contract_kernel, grid=(d // tile,), in_specs=[pl.BlockSpec...  52.8 us
    pallas_call x3, Pallas kernels, outer(): pl.pallas_call(functools.partial(outer_kernel, len(pairs), extra is not N...  46.4 us
    pallas_call x5, Pallas kernels, over_rows(): pl.pallas_call(functools.partial(kernel, m // 2 // TILE), grid=(m // TILE...  32 us
    unnamed x97, local copies, waits for them, and re-layouts  21.5 us
    pallas_call x1, Pallas kernels, expand(): pl.pallas_call(expand_kernel, grid=(sides, n // tile), in_specs=[pl.Block...  17.1 us
    pallas_call x2, Pallas kernels, project(): pl.pallas_call(project_kernel, grid=(sides,), in_specs=[pl.BlockSpec((m,...  14 us
  transfers between devices with their start and end apart: 78, of which 42 were waited for; matrix products, arithmetic and copies ran while one was open for 3% of the time, Pallas kernels for 32%

profile of v2, /device:TPU:0, one launch (start us, length us, event | category | flops | bytes accessed | tf_op | source)
XLA Modules:
  0.0 637.9 jit_solution(16404507488276684664)
XLA Ops:
  14.2 5.6 collective-permute-done.refs_1_
  19.8 6.2 collective-permute-done.1.refs_2_
  41.6 4.1 collective-permute-done.5.refs_4_
  55.1 17.9 %collective-permute-done.3.refs_2_ = bf16[256,2048]{1,0:T(8,128)(2,1)} collective-permute-done((bf16[256,2048]{1,0:T(8,128)(2,1)S(1)}, bf16[256,2048]{1,0:T(8,128)(2,1)}, u32[]{:S(2)}, u32[]{:S(2)}) %collective-permute-start.3) | collective-permute-done | bytes 1048608 | tf_op jit(solution)/shard_map/ppermute | solution.py:600
  80.2 5.7 collective-permute-done.11.refs_1_
  86.1 4.0 collective-permute-done.13.refs_3_
  95.4 5.8 collective-permute-done.14.refs_1_
  101.2 4.5 collective-permute-done.15.refs_2_
  116.9 4.7 collective-permute-start.19
  126.4 10.1 %project.2.p_ref = bf16[2,1024,768]{2,1,0:T(8,128)(2,1)S(1)} custom-call(bf16[1024,2048]{1,0:T(8,128)(2,1)} %copy-done.3, bf16[2,2048,1024]{2,1,0:T(8,128)(2,1)} %bitcast.74), custom_call_target="tpu_custom_call" | custom-call | flops 6442450944 | bytes 13631488 | tf_op jit(solution)/shard_map/project/pallas_call | solution.py:188
  138.2 5.5 attend.1
  143.6 4.2 contract.8
  155.7 8.8 %collective-permute-done.24 = bf16[256,2048]{1,0:T(8,128)(2,1)S(1)} collective-permute-done((bf16[256,2048]{1,0:T(8,128)(2,1)S(1)}, bf16[256,2048]{1,0:T(8,128)(2,1)S(1)}, u32[]{:S(2)}, u32[]{:S(2)}) %collective-permute-start.24) | collective-permute-done | bytes 1048608 | tf_op jit(solution)/shard_map/ppermute | solution.py:600
  168.4 6.0 collective-permute-done.21.refs_2_
  176.5 10.0 %collective-permute-done.25.refs_5_ = bf16[256,2048]{1,0:T(8,128)(2,1)S(1)} collective-permute-done((bf16[256,2048]{1,0:T(8,128)(2,1)S(1)}, bf16[256,2048]{1,0:T(8,128)(2,1)S(1)}, u32[]{:S(2)}, u32[]{:S(2)}) %collective-permute-start.25) | collective-permute-done | bytes 1048608 | tf_op jit(solution)/shard_map/ppermute | solution.py:600
  186.5 6.0 collective-permute-done.22.refs_1_
  192.5 6.5 %middle.1 = (f32[512,2048]{1,0:T(8,128)}, bf16[256,2048]{1,0:T(8,128)(2,1)S(1)}, bf16[256,2048]{1,0:T(8,128)(2,1)S(1)}) custom-call(bf16[256,2048]{1,0:T(8,128)(2,1)S(1)} %get-tuple-element.158.refs_0_, bf16[256,2048]{1,0:T(8,128)(2,1)S(1)} %collective-permute-done.22.refs_1_, bf16[256,2048]{1,0:T(8,128)(2,1)S(1)} %collective-permute-done.21.refs_2_, ...), custom_call_target="tpu_custom_call" | custom-call | flops 20971520 | bytes 16777216 | tf_op jit(solution)/shard_map/middle/pallas_call | solution.py:457
  207.7 5.0 collective-permute-done.28.refs_4_
  213.5 4.1 collective-permute-done.27.refs_3_
  220.6 19.1 %collective-permute-done.26.refs_2_ = bf16[256,2048]{1,0:T(8,128)(2,1)S(1)} collective-permute-done((bf16[256,2048]{1,0:T(8,128)(2,1)S(1)}, bf16[256,2048]{1,0:T(8,128)(2,1)S(1)}, u32[]{:S(2)}, u32[]{:S(2)}) %collective-permute-start.26) | collective-permute-done | bytes 1048608 | tf_op jit(solution)/shard_map/ppermute | solution.py:600
  248.4 17.1 %expand.1 = (bf16[2,1024,1024]{2,1,0:T(8,128)(2,1)S(1)}, f32[2,1024,1024]{2,1,0:T(8,128)}) custom-call(bf16[1024,2048]{1,0:T(8,128)(2,1)} %copy-done.4, bf16[2,2048,1024]{2,1,0:T(8,128)(2,1)} %bitcast.94, f32[2,1,1024]{2,1,0:T(1,128)S(1)} %fusion.b_ref), custom_call_target="tpu_custom_call" | custom-call | flops 8589934592 | bytes 25165824 | tf_op jit(solution)/shard_map/expand/pallas_call | solution.py:216
  269.2 15.7 %outer.3 = bf16[4,2,512,1024]{3,2,1,0:T(8,128)(2,1)} custom-call(s32[2]{0:T(128)S(1)} %iota.48.pick_ref, bf16[1024,2048]{1,0:T(8,128)(2,1)S(1)} %assemble.6.refs_0_.a_ref, bf16[2,1024,1024]{2,1,0:T(8,128)(2,1)} %copy-done.24), custom_call_target="tpu_custom_call" | custom-call | flops 8589934592 | bytes 16777216 | tf_op jit(solution)/shard_map/outer/pallas_call | solution.py:320
  285.0 13.5 %expand_back.1 = (bf16[2,1024,1024]{2,1,0:T(8,128)(2,1)S(1)}, f32[2,1,1024]{2,1,0:T(1,128)S(1)}) custom-call(bf16[1024,2048]{1,0:T(8,128)(2,1)} %copy-done.6, bf16[2,2048,1024]{2,1,0:T(8,128)(2,1)} %bitcast.91, f32[2,1024,1024]{2,1,0:T(8,128)} %get-tuple-element.177.d_ref), custom_call_target="tpu_custom_call" | custom-call | flops 8589934592 | bytes 25165824 | tf_op jit(solution)/shard_map/expand_back/pallas_call | solution.py:244
  300.4 7.9 %contract.11 = (bf16[256,2048]{1,0:T(8,128)(2,1)S(1)}, bf16[256,2048]{1,0:T(8,128)(2,1)S(1)}) custom-call(bf16[2,1024,1024]{2,1,0:T(8,128)(2,1)} %copy-done.25, bf16[2,2048,1024]{2,1,0:T(8,128)(2,1)} %bitcast.95), custom_call_target="tpu_custom_call" | custom-call | flops 4294967296 | bytes 12582912 | tf_op jit(solution)/shard_map/contract/pallas_call | solution.py:277
  310.6 8.0 %contract.10 = (bf16[256,2048]{1,0:T(8,128)(2,1)S(1)}, bf16[256,2048]{1,0:T(8,128)(2,1)S(1)}) custom-call(bf16[2,1024,1024]{2,1,0:T(8,128)(2,1)} %copy-done.25, bf16[2,2048,1024]{2,1,0:T(8,128)(2,1)} %bitcast.96), custom_call_target="tpu_custom_call" | custom-call | flops 4294967296 | bytes 12582912 | tf_op jit(solution)/shard_map/contract/pallas_call | solution.py:277
  318.6 15.8 %collective-permute-done.35.refs_2_ = bf16[256,2048]{1,0:T(8,128)(2,1)S(1)} collective-permute-done((bf16[256,2048]{1,0:T(8,128)(2,1)S(1)}, bf16[256,2048]{1,0:T(8,128)(2,1)S(1)}, u32[]{:S(2)}, u32[]{:S(2)}) %collective-permute-start.35) | collective-permute-done | bytes 1048608 | tf_op jit(solution)/shard_map/ppermute | solution.py:600
  334.4 14.8 %outer.4 = bf16[4,2,512,1024]{3,2,1,0:T(8,128)(2,1)} custom-call(s32[2]{0:T(128)S(1)} %iota.49.pick_ref, bf16[1024,2048]{1,0:T(8,128)(2,1)S(1)} %copy-done.5, bf16[2,1024,1024]{2,1,0:T(8,128)(2,1)} %copy-done.25), custom_call_target="tpu_custom_call" | custom-call | flops 8589934592 | bytes 16777216 | tf_op jit(solution)/shard_map/outer/pallas_call | solution.py:320
  356.6 9.5 %collective-permute-done.37.refs_4_ = bf16[256,2048]{1,0:T(8,128)(2,1)S(1)} collective-permute-done((bf16[256,2048]{1,0:T(8,128)(2,1)}, bf16[256,2048]{1,0:T(8,128)(2,1)S(1)}, u32[]{:S(2)}, u32[]{:S(2)}) %collective-permute-start.37) | collective-permute-done | bytes 1048608 | tf_op jit(solution)/shard_map/ppermute | solution.py:600
  369.2 8.2 %collective-permute-done.36.refs_1_ = bf16[256,2048]{1,0:T(8,128)(2,1)S(1)} collective-permute-done((bf16[256,2048]{1,0:T(8,128)(2,1)S(1)}, bf16[256,2048]{1,0:T(8,128)(2,1)S(1)}, u32[]{:S(2)}, u32[]{:S(2)}) %collective-permute-start.36) | collective-permute-done | bytes 1048608 | tf_op jit(solution)/shard_map/ppermute | solution.py:600
  377.5 9.5 %middle_back.1 = (f32[512,2048]{1,0:T(8,128)}, f32[8,2048]{1,0:T(8,128)S(1)}, bf16[256,2048]{1,0:T(8,128)(2,1)S(1)}, bf16[256,2048]{1,0:T(8,128)(2,1)S(1)}) custom-call(bf16[256,2048]{1,0:T(8,128)(2,1)S(1)} %get-tuple-element.184.refs_0_, bf16[256,2048]{1,0:T(8,128)(2,1)S(1)} %collective-permute-done.36.refs_1_, ...), custom_call_target="tpu_custom_call" | custom-call | flops 20971520 | bytes 16777216 | tf_op jit(solution)/shard_map/middle_back/pallas_call | solution.py:457
  395.7 5.0 collective-permute-done.42.refs_4_
  407.4 8.7 %contract.12 = (bf16[256,2048]{1,0:T(8,128)(2,1)}, bf16[256,2048]{1,0:T(8,128)(2,1)}) custom-call(bf16[2,1024,1024]{2,1,0:T(8,128)(2,1)} %copy-done.24, bf16[2,2048,1024]{2,1,0:T(8,128)(2,1)} %bitcast.92), custom_call_target="tpu_custom_call" | custom-call | flops 4294967296 | bytes 12582912 | tf_op jit(solution)/shard_map/contract/pallas_call | solution.py:277
  417.4 8.0 %contract.13 = (bf16[256,2048]{1,0:T(8,128)(2,1)S(1)}, bf16[256,2048]{1,0:T(8,128)(2,1)S(1)}) custom-call(bf16[2,1024,1024]{2,1,0:T(8,128)(2,1)} %copy-done.24, bf16[2,2048,1024]{2,1,0:T(8,128)(2,1)} %bitcast.93), custom_call_target="tpu_custom_call" | custom-call | flops 4294967296 | bytes 12582912 | tf_op jit(solution)/shard_map/contract/pallas_call | solution.py:277
  435.3 3.9 project.3.g_ref
  439.2 9.5 %attend_back.1.refs_1_.a_ref = bf16[2,1024,768]{2,1,0:T(8,128)(2,1)} custom-call(s32[1024,8]{1,0:T(8,128)S(1)} %copy-done.18, bf16[2,1024,768]{2,1,0:T(8,128)(2,1)} %copy-done.26, bf16[2,1024,256]{2,1,0:T(8,128)(2,1)S(1)} %project.3.g_ref, f32[2,1024,256]{2,1,0:T(8,128)S(1)} %copy-done.28), custom_call_target="tpu_custom_call" | custom-call | flops 16106127360 | bytes 25165824 | tf_op jit(solution)/shard_map/attend_back/pallas_call | solution.py:163
  454.2 15.9 %outer.5 = bf16[4,2,512,1024]{3,2,1,0:T(8,128)(2,1)} custom-call(s32[2]{0:T(128)S(1)} %iota.42.pick_ref, bf16[1024,2048]{1,0:T(8,128)(2,1)} %copy-done.3, bf16[2,1024,768]{2,1,0:T(8,128)(2,1)S(1)} %copy-done.21, bf16[1024,2048]{1,0:T(8,128)(2,1)} %copy-done.1, bf16[2,1024,256]{2,1,0:T(8,128)(2,1)S(1)} %get-tuple-element.157.a_ref.refs_3_), custom_call_target="tpu_custom_call" | custom-call | flops 8589934592 | bytes 16777216 | tf_op jit(solution)/shard_map/outer/pallas_call | solution.py:320
  481.4 6.1 contract.14
  495.6 9.3 %collective-permute-done.48.refs_1_ = bf16[256,2048]{1,0:T(8,128)(2,1)S(1)} collective-permute-done((bf16[256,2048]{1,0:T(8,128)(2,1)S(1)}, bf16[256,2048]{1,0:T(8,128)(2,1)S(1)}, u32[]{:S(2)}, u32[]{:S(2)}) %collective-permute-start.48) | collective-permute-done | bytes 1048608 | tf_op jit(solution)/shard_map/ppermute | solution.py:600
  504.9 14.0 %collective-permute-done.51.refs_1_ = bf16[128,1024]{1,0:T(8,128)(2,1)S(1)} collective-permute-done((bf16[128,1024]{1,0:T(8,128)(2,1)S(1)}, bf16[128,1024]{1,0:T(8,128)(2,1)S(1)}, u32[]{:S(2)}, u32[]{:S(2)}) %collective-permute-start.51) | collective-permute-done | bytes 262176 | tf_op jit(solution)/shard_map/ppermute | solution.py:600
  522.8 5.9 output.1
  530.6 6.1 contract.15
  541.9 8.2 %collective-permute-done.54.refs_2_ = bf16[256,2048]{1,0:T(8,128)(2,1)S(1)} collective-permute-done((bf16[256,2048]{1,0:T(8,128)(2,1)S(1)}, bf16[256,2048]{1,0:T(8,128)(2,1)S(1)}, u32[]{:S(2)}, u32[]{:S(2)}) %collective-permute-start.54) | collective-permute-done | bytes 1048608 | tf_op jit(solution)/shard_map/ppermute | solution.py:600
  555.4 6.0 collective-permute-done.58.refs_5_
  561.4 7.5 %collective-permute-done.55.refs_1_ = bf16[256,2048]{1,0:T(8,128)(2,1)S(1)} collective-permute-done((bf16[256,2048]{1,0:T(8,128)(2,1)S(1)}, bf16[256,2048]{1,0:T(8,128)(2,1)S(1)}, u32[]{:S(2)}, u32[]{:S(2)}) %collective-permute-start.55) | collective-permute-done | bytes 1048608 | tf_op jit(solution)/shard_map/ppermute | solution.py:600
  568.9 7.5 %input_back.1 = (bf16[512,2048]{1,0:T(8,128)(2,1)}, f32[8,2048]{1,0:T(8,128)S(1)}) custom-call(bf16[256,2048]{1,0:T(8,128)(2,1)S(1)} %get-tuple-element.224.refs_0_, bf16[256,2048]{1,0:T(8,128)(2,1)S(1)} %collective-permute-done.55.refs_1_, bf16[256,2048]{1,0:T(8,128)(2,1)S(1)} %collective-permute-done.54.refs_2_, ...), custom_call_target="tpu_custom_call" | custom-call | flops 20971520 | bytes 16777216 | tf_op jit(solution)/shard_map/input_back/pallas_call | solution.py:457
  589.0 10.7 %collective-permute-done.62 = f32[160,128]{1,0:T(8,128)S(1)} collective-permute-done((f32[160,128]{1,0:T(8,128)S(1)}, f32[160,128]{1,0:T(8,128)S(1)}, u32[]{:S(2)}, u32[]{:S(2)}) %collective-permute-start.62) | collective-permute-done | bytes 81952 | tf_op jit(solution)/shard_map/ppermute | solution.py:600
  620.1 4.3 collective-permute-done.69.refs_1_
  624.4 4.4 collective-permute-done.70.refs_2_
  (315 shorter events, 217.3 us)
Async XLA Ops:
  7.2 119.3 %all-gather.4.cloned.1.call-start = ((), (), s32[]{:S(2)}) async-start(), calls=%async_computation.3 | async-start | bytes 9437184 | tf_op jit(solution)/shard_map/all_gather | solution.py:650
  27.6 220.8 %all-gather.6.cloned.1.call-start = ((), (), s32[]{:S(2)}) async-start(), calls=%async_computation.4 | async-start | bytes 9437184 | tf_op jit(solution)/shard_map/all_gather | solution.py:650
  33.4 17.8 %collective-permute-start.4 = (bf16[256,2048]{1,0:T(8,128)(2,1)}, bf16[256,2048]{1,0:T(8,128)(2,1)S(1)}, u32[]{:S(2)}, u32[]{:S(2)}) collective-permute-start(bf16[256,2048]{1,0:T(8,128)(2,1)} %get-tuple-element.143.refs_1_), channel_id=1, source_target_pairs={{0,4},{3,7},{4,0},{7,3},{8,12},{11,15},{12,8},{15,11},{16,20},{19,... | collective-permute-start | bytes 3145736 | tf_op jit(solution)/shard_map/ppermute | solution.py:600
  36.2 36.7 %collective-permute-start.3 = (bf16[256,2048]{1,0:T(8,128)(2,1)S(1)}, bf16[256,2048]{1,0:T(8,128)(2,1)}, u32[]{:S(2)}, u32[]{:S(2)}) collective-permute-start(bf16[256,2048]{1,0:T(8,128)(2,1)S(1)} %get-tuple-element.142.refs_0_), channel_id=1, source_target_pairs={{0,4},{3,7},{4,0},{7,3},{8,12},{11,15},{12,8},{15,11},{16,20},{19,... | collective-permute-start | bytes 3145736 | tf_op jit(solution)/shard_map/ppermute | solution.py:600
  39.3 33.6 %collective-permute-start.6 = (bf16[256,2048]{1,0:T(8,128)(2,1)}, bf16[256,2048]{1,0:T(8,128)(2,1)}, u32[]{:S(2)}, u32[]{:S(2)}) collective-permute-start(bf16[256,2048]{1,0:T(8,128)(2,1)} %get-tuple-element.143.refs_1_), channel_id=1, source_target_pairs={{0,2},{3,1},{4,6},{7,5},{8,10},{11,9},{12,14},{15,13},{16,18},{19,... | collective-permute-start | bytes 3145736 | tf_op jit(solution)/shard_map/ppermute | solution.py:600
  45.7 27.3 %collective-permute-start.7 = (bf16[256,2048]{1,0:T(8,128)(2,1)S(1)}, bf16[256,2048]{1,0:T(8,128)(2,1)}, u32[]{:S(2)}, u32[]{:S(2)}) collective-permute-start(bf16[256,2048]{1,0:T(8,128)(2,1)S(1)} %collective-permute-done.5.refs_4_), channel_id=1, source_target_pairs={{1,5},{2,6},{5,1},{6,2},{9,13},{10,14},{13,9},{14,10},{17,21},{18,... | collective-permute-start | bytes 3145736 | tf_op jit(solution)/shard_map/ppermute | solution.py:600
  51.2 21.7 %collective-permute-start.8 = (bf16[256,2048]{1,0:T(8,128)(2,1)S(1)}, bf16[256,2048]{1,0:T(8,128)(2,1)}, u32[]{:S(2)}, u32[]{:S(2)}) collective-permute-start(bf16[256,2048]{1,0:T(8,128)(2,1)S(1)} %collective-permute-done.4.refs_3_), channel_id=1, source_target_pairs={{0,2},{3,1},{4,6},{7,5},{8,10},{11,9},{12,14},{15,13},{16,18},{19,... | collective-permute-start | bytes 3145736 | tf_op jit(solution)/shard_map/ppermute | solution.py:600
  91.7 193.3 %all-gather.8.cloned.1.call-start = ((), (), s32[]{:S(2)}) async-start(), calls=%async_computation.5 | async-start | bytes 9437184 | tf_op jit(solution)/shard_map/all_gather | solution.py:650
  107.2 325.8 %reduce-scatter.4.cloned.1.call-start = ((), (), s32[]{:S(2)}) async-start(), calls=%async_computation.6 | async-start | bytes 9437184 | tf_op jit(solution)/shard_map/reduce_scatter | solution.py:654
  114.4 34.8 %collective-permute-start.17 = (bf16[256,2048]{1,0:T(8,128)(2,1)S(1)}, bf16[256,2048]{1,0:T(8,128)(2,1)}, u32[]{:S(2)}, u32[]{:S(2)}) collective-permute-start(bf16[256,2048]{1,0:T(8,128)(2,1)S(1)} %get-tuple-element.169.refs_0_), channel_id=1, source_target_pairs={{0,4},{3,7},{4,0},{7,3},{8,12},{11,15},{12,8},{15,11},{16,20},{19,... | collective-permute-start | bytes 3145736 | tf_op jit(solution)/shard_map/ppermute | solution.py:600
  116.9 33.7 %collective-permute-start.19 = (bf16[256,2048]{1,0:T(8,128)(2,1)S(1)}, bf16[256,2048]{1,0:T(8,128)(2,1)}, u32[]{:S(2)}, u32[]{:S(2)}) collective-permute-start(bf16[256,2048]{1,0:T(8,128)(2,1)S(1)} %get-tuple-element.169.refs_0_), channel_id=1, source_target_pairs={{0,2},{3,1},{4,6},{7,5},{8,10},{11,9},{12,14},{15,13},{16,18},{19,... | collective-permute-start | bytes 3145736 | tf_op jit(solution)/shard_map/ppermute | solution.py:600
  121.7 29.0 %collective-permute-start.18 = (bf16[256,2048]{1,0:T(8,128)(2,1)S(1)}, bf16[256,2048]{1,0:T(8,128)(2,1)}, u32[]{:S(2)}, u32[]{:S(2)}) collective-permute-start(bf16[256,2048]{1,0:T(8,128)(2,1)S(1)} %get-tuple-element.170.refs_1_), channel_id=1, source_target_pairs={{0,4},{3,7},{4,0},{7,3},{8,12},{11,15},{12,8},{15,11},{16,20},{19,... | collective-permute-start | bytes 3145736 | tf_op jit(solution)/shard_map/ppermute | solution.py:600
  124.1 26.5 %collective-permute-start.20 = (bf16[256,2048]{1,0:T(8,128)(2,1)S(1)}, bf16[256,2048]{1,0:T(8,128)(2,1)}, u32[]{:S(2)}, u32[]{:S(2)}) collective-permute-start(bf16[256,2048]{1,0:T(8,128)(2,1)S(1)} %get-tuple-element.170.refs_1_), channel_id=1, source_target_pairs={{0,2},{3,1},{4,6},{7,5},{8,10},{11,9},{12,14},{15,13},{16,18},{19,... | collective-permute-start | bytes 3145736 | tf_op jit(solution)/shard_map/ppermute | solution.py:600
  149.1 25.4 %collective-permute-start.21 = (bf16[256,2048]{1,0:T(8,128)(2,1)S(1)}, bf16[256,2048]{1,0:T(8,128)(2,1)S(1)}, u32[]{:S(2)}, u32[]{:S(2)}) collective-permute-start(bf16[256,2048]{1,0:T(8,128)(2,1)S(1)} %get-tuple-element.155), channel_id=1, source_target_pairs={{0,4},{1,5},{2,6},{3,7},{4,0},{5,1},{6,2},{7,3},{8,12},{9,13},{10,... | collective-permute-start | bytes 3145736 | tf_op jit(solution)/shard_map/ppermute | solution.py:600
  154.4 22.0 %collective-permute-start.23 = (bf16[256,2048]{1,0:T(8,128)(2,1)S(1)}, bf16[256,2048]{1,0:T(8,128)(2,1)S(1)}, u32[]{:S(2)}, u32[]{:S(2)}) collective-permute-start(bf16[256,2048]{1,0:T(8,128)(2,1)S(1)} %get-tuple-element.159.refs_3_), channel_id=1, source_target_pairs={{1,3},{2,0},{5,7},{6,4},{9,11},{10,8},{13,15},{14,12},{17,19},{18,... | collective-permute-start | bytes 3145736 | tf_op jit(solution)/shard_map/ppermute | solution.py:600
  164.9 21.5 %collective-permute-start.25 = (bf16[256,2048]{1,0:T(8,128)(2,1)S(1)}, bf16[256,2048]{1,0:T(8,128)(2,1)S(1)}, u32[]{:S(2)}, u32[]{:S(2)}) collective-permute-start(bf16[256,2048]{1,0:T(8,128)(2,1)S(1)} %add_convert_fusion.6), channel_id=1, source_target_pairs={{0,4},{3,7},{4,0},{7,3},{8,12},{11,15},{12,8},{15,11},{16,20},{19,... | collective-permute-start | bytes 3145736 | tf_op jit(solution)/shard_map/ppermute | solution.py:600
  174.9 17.6 %collective-permute-start.22 = (bf16[256,2048]{1,0:T(8,128)(2,1)S(1)}, bf16[256,2048]{1,0:T(8,128)(2,1)S(1)}, u32[]{:S(2)}, u32[]{:S(2)}) collective-permute-start(bf16[256,2048]{1,0:T(8,128)(2,1)S(1)} %add_convert_fusion.7), channel_id=1, source_target_pairs={{1,3},{2,0},{5,7},{6,4},{9,11},{10,8},{13,15},{14,12},{17,19},{18,... | collective-permute-start | bytes 3145736 | tf_op jit(solution)/shard_map/ppermute | solution.py:600
  200.5 17.0 %collective-permute-start.27 = (bf16[256,2048]{1,0:T(8,128)(2,1)S(1)}, bf16[256,2048]{1,0:T(8,128)(2,1)S(1)}, u32[]{:S(2)}, u32[]{:S(2)}) collective-permute-start(bf16[256,2048]{1,0:T(8,128)(2,1)S(1)} %get-tuple-element.161.refs_1_), channel_id=1, source_target_pairs={{0,4},{3,7},{4,0},{7,3},{8,12},{11,15},{12,8},{15,11},{16,20},{19,... | collective-permute-start | bytes 3145736 | tf_op jit(solution)/shard_map/ppermute | solution.py:600
  203.9 35.8 %collective-permute-start.26 = (bf16[256,2048]{1,0:T(8,128)(2,1)S(1)}, bf16[256,2048]{1,0:T(8,128)(2,1)S(1)}, u32[]{:S(2)}, u32[]{:S(2)}) collective-permute-start(bf16[256,2048]{1,0:T(8,128)(2,1)S(1)} %get-tuple-element.160.refs_0_), channel_id=1, source_target_pairs={{0,4},{3,7},{4,0},{7,3},{8,12},{11,15},{12,8},{15,11},{16,20},{19,... | collective-permute-start | bytes 3145736 | tf_op jit(solution)/shard_map/ppermute | solution.py:600
  206.4 33.3 %collective-permute-start.29 = (bf16[256,2048]{1,0:T(8,128)(2,1)S(1)}, bf16[256,2048]{1,0:T(8,128)(2,1)S(1)}, u32[]{:S(2)}, u32[]{:S(2)}) collective-permute-start(bf16[256,2048]{1,0:T(8,128)(2,1)S(1)} %get-tuple-element.161.refs_1_), channel_id=1, source_target_pairs={{0,2},{3,1},{4,6},{7,5},{8,10},{11,9},{12,14},{15,13},{16,18},{19,... | collective-permute-start | bytes 3145736 | tf_op jit(solution)/shard_map/ppermute | solution.py:600
  212.7 27.0 %collective-permute-start.30 = (bf16[256,2048]{1,0:T(8,128)(2,1)S(1)}, bf16[256,2048]{1,0:T(8,128)(2,1)S(1)}, u32[]{:S(2)}, u32[]{:S(2)}) collective-permute-start(bf16[256,2048]{1,0:T(8,128)(2,1)S(1)} %collective-permute-done.28.refs_4_), channel_id=1, source_target_pairs={{1,5},{2,6},{5,1},{6,2},{9,13},{10,14},{13,9},{14,10},{17,21},{18,... | collective-permute-start | bytes 3145736 | tf_op jit(solution)/shard_map/ppermute | solution.py:600
  217.6 22.1 %collective-permute-start.31 = (bf16[256,2048]{1,0:T(8,128)(2,1)S(1)}, bf16[256,2048]{1,0:T(8,128)(2,1)S(1)}, u32[]{:S(2)}, u32[]{:S(2)}) collective-permute-start(bf16[256,2048]{1,0:T(8,128)(2,1)S(1)} %collective-permute-done.27.refs_3_), channel_id=1, source_target_pairs={{0,2},{3,1},{4,6},{7,5},{8,10},{11,9},{12,14},{15,13},{16,18},{19,... | collective-permute-start | bytes 3145736 | tf_op jit(solution)/shard_map/ppermute | solution.py:600
  242.1 25.4 %collective-permute-start.33 = (bf16[256,2048]{1,0:T(8,128)(2,1)}, bf16[256,2048]{1,0:T(8,128)(2,1)}, u32[]{:S(2)}, u32[]{:S(2)}) collective-permute-start(bf16[256,2048]{1,0:T(8,128)(2,1)} %collective-permute-done.19.refs_4_), channel_id=1, source_target_pairs={{1,5},{2,6},{5,1},{6,2},{9,13},{10,14},{13,9},{14,10},{17,21},{18,... | collective-permute-start | bytes 3145736 | tf_op jit(solution)/shard_map/ppermute | solution.py:600
  243.7 23.7 %collective-permute-start.34 = (bf16[256,2048]{1,0:T(8,128)(2,1)}, bf16[256,2048]{1,0:T(8,128)(2,1)}, u32[]{:S(2)}, u32[]{:S(2)}) collective-permute-start(bf16[256,2048]{1,0:T(8,128)(2,1)} %collective-permute-done.18.refs_3_), channel_id=1, source_target_pairs={{0,2},{3,1},{4,6},{7,5},{8,10},{11,9},{12,14},{15,13},{16,18},{19,... | collective-permute-start | bytes 3145736 | tf_op jit(solution)/shard_map/ppermute | solution.py:600
  284.9 185.2 %reduce-scatter.6.cloned.1.call-start = ((), (), s32[]{:S(2)}) async-start(), calls=%async_computation.7 | async-start | bytes 9437184 | tf_op jit(solution)/shard_map/reduce_scatter | solution.py:654
  308.4 26.0 %collective-permute-start.35 = (bf16[256,2048]{1,0:T(8,128)(2,1)S(1)}, bf16[256,2048]{1,0:T(8,128)(2,1)S(1)}, u32[]{:S(2)}, u32[]{:S(2)}) collective-permute-start(bf16[256,2048]{1,0:T(8,128)(2,1)S(1)} %get-tuple-element.180), channel_id=1, source_target_pairs={{0,4},{1,5},{2,6},{3,7},{4,0},{5,1},{6,2},{7,3},{8,12},{9,13},{10,... | collective-permute-start | bytes 3145736 | tf_op jit(solution)/shard_map/ppermute | solution.py:600
  309.0 25.4 %collective-permute-start.38 = (bf16[256,2048]{1,0:T(8,128)(2,1)S(1)}, bf16[256,2048]{1,0:T(8,128)(2,1)S(1)}, u32[]{:S(2)}, u32[]{:S(2)}) collective-permute-start(bf16[256,2048]{1,0:T(8,128)(2,1)S(1)} %get-tuple-element.182), channel_id=1, source_target_pairs={{1,3},{2,0},{5,7},{6,4},{9,11},{10,8},{13,15},{14,12},{17,19},{18,... | collective-permute-start | bytes 3145736 | tf_op jit(solution)/shard_map/ppermute | solution.py:600
  349.2 264.6 %reduce-scatter.8.cloned.1.call-start = ((), (), s32[]{:S(2)}) async-start(), calls=%async_computation.8 | async-start | bytes 9437184 | tf_op jit(solution)/shard_map/reduce_scatter | solution.py:654
  355.3 22.1 %collective-permute-start.36 = (bf16[256,2048]{1,0:T(8,128)(2,1)S(1)}, bf16[256,2048]{1,0:T(8,128)(2,1)S(1)}, u32[]{:S(2)}, u32[]{:S(2)}) collective-permute-start(bf16[256,2048]{1,0:T(8,128)(2,1)S(1)} %add_convert_fusion.5), channel_id=1, source_target_pairs={{1,3},{2,0},{5,7},{6,4},{9,11},{10,8},{13,15},{14,12},{17,19},{18,... | collective-permute-start | bytes 3145736 | tf_op jit(solution)/shard_map/ppermute | solution.py:600
  390.7 36.6 %collective-permute-start.40 = (bf16[256,2048]{1,0:T(8,128)(2,1)S(1)}, bf16[256,2048]{1,0:T(8,128)(2,1)S(1)}, u32[]{:S(2)}, u32[]{:S(2)}) collective-permute-start(bf16[256,2048]{1,0:T(8,128)(2,1)S(1)} %get-tuple-element.191.refs_0_), channel_id=1, source_target_pairs={{0,4},{3,7},{4,0},{7,3},{8,12},{11,15},{12,8},{15,11},{16,20},{19,... | collective-permute-start | bytes 3145736 | tf_op jit(solution)/shard_map/ppermute | solution.py:600
  394.3 33.8 %collective-permute-start.43 = (bf16[256,2048]{1,0:T(8,128)(2,1)S(1)}, bf16[256,2048]{1,0:T(8,128)(2,1)S(1)}, u32[]{:S(2)}, u32[]{:S(2)}) collective-permute-start(bf16[256,2048]{1,0:T(8,128)(2,1)S(1)} %get-tuple-element.192.refs_1_), channel_id=1, source_target_pairs={{0,2},{3,1},{4,6},{7,5},{8,10},{11,9},{12,14},{15,13},{16,18},{19,... | collective-permute-start | bytes 3145736 | tf_op jit(solution)/shard_map/ppermute | solution.py:600
  400.7 27.4 %collective-permute-start.44 = (bf16[256,2048]{1,0:T(8,128)(2,1)S(1)}, bf16[256,2048]{1,0:T(8,128)(2,1)S(1)}, u32[]{:S(2)}, u32[]{:S(2)}) collective-permute-start(bf16[256,2048]{1,0:T(8,128)(2,1)S(1)} %collective-permute-done.42.refs_4_), channel_id=1, source_target_pairs={{1,5},{2,6},{5,1},{6,2},{9,13},{10,14},{13,9},{14,10},{17,21},{18,... | collective-permute-start | bytes 3145736 | tf_op jit(solution)/shard_map/ppermute | solution.py:600
  405.1 23.4 %collective-permute-start.45 = (bf16[256,2048]{1,0:T(8,128)(2,1)S(1)}, bf16[256,2048]{1,0:T(8,128)(2,1)S(1)}, u32[]{:S(2)}, u32[]{:S(2)}) collective-permute-start(bf16[256,2048]{1,0:T(8,128)(2,1)S(1)} %collective-permute-done.41.refs_3_), channel_id=1, source_target_pairs={{0,2},{3,1},{4,6},{7,5},{8,10},{11,9},{12,14},{15,13},{16,18},{19,... | collective-permute-start | bytes 3145736 | tf_op jit(solution)/shard_map/ppermute | solution.py:600
  416.1 23.1 %collective-permute-start.46 = (bf16[256,2048]{1,0:T(8,128)(2,1)}, bf16[256,2048]{1,0:T(8,128)(2,1)}, u32[]{:S(2)}, u32[]{:S(2)}) collective-permute-start(bf16[256,2048]{1,0:T(8,128)(2,1)} %get-tuple-element.195), channel_id=1, source_target_pairs={{1,3},{2,0},{5,7},{6,4},{9,11},{10,8},{13,15},{14,12},{17,19},{18,... | collective-permute-start | bytes 3145736 | tf_op jit(solution)/shard_map/ppermute | solution.py:600
  427.3 25.1 %collective-permute-start.47 = (bf16[256,2048]{1,0:T(8,128)(2,1)}, bf16[256,2048]{1,0:T(8,128)(2,1)S(1)}, u32[]{:S(2)}, u32[]{:S(2)}) collective-permute-start(bf16[256,2048]{1,0:T(8,128)(2,1)} %get-tuple-element.194), channel_id=1, source_target_pairs={{0,4},{1,5},{2,6},{3,7},{4,0},{5,1},{6,2},{7,3},{8,12},{9,13},{10,... | collective-permute-start | bytes 3145736 | tf_op jit(solution)/shard_map/ppermute | solution.py:600
  471.4 20.5 %collective-permute-start.49 = (bf16[256,2048]{1,0:T(8,128)(2,1)S(1)}, bf16[256,2048]{1,0:T(8,128)(2,1)S(1)}, u32[]{:S(2)}, u32[]{:S(2)}) collective-permute-start(bf16[256,2048]{1,0:T(8,128)(2,1)S(1)} %copy-done.15), channel_id=1, source_target_pairs={{1,3},{2,0},{5,7},{6,4},{9,11},{10,8},{13,15},{14,12},{17,19},{18,... | collective-permute-start | bytes 3145736 | tf_op jit(solution)/shard_map/ppermute | solution.py:600
  475.6 20.1 %collective-permute-start.50 = (bf16[256,2048]{1,0:T(8,128)(2,1)}, bf16[256,2048]{1,0:T(8,128)(2,1)}, u32[]{:S(2)}, u32[]{:S(2)}) collective-permute-start(bf16[256,2048]{1,0:T(8,128)(2,1)} %add_convert_fusion.2), channel_id=1, source_target_pairs={{0,4},{3,7},{4,0},{7,3},{8,12},{11,15},{12,8},{15,11},{16,20},{19,... | collective-permute-start | bytes 3145736 | tf_op jit(solution)/shard_map/ppermute | solution.py:600
  479.7 25.2 %collective-permute-start.48 = (bf16[256,2048]{1,0:T(8,128)(2,1)S(1)}, bf16[256,2048]{1,0:T(8,128)(2,1)S(1)}, u32[]{:S(2)}, u32[]{:S(2)}) collective-permute-start(bf16[256,2048]{1,0:T(8,128)(2,1)S(1)} %add_convert_fusion.3), channel_id=1, source_target_pairs={{1,3},{2,0},{5,7},{6,4},{9,11},{10,8},{13,15},{14,12},{17,19},{18,... | collective-permute-start | bytes 3145736 | tf_op jit(solution)/shard_map/ppermute | solution.py:600
  487.5 50.4 %collective-permute-start.57 = (bf16[256,2048]{1,0:T(8,128)(2,1)S(1)}, bf16[256,2048]{1,0:T(8,128)(2,1)S(1)}, u32[]{:S(2)}, u32[]{:S(2)}) collective-permute-start(bf16[256,2048]{1,0:T(8,128)(2,1)S(1)} %get-tuple-element.209), channel_id=1, source_target_pairs={{1,3},{2,0},{5,7},{6,4},{9,11},{10,8},{13,15},{14,12},{17,19},{18,... | collective-permute-start | bytes 3145736 | tf_op jit(solution)/shard_map/ppermute | solution.py:600
  489.1 29.9 %collective-permute-start.51 = (bf16[128,1024]{1,0:T(8,128)(2,1)S(1)}, bf16[128,1024]{1,0:T(8,128)(2,1)S(1)}, u32[]{:S(2)}, u32[]{:S(2)}) collective-permute-start(bf16[128,1024]{1,0:T(8,128)(2,1)S(1)} %get-tuple-element.204), channel_id=1, source_target_pairs={{0,2},{1,3},{2,0},{3,1},{4,6},{5,7},{6,4},{7,5},{8,10},{9,11},{10,... | collective-permute-start | bytes 786440 | tf_op jit(solution)/shard_map/ppermute | solution.py:600
  491.9 27.0 %collective-permute-start.52 = (bf16[128,1024]{1,0:T(8,128)(2,1)S(1)}, bf16[128,1024]{1,0:T(8,128)(2,1)S(1)}, u32[]{:S(2)}, u32[]{:S(2)}) collective-permute-start(bf16[128,1024]{1,0:T(8,128)(2,1)S(1)} %get-tuple-element.205), channel_id=1, source_target_pairs={{0,4},{1,5},{2,6},{3,7},{4,0},{5,1},{6,2},{7,3},{8,12},{9,13},{10,... | collective-permute-start | bytes 786440 | tf_op jit(solution)/shard_map/ppermute | solution.py:600
  495.6 27.1 %collective-permute-start.53 = (bf16[128,1024]{1,0:T(8,128)(2,1)S(1)}, bf16[128,1024]{1,0:T(8,128)(2,1)S(1)}, u32[]{:S(2)}, u32[]{:S(2)}) collective-permute-start(bf16[128,1024]{1,0:T(8,128)(2,1)S(1)} %get-tuple-element.206), channel_id=1, source_target_pairs={{0,6},{1,7},{2,4},{3,5},{4,2},{5,3},{6,0},{7,1},{8,14},{9,15},{10,... | collective-permute-start | bytes 786440 | tf_op jit(solution)/shard_map/ppermute | solution.py:600
  528.7 25.2 %collective-permute-start.59 = (bf16[512,2048]{1,0:T(8,128)(2,1)}, bf16[512,2048]{1,0:T(8,128)(2,1)S(1)}, u32[]{:S(2)}, u32[]{:S(2)}) collective-permute-start(bf16[512,2048]{1,0:T(8,128)(2,1)} %output.1), channel_id=1, source_target_pairs={{0,1},{3,2},{4,5},{7,6},{8,9},{11,10},{12,13},{15,14},{16,17},{19,... | collective-permute-start | bytes 6291464 | tf_op jit(solution)/shard_map/ppermute | solution.py:600
  530.1 20.0 %collective-permute-start.54 = (bf16[256,2048]{1,0:T(8,128)(2,1)S(1)}, bf16[256,2048]{1,0:T(8,128)(2,1)S(1)}, u32[]{:S(2)}, u32[]{:S(2)}) collective-permute-start(bf16[256,2048]{1,0:T(8,128)(2,1)S(1)} %get-tuple-element.208), channel_id=1, source_target_pairs={{0,4},{1,5},{2,6},{3,7},{4,0},{5,1},{6,2},{7,3},{8,12},{9,13},{10,... | collective-permute-start | bytes 3145736 | tf_op jit(solution)/shard_map/ppermute | solution.py:600
  536.7 18.7 %collective-permute-start.56 = (bf16[256,2048]{1,0:T(8,128)(2,1)S(1)}, bf16[256,2048]{1,0:T(8,128)(2,1)S(1)}, u32[]{:S(2)}, u32[]{:S(2)}) collective-permute-start(bf16[256,2048]{1,0:T(8,128)(2,1)S(1)} %get-tuple-element.227.refs_3_), channel_id=1, source_target_pairs={{1,3},{2,0},{5,7},{6,4},{9,11},{10,8},{13,15},{14,12},{17,19},{18,... | collective-permute-start | bytes 3145736 | tf_op jit(solution)/shard_map/ppermute | solution.py:600
  538.4 23.0 %collective-permute-start.58 = (bf16[256,2048]{1,0:T(8,128)(2,1)S(1)}, bf16[256,2048]{1,0:T(8,128)(2,1)S(1)}, u32[]{:S(2)}, u32[]{:S(2)}) collective-permute-start(bf16[256,2048]{1,0:T(8,128)(2,1)S(1)} %add_convert_fusion), channel_id=1, source_target_pairs={{0,4},{3,7},{4,0},{7,3},{8,12},{11,15},{12,8},{15,11},{16,20},{19,... | collective-permute-start | bytes 3145736 | tf_op jit(solution)/shard_map/ppermute | solution.py:600
  550.5 18.3 %collective-permute-start.55 = (bf16[256,2048]{1,0:T(8,128)(2,1)S(1)}, bf16[256,2048]{1,0:T(8,128)(2,1)S(1)}, u32[]{:S(2)}, u32[]{:S(2)}) collective-permute-start(bf16[256,2048]{1,0:T(8,128)(2,1)S(1)} %add_convert_fusion.1), channel_id=1, source_target_pairs={{1,3},{2,0},{5,7},{6,4},{9,11},{10,8},{13,15},{14,12},{17,19},{18,... | collective-permute-start | bytes 3145736 | tf_op jit(solution)/shard_map/ppermute | solution.py:600
  576.3 35.9 %collective-permute-start.66 = (bf16[512,2048]{1,0:T(8,128)(2,1)}, bf16[512,2048]{1,0:T(8,128)(2,1)}, u32[]{:S(2)}, u32[]{:S(2)}) collective-permute-start(bf16[512,2048]{1,0:T(8,128)(2,1)} %get-tuple-element.244), channel_id=1, source_target_pairs={{0,1},{3,2},{4,5},{7,6},{8,9},{11,10},{12,13},{15,14},{16,17},{19,... | collective-permute-start | bytes 6291464 | tf_op jit(solution)/shard_map/ppermute | solution.py:600
  (79 other events, 870.0 us)
Sparse Core Ops, SparseCore 0:
  27.7 82.3 all-gather.3
  112.3 80.5 all-gather.5
  194.5 80.5 all-gather.7
  285.0 91.2 reduce-scatter.3
  378.4 87.9 reduce-scatter.5
  470.3 90.2 reduce-scatter.7

commit v3 on v2

--- a/solution.py
+++ b/solution.py
@@ -139,7 +139,7 @@
 
 
 def cost(flops, moved, exps=0):
-    return pl.CostEstimate(flops=flops, bytes_accessed=moved, transcendentals=exps)
+    return pl.CostEstimate(flops=flops * 4, bytes_accessed=moved * 4, transcendentals=exps)
 
 
 def attend(info, projected, block):
@@ -621,13 +621,14 @@
         far_low, far_top = send(y_low, owners_x), send(x_top, others_y)
         return assemble(own_flag, (top, low, y_top, y_low), (x_top, x_low, far_top, far_low))
 
-    def collect(far, near):
+    def collect(far, near, *work):
         far_top, far_low = far
         near_top, near_low = near
         by_y, to_far = send(far_top, flip_y), send(far_low, others_x)
         by_x = send(near_low, others_x)
-        from_y = send((wide(far_low) + wide(to_far)).astype(BF), owners_y)
-        from_x = send((wide(near_top) + wide(by_y)).astype(BF), others_x)
+        ahead_y, ahead_x, *_ = lax.optimization_barrier((to_far, by_y, *work))
+        from_y = send((wide(far_low) + wide(ahead_y)).astype(BF), owners_y)
+        from_x = send((wide(near_top) + wide(ahead_x)).astype(BF), others_x)
         return (near_top, from_x, by_y, near_low, by_x, from_y), (to_far, by_y)
 
     def from_owner(v):
@@ -688,19 +689,17 @@
     )
     upstream_own = (live_mask * wide(cotangent)).astype(BF)
     upstream_own = (upstream_own[: block // 2], upstream_own[block // 2 :])
-    upstream_moved = spread_out(*lax.optimization_barrier((*upstream_own, *reduce_got))[:2])
 
     both = jnp.arange(2, dtype=jnp.int32)
     projected = project(first, heads_all, 3 * part, 0)
     mixed, log_sums = attend(info_two, projected, block)
     far = contract(mixed, heads_all, 3, 1)
-    mixed_near, *upstream_moved = lax.optimization_barrier((mixed, *upstream_moved, *far))[:7]
-    attended, _ = collect(far, contract(mixed_near, heads_all, 3, 0))
+    attended, _ = collect(far, contract(after(mixed, *far), heads_all, 3, 0))
     middle, *second_own = over_rows(
         middle_kernel, attended, (inputs,), (row(output_bias), row(gamma_second), row(beta_second)), (F32,), pieces=2
     )
     second = spread_on(spread_out(*second_own))
-    upstream_low = spread_on(lax.optimization_barrier((*upstream_moved, second))[:6])
+    upstream_low = spread_on(spread_out(*lax.optimization_barrier((*upstream_own, second))[:2]))
     activated, slope = expand(second, expand_all, bias)
     reduce_terms = outer(both, [(upstream_low, activated)], depth)
     reduce_part = scatter(reduce_terms, ("z", "c"))
@@ -709,8 +708,8 @@
     sum_low, expand_bias_gradient = expand_back(upstream_last, reduce_all, slope)
     expand_bias_gradient = expand_bias_gradient.reshape(2, inner)
     far, near = contract(sum_low, expand_all, 0, 1), contract(sum_low, expand_all, 0, 0)
-    second_back, moved = collect(far, near)
-    expand_terms = outer(both, [(second, after(sum_low, *moved, *near))], depth)
+    expand_terms = outer(both, [(second, after(sum_low, *far, *near))], depth)
+    second_back, _ = collect(far, near, expand_terms)
     expand_part = scatter(expand_terms, ("z", "c"))
     second_back = lax.optimization_barrier((*second_back, expand_terms))[:6]
     middle_back, sums_second, *middle_own = over_rows(
@@ -724,24 +723,21 @@
     )
     active_last = after(activated, *middle_own)
     far, near = contract(active_last, reduce_all, 0, 1), contract(active_last, reduce_all, 0, 0)
-    branch, moved = collect(far, near)
     middle_low = spread_on(spread_out(*middle_own))
+    terms = lax.optimization_barrier((*far, *near, middle_low))
+    branch, moved = collect(terms[:2], terms[2:4])
 
     mixed_back = project(after(middle_low, reduce_part, *far, *near), heads_all, part, 3)
-    projected_back = attend_back(info_two, projected, after(mixed_back, moved[0]), log_sums, block)
-    projected_back = after(projected_back, moved[1])
-    heads_terms = outer(both, [(first, projected_back), (middle_low, mixed)], depth)
+    projected_back = attend_back(info_two, projected, mixed_back, log_sums, block)
+    far = contract(projected_back, heads_all, 0, 1)
+    near = contract(after(projected_back, *far, *moved), heads_all, 0, 0)
+    first_back, ahead = collect(far, near)
+    heads_terms = outer(both, [(first, after(projected_back, *near, *ahead)), (middle_low, mixed)], depth)
     heads_part = scatter(after(heads_terms, expand_part), ("z", "c"))
-    far = contract(after(projected_back, heads_terms), heads_all, 0, 1)
-    reduce_got = shuffle(part_rows(plane_flag, reduce_part))
-    projected_near, *rest = lax.optimization_barrier((projected_back, *branch, *reduce_got, *far))
-    branch, reduce_got = rest[:6], rest[6:10]
-    near = contract(projected_near, heads_all, 0, 0)
-    first_back, _ = collect(far, near)
+    reduce_got = shuffle(part_rows(plane_flag, reduce_part), *far, *near)
     (outputs,) = over_rows(output_kernel, branch, (middle, live_wide), (row(reduce_bias),), (BF,))
     outputs = from_owner(outputs)
     (reduce_gradient,) = place(plane_flag, reduce_got, 1, F32)
-    *first_back, outputs, reduce_gradient = lax.optimization_barrier((*first_back, outputs, reduce_gradient))
     input_gradient, sums_first = over_rows(
         input_back_kernel, first_back, (inputs, middle_back), (row(gamma_first),), (BF,), sums=True
     )
@@ -772,7 +768,6 @@
         lambda y, x, c: (1 - y, x, c),
     ):
         sums = sums + send(sums, route)
-    sums, expand_gradient = lax.optimization_barrier((sums, expand_gradient))
     step = 1
     while step < depth:
         sums = sums + lax.ppermute(sums, "z", [(i, i ^ step) for i in range(depth)])

time: 648 us -> 621 us (0.958)
  waiting for transfers between devices: 250 us -> 218 us
    ppermute x70, waiting for transfers between devices: 243 us -> 214 us  [body(): send = lambda v, route: lax.ppermute(v, ALL, pairs_of(depth, route))]
    unnamed x97 -> x109, local copies, waits for them, and re-layouts: 21.5 us -> 20.4 us
  transfers between devices with their start and end apart: 78 -> 78, of which waited for: 42 -> 37; matrix products, arithmetic and copies ran while one was open for 3% -> 3% of each run, Pallas kernels for 32% -> 33%
where the time goes in v3:
time: 621 us; the launch traced here: 610 us
  waiting for transfers between devices  218 us (35%)
  Pallas kernels  207 us (33%)
  starting transfers between devices  126 us (20%)
  local copies, waits for them, and re-layouts  26.9 us (4%)
  between operations  16 us (3%)
  other arithmetic  15.9 us (3%)
    ppermute x70, waiting for transfers between devices, body(): send = lambda v, route: lax.ppermute(v, ALL, pairs_of(depth, route))  214 us
    ppermute x70, starting transfers between devices, body(): send = lambda v, route: lax.ppermute(v, ALL, pairs_of(depth, route))  124 us
    pallas_call x8, Pallas kernels, contract(): pl.pallas_call(contract_kernel, grid=(d // tile,), in_specs=[pl.BlockSpec...  54.3 us
    pallas_call x3, Pallas kernels, outer(): pl.pallas_call(functools.partial(outer_kernel, len(pairs), extra is not N...  46.3 us
    pallas_call x5, Pallas kernels, over_rows(): pl.pallas_call(functools.partial(kernel, m // 2 // TILE), grid=(m // TILE...  32.1 us
    unnamed x109, local copies, waits for them, and re-layouts  20.4 us
    pallas_call x1, Pallas kernels, expand(): pl.pallas_call(expand_kernel, grid=(sides, n // tile), in_specs=[pl.Block...  17.1 us
    pallas_call x2, Pallas kernels, project(): pl.pallas_call(project_kernel, grid=(sides,), in_specs=[pl.BlockSpec((m,...  13.9 us
  transfers between devices with their start and end apart: 78, of which 37 were waited for; matrix products, arithmetic and copies ran while one was open for 3% of the time, Pallas kernels for 33%

profile of v3, /device:TPU:0, one launch (start us, length us, event | category | flops | bytes accessed | tf_op | source)
XLA Modules:
  0.0 610.0 jit_solution(3990919426581404627)
XLA Ops:
  14.2 5.6 collective-permute-done.refs_1_
  19.8 6.2 %collective-permute-done.1.refs_2_ = bf16[128,1024]{1,0:T(8,128)(2,1)S(1)} collective-permute-done((bf16[128,1024]{1,0:T(8,128)(2,1)S(1)}, bf16[128,1024]{1,0:T(8,128)(2,1)S(1)}, u32[]{:S(2)}, u32[]{:S(2)}) %collective-permute-start.1) | collective-permute-done | bytes 262176 | tf_op jit(solution)/shard_map/ppermute | solution.py:600
  41.6 4.1 collective-permute-done.5.refs_4_
  47.4 3.9 collective-permute-done.4.refs_3_
  55.1 17.8 %collective-permute-done.3.refs_2_ = bf16[256,2048]{1,0:T(8,128)(2,1)} collective-permute-done((bf16[256,2048]{1,0:T(8,128)(2,1)S(1)}, bf16[256,2048]{1,0:T(8,128)(2,1)}, u32[]{:S(2)}, u32[]{:S(2)}) %collective-permute-start.3) | collective-permute-done | bytes 1048608 | tf_op jit(solution)/shard_map/ppermute | solution.py:600
  80.3 5.7 collective-permute-done.22.refs_1_
  86.3 3.9 collective-permute-done.24.refs_3_
  99.9 7.7 %collective-permute-done.10 = s32[512,8]{0,1:T(8,128)S(1)} collective-permute-done((s32[512,8]{0,1:T(8,128)S(1)}, s32[512,8]{0,1:T(8,128)S(1)}, u32[]{:S(2)}, u32[]{:S(2)}) %collective-permute-start.10) | collective-permute-done | bytes 16416 | tf_op jit(solution)/shard_map/ppermute | solution.py:600
  110.1 10.0 %project.2.p_ref = bf16[2,1024,768]{2,1,0:T(8,128)(2,1)S(1)} custom-call(bf16[1024,2048]{1,0:T(8,128)(2,1)} %copy-done.1, bf16[2,2048,1024]{2,1,0:T(8,128)(2,1)} %bitcast.85), custom_call_target="tpu_custom_call" | custom-call | flops 25769803776 | bytes 54525952 | tf_op jit(solution)/shard_map/project/pallas_call | solution.py:188
  121.8 5.5 attend.1
  127.3 4.2 contract.8
  134.4 3.7 contract.9
  139.4 8.8 %collective-permute-done.11 = bf16[256,2048]{1,0:T(8,128)(2,1)S(1)} collective-permute-done((bf16[256,2048]{1,0:T(8,128)(2,1)S(1)}, bf16[256,2048]{1,0:T(8,128)(2,1)S(1)}, u32[]{:S(2)}, u32[]{:S(2)}) %collective-permute-start.11) | collective-permute-done | bytes 1048608 | tf_op jit(solution)/shard_map/ppermute | solution.py:600
  148.2 9.5 %collective-permute-done.12.refs_2_ = bf16[256,2048]{1,0:T(8,128)(2,1)S(1)} collective-permute-done((bf16[256,2048]{1,0:T(8,128)(2,1)S(1)}, bf16[256,2048]{1,0:T(8,128)(2,1)S(1)}, u32[]{:S(2)}, u32[]{:S(2)}) %collective-permute-start.12) | collective-permute-done | bytes 1048608 | tf_op jit(solution)/shard_map/ppermute | solution.py:600
  163.5 11.4 %collective-permute-done.15.refs_5_ = bf16[256,2048]{1,0:T(8,128)(2,1)S(1)} collective-permute-done((bf16[256,2048]{1,0:T(8,128)(2,1)S(1)}, bf16[256,2048]{1,0:T(8,128)(2,1)S(1)}, u32[]{:S(2)}, u32[]{:S(2)}) %collective-permute-start.15) | collective-permute-done | bytes 1048608 | tf_op jit(solution)/shard_map/ppermute | solution.py:600
  174.9 3.9 collective-permute-done.13.refs_1_
  178.8 6.7 %middle.1 = (f32[512,2048]{1,0:T(8,128)}, bf16[256,2048]{1,0:T(8,128)(2,1)S(1)}, bf16[256,2048]{1,0:T(8,128)(2,1)S(1)}) custom-call(bf16[256,2048]{1,0:T(8,128)(2,1)S(1)} %get-tuple-element.130.refs_0_, bf16[256,2048]{1,0:T(8,128)(2,1)S(1)} %collective-permute-done.13.refs_1_, bf16[256,2048]{1,0:T(8,128)(2,1)S(1)} %collective-permute-done.12.refs_2_, ...), custom_call_target="tpu_custom_call" | custom-call | flops 83886080 | bytes 67108864 | tf_op jit(solution)/shard_map/middle/pallas_call | solution.py:457
  190.1 3.7 collective-permute-start.16
  195.1 4.2 collective-permute-done.18.refs_4_
  200.0 4.8 collective-permute-done.17.refs_3_
  206.9 19.3 %collective-permute-done.16.refs_2_ = bf16[256,2048]{1,0:T(8,128)(2,1)S(1)} collective-permute-done((bf16[256,2048]{1,0:T(8,128)(2,1)S(1)}, bf16[256,2048]{1,0:T(8,128)(2,1)S(1)}, u32[]{:S(2)}, u32[]{:S(2)}) %collective-permute-start.16) | collective-permute-done | bytes 1048608 | tf_op jit(solution)/shard_map/ppermute | solution.py:600
  249.9 17.1 %expand.1 = (bf16[2,1024,1024]{2,1,0:T(8,128)(2,1)S(1)}, f32[2,1024,1024]{2,1,0:T(8,128)}) custom-call(bf16[1024,2048]{1,0:T(8,128)(2,1)} %copy-done.2, bf16[2,2048,1024]{2,1,0:T(8,128)(2,1)} %bitcast.91, f32[2,1,1024]{2,1,0:T(1,128)S(1)} %fusion.b_ref), custom_call_target="tpu_custom_call" | custom-call | flops 34359738368 | bytes 100663296 | tf_op jit(solution)/shard_map/expand/pallas_call | solution.py:216
  270.8 15.6 %outer.3 = bf16[4,2,512,1024]{3,2,1,0:T(8,128)(2,1)} custom-call(s32[2]{0:T(128)S(1)} %iota.48.pick_ref, bf16[1024,2048]{1,0:T(8,128)(2,1)S(1)} %assemble.6.refs_0_.a_ref, bf16[2,1024,1024]{2,1,0:T(8,128)(2,1)} %copy-done.29), custom_call_target="tpu_custom_call" | custom-call | flops 34359738368 | bytes 67108864 | tf_op jit(solution)/shard_map/outer/pallas_call | solution.py:320
  286.5 13.3 %expand_back.1 = (bf16[2,1024,1024]{2,1,0:T(8,128)(2,1)S(1)}, f32[2,1,1024]{2,1,0:T(1,128)S(1)}) custom-call(bf16[1024,2048]{1,0:T(8,128)(2,1)} %copy-done.6, bf16[2,2048,1024]{2,1,0:T(8,128)(2,1)} %bitcast.94, f32[2,1024,1024]{2,1,0:T(8,128)} %get-tuple-element.149.d_ref), custom_call_target="tpu_custom_call" | custom-call | flops 34359738368 | bytes 100663296 | tf_op jit(solution)/shard_map/expand_back/pallas_call | solution.py:244
  301.8 8.5 %contract.11 = (bf16[256,2048]{1,0:T(8,128)(2,1)}, bf16[256,2048]{1,0:T(8,128)(2,1)S(1)}) custom-call(bf16[2,1024,1024]{2,1,0:T(8,128)(2,1)} %copy-done.30, bf16[2,2048,1024]{2,1,0:T(8,128)(2,1)} %bitcast.92), custom_call_target="tpu_custom_call" | custom-call | flops 17179869184 | bytes 50331648 | tf_op jit(solution)/shard_map/contract/pallas_call | solution.py:277
  313.4 8.7 %contract.10 = (bf16[256,2048]{1,0:T(8,128)(2,1)S(1)}, bf16[256,2048]{1,0:T(8,128)(2,1)}) custom-call(bf16[2,1024,1024]{2,1,0:T(8,128)(2,1)} %copy-done.30, bf16[2,2048,1024]{2,1,0:T(8,128)(2,1)} %bitcast.93), custom_call_target="tpu_custom_call" | custom-call | flops 17179869184 | bytes 50331648 | tf_op jit(solution)/shard_map/contract/pallas_call | solution.py:277
  323.4 14.8 %outer.4 = bf16[4,2,512,1024]{3,2,1,0:T(8,128)(2,1)} custom-call(s32[2]{0:T(128)S(1)} %iota.49.pick_ref, bf16[1024,2048]{1,0:T(8,128)(2,1)S(1)} %copy-done.3, bf16[2,1024,1024]{2,1,0:T(8,128)(2,1)} %copy-done.30), custom_call_target="tpu_custom_call" | custom-call | flops 34359738368 | bytes 67108864 | tf_op jit(solution)/shard_map/outer/pallas_call | solution.py:320
  344.5 12.3 %collective-permute-done.39.refs_5_ = bf16[256,2048]{1,0:T(8,128)(2,1)S(1)} collective-permute-done((bf16[256,2048]{1,0:T(8,128)(2,1)S(1)}, bf16[256,2048]{1,0:T(8,128)(2,1)S(1)}, u32[]{:S(2)}, u32[]{:S(2)}) %collective-permute-start.39) | collective-permute-done | bytes 1048608 | tf_op jit(solution)/shard_map/ppermute | solution.py:600
  360.1 9.4 %middle_back.1 = (f32[512,2048]{1,0:T(8,128)}, f32[8,2048]{1,0:T(8,128)S(1)}, bf16[256,2048]{1,0:T(8,128)(2,1)S(1)}, bf16[256,2048]{1,0:T(8,128)(2,1)S(1)}) custom-call(bf16[256,2048]{1,0:T(8,128)(2,1)S(1)} %get-tuple-element.158.refs_0_, bf16[256,2048]{1,0:T(8,128)(2,1)S(1)} %collective-permute-done.37.refs_1_, ...), custom_call_target="tpu_custom_call" | custom-call | flops 83886080 | bytes 67108864 | tf_op jit(solution)/shard_map/middle_back/pallas_call | solution.py:457
  378.3 8.4 %contract.13 = (bf16[256,2048]{1,0:T(8,128)(2,1)S(1)}, bf16[256,2048]{1,0:T(8,128)(2,1)S(1)}) custom-call(bf16[2,1024,1024]{2,1,0:T(8,128)(2,1)} %copy-done.29, bf16[2,2048,1024]{2,1,0:T(8,128)(2,1)} %bitcast.95), custom_call_target="tpu_custom_call" | custom-call | flops 17179869184 | bytes 50331648 | tf_op jit(solution)/shard_map/contract/pallas_call | solution.py:277
  390.9 8.5 %contract.12 = (bf16[256,2048]{1,0:T(8,128)(2,1)}, bf16[256,2048]{1,0:T(8,128)(2,1)S(1)}) custom-call(bf16[2,1024,1024]{2,1,0:T(8,128)(2,1)} %copy-done.29, bf16[2,2048,1024]{2,1,0:T(8,128)(2,1)} %bitcast.96), custom_call_target="tpu_custom_call" | custom-call | flops 17179869184 | bytes 50331648 | tf_op jit(solution)/shard_map/contract/pallas_call | solution.py:277
  399.5 10.8 %collective-permute-done.40.refs_2_ = bf16[256,2048]{1,0:T(8,128)(2,1)S(1)} collective-permute-done((bf16[256,2048]{1,0:T(8,128)(2,1)S(1)}, bf16[256,2048]{1,0:T(8,128)(2,1)S(1)}, u32[]{:S(2)}, u32[]{:S(2)}) %collective-permute-start.40) | collective-permute-done | bytes 1048608 | tf_op jit(solution)/shard_map/ppermute | solution.py:600
  417.5 3.9 project.3.g_ref
  421.4 9.5 %attend_back.1.a_ref.refs_1_ = bf16[2,1024,768]{2,1,0:T(8,128)(2,1)} custom-call(s32[1024,8]{1,0:T(8,128)S(1)} %copy-done.21, bf16[2,1024,768]{2,1,0:T(8,128)(2,1)} %copy-done.31, bf16[2,1024,256]{2,1,0:T(8,128)(2,1)S(1)} %project.3.g_ref, f32[2,1024,256]{2,1,0:T(8,128)S(1)} %copy-done.33), custom_call_target="tpu_custom_call" | custom-call | flops 64424509440 | bytes 100663296 | tf_op jit(solution)/shard_map/attend_back/pallas_call | solution.py:163
  432.9 6.1 %contract.14 = (bf16[256,2048]{1,0:T(8,128)(2,1)S(1)}, bf16[256,2048]{1,0:T(8,128)(2,1)S(1)}) custom-call(bf16[2,1024,768]{2,1,0:T(8,128)(2,1)S(1)} %copy-done.28, bf16[2,2048,1024]{2,1,0:T(8,128)(2,1)} %bitcast.89), custom_call_target="tpu_custom_call" | custom-call | flops 12884901888 | bytes 39845888 | tf_op jit(solution)/shard_map/contract/pallas_call | solution.py:277
  441.5 6.1 %contract.15 = (bf16[256,2048]{1,0:T(8,128)(2,1)S(1)}, bf16[256,2048]{1,0:T(8,128)(2,1)S(1)}) custom-call(bf16[2,1024,768]{2,1,0:T(8,128)(2,1)S(1)} %copy-done.28, bf16[2,2048,1024]{2,1,0:T(8,128)(2,1)} %bitcast.90), custom_call_target="tpu_custom_call" | custom-call | flops 12884901888 | bytes 39845888 | tf_op jit(solution)/shard_map/contract/pallas_call | solution.py:277
  448.6 8.1 %collective-permute-done.48 = bf16[256,2048]{1,0:T(8,128)(2,1)S(1)} collective-permute-done((bf16[256,2048]{1,0:T(8,128)(2,1)S(1)}, bf16[256,2048]{1,0:T(8,128)(2,1)S(1)}, u32[]{:S(2)}, u32[]{:S(2)}) %collective-permute-start.48) | collective-permute-done | bytes 1048608 | tf_op jit(solution)/shard_map/ppermute | solution.py:600
  456.7 8.9 %collective-permute-done.49.refs_2_ = bf16[256,2048]{1,0:T(8,128)(2,1)S(1)} collective-permute-done((bf16[256,2048]{1,0:T(8,128)(2,1)S(1)}, bf16[256,2048]{1,0:T(8,128)(2,1)S(1)}, u32[]{:S(2)}, u32[]{:S(2)}) %collective-permute-start.49) | collective-permute-done | bytes 1048608 | tf_op jit(solution)/shard_map/ppermute | solution.py:600
  465.6 15.8 %outer.5 = bf16[4,2,512,1024]{3,2,1,0:T(8,128)(2,1)} custom-call(s32[2]{0:T(128)S(1)} %iota.42.pick_ref, bf16[1024,2048]{1,0:T(8,128)(2,1)} %copy-done.1, bf16[2,1024,768]{2,1,0:T(8,128)(2,1)S(1)} %copy-done.28, bf16[1024,2048]{1,0:T(8,128)(2,1)} %copy-done.4, bf16[2,1024,256]{2,1,0:T(8,128)(2,1)S(1)} %copy-done.27), custom_call_target="tpu_custom_call" | custom-call | flops 34359738368 | bytes 67108864 | tf_op jit(solution)/shard_map/outer/pallas_call | solution.py:320
  501.7 7.9 %collective-permute-done.59.refs_1_ = bf16[256,2048]{1,0:T(8,128)(2,1)S(1)} collective-permute-done((bf16[256,2048]{1,0:T(8,128)(2,1)S(1)}, bf16[256,2048]{1,0:T(8,128)(2,1)S(1)}, u32[]{:S(2)}, u32[]{:S(2)}) %collective-permute-start.59) | collective-permute-done | bytes 1048608 | tf_op jit(solution)/shard_map/ppermute | solution.py:600
  509.6 6.0 output.1
  520.8 11.2 %collective-permute-done.53.refs_1_ = bf16[256,2048]{1,0:T(8,128)(2,1)S(1)} collective-permute-done((bf16[256,2048]{1,0:T(8,128)(2,1)S(1)}, bf16[256,2048]{1,0:T(8,128)(2,1)S(1)}, u32[]{:S(2)}, u32[]{:S(2)}) %collective-permute-start.53) | collective-permute-done | bytes 1048608 | tf_op jit(solution)/shard_map/ppermute | solution.py:600
  532.1 7.4 %input_back.1 = (bf16[512,2048]{1,0:T(8,128)(2,1)}, f32[8,2048]{1,0:T(8,128)S(1)}) custom-call(bf16[256,2048]{1,0:T(8,128)(2,1)S(1)} %get-tuple-element.179.refs_0_, bf16[256,2048]{1,0:T(8,128)(2,1)S(1)} %collective-permute-done.53.refs_1_, bf16[256,2048]{1,0:T(8,128)(2,1)S(1)} %collective-permute-done.49.refs_2_, bf16[256,2048]{1,0:T(8,128)(2,1)S(1)} %copy-done.19, ...), custom_call_target="tpu_custom_call" | custom-call | flops 83886080 | bytes 67108864 | tf_op jit(solution)/shard_map/input_back/pallas_call | solution.py:457
  545.5 4.2 collective-permute-done.65
  557.3 3.7 collective-permute-done.67
  564.9 7.1 %collective-permute-start.58 = (bf16[128,1024]{1,0:T(8,128)(2,1)S(1)}, bf16[128,1024]{1,0:T(8,128)(2,1)S(1)}, u32[]{:S(2)}, u32[]{:S(2)}) collective-permute-start(bf16[128,1024]{1,0:T(8,128)(2,1)S(1)} %get-tuple-element.200), channel_id=1, source_target_pairs={{0,6},{1,7},{2,4},{3,5},{4,2},{5,3},{6,0},{7,1},{8,14},{9,15},{10,... | collective-permute-start | bytes 786440 | tf_op jit(solution)/shard_map/ppermute | solution.py:600
  591.7 5.2 collective-permute-done.69.refs_1_
  597.0 3.9 collective-permute-done.70.refs_2_
  (327 shorter events, 200.6 us)
Async XLA Ops:
  7.2 103.0 %all-gather.4.cloned.1.call-start = ((), (), s32[]{:S(2)}) async-start(), calls=%async_computation.3 | async-start | bytes 9437184 | tf_op jit(solution)/shard_map/all_gather | solution.py:651
  27.6 222.3 %all-gather.6.cloned.1.call-start = ((), (), s32[]{:S(2)}) async-start(), calls=%async_computation.4 | async-start | bytes 9437184 | tf_op jit(solution)/shard_map/all_gather | solution.py:651
  33.4 17.8 %collective-permute-start.4 = (bf16[256,2048]{1,0:T(8,128)(2,1)}, bf16[256,2048]{1,0:T(8,128)(2,1)S(1)}, u32[]{:S(2)}, u32[]{:S(2)}) collective-permute-start(bf16[256,2048]{1,0:T(8,128)(2,1)} %get-tuple-element.125.refs_1_), channel_id=1, source_target_pairs={{0,4},{3,7},{4,0},{7,3},{8,12},{11,15},{12,8},{15,11},{16,20},{19,... | collective-permute-start | bytes 3145736 | tf_op jit(solution)/shard_map/ppermute | solution.py:600
  36.2 36.7 %collective-permute-start.3 = (bf16[256,2048]{1,0:T(8,128)(2,1)S(1)}, bf16[256,2048]{1,0:T(8,128)(2,1)}, u32[]{:S(2)}, u32[]{:S(2)}) collective-permute-start(bf16[256,2048]{1,0:T(8,128)(2,1)S(1)} %get-tuple-element.124.refs_0_), channel_id=1, source_target_pairs={{0,4},{3,7},{4,0},{7,3},{8,12},{11,15},{12,8},{15,11},{16,20},{19,... | collective-permute-start | bytes 3145736 | tf_op jit(solution)/shard_map/ppermute | solution.py:600
  39.3 33.6 %collective-permute-start.6 = (bf16[256,2048]{1,0:T(8,128)(2,1)}, bf16[256,2048]{1,0:T(8,128)(2,1)}, u32[]{:S(2)}, u32[]{:S(2)}) collective-permute-start(bf16[256,2048]{1,0:T(8,128)(2,1)} %get-tuple-element.125.refs_1_), channel_id=1, source_target_pairs={{0,2},{3,1},{4,6},{7,5},{8,10},{11,9},{12,14},{15,13},{16,18},{19,... | collective-permute-start | bytes 3145736 | tf_op jit(solution)/shard_map/ppermute | solution.py:600
  45.7 27.3 %collective-permute-start.7 = (bf16[256,2048]{1,0:T(8,128)(2,1)S(1)}, bf16[256,2048]{1,0:T(8,128)(2,1)}, u32[]{:S(2)}, u32[]{:S(2)}) collective-permute-start(bf16[256,2048]{1,0:T(8,128)(2,1)S(1)} %collective-permute-done.5.refs_4_), channel_id=1, source_target_pairs={{1,5},{2,6},{5,1},{6,2},{9,13},{10,14},{13,9},{14,10},{17,21},{18,... | collective-permute-start | bytes 3145736 | tf_op jit(solution)/shard_map/ppermute | solution.py:600
  51.2 21.7 %collective-permute-start.8 = (bf16[256,2048]{1,0:T(8,128)(2,1)S(1)}, bf16[256,2048]{1,0:T(8,128)(2,1)}, u32[]{:S(2)}, u32[]{:S(2)}) collective-permute-start(bf16[256,2048]{1,0:T(8,128)(2,1)S(1)} %collective-permute-done.4.refs_3_), channel_id=1, source_target_pairs={{0,2},{3,1},{4,6},{7,5},{8,10},{11,9},{12,14},{15,13},{16,18},{19,... | collective-permute-start | bytes 3145736 | tf_op jit(solution)/shard_map/ppermute | solution.py:600
  91.8 194.7 %all-gather.8.cloned.1.call-start = ((), (), s32[]{:S(2)}) async-start(), calls=%async_computation.5 | async-start | bytes 9437184 | tf_op jit(solution)/shard_map/all_gather | solution.py:651
  109.5 305.7 %reduce-scatter.4.cloned.1.call-start = ((), (), s32[]{:S(2)}) async-start(), calls=%async_computation.6 | async-start | bytes 9437184 | tf_op jit(solution)/shard_map/reduce_scatter | solution.py:655
  132.8 24.9 %collective-permute-start.12 = (bf16[256,2048]{1,0:T(8,128)(2,1)S(1)}, bf16[256,2048]{1,0:T(8,128)(2,1)S(1)}, u32[]{:S(2)}, u32[]{:S(2)}) collective-permute-start(bf16[256,2048]{1,0:T(8,128)(2,1)S(1)} %get-tuple-element.127), channel_id=1, source_target_pairs={{0,4},{1,5},{2,6},{3,7},{4,0},{5,1},{6,2},{7,3},{8,12},{9,13},{10,... | collective-permute-start | bytes 3145736 | tf_op jit(solution)/shard_map/ppermute | solution.py:600
  138.1 25.4 %collective-permute-start.14 = (bf16[256,2048]{1,0:T(8,128)(2,1)S(1)}, bf16[256,2048]{1,0:T(8,128)(2,1)S(1)}, u32[]{:S(2)}, u32[]{:S(2)}) collective-permute-start(bf16[256,2048]{1,0:T(8,128)(2,1)S(1)} %get-tuple-element.132.refs_3_), channel_id=1, source_target_pairs={{1,3},{2,0},{5,7},{6,4},{9,11},{10,8},{13,15},{14,12},{17,19},{18,... | collective-permute-start | bytes 3145736 | tf_op jit(solution)/shard_map/ppermute | solution.py:600
  158.1 16.8 %collective-permute-start.15 = (bf16[256,2048]{1,0:T(8,128)(2,1)S(1)}, bf16[256,2048]{1,0:T(8,128)(2,1)S(1)}, u32[]{:S(2)}, u32[]{:S(2)}) collective-permute-start(bf16[256,2048]{1,0:T(8,128)(2,1)S(1)} %add_convert_fusion.6), channel_id=1, source_target_pairs={{0,4},{3,7},{4,0},{7,3},{8,12},{11,15},{12,8},{15,11},{16,20},{19,... | collective-permute-start | bytes 3145736 | tf_op jit(solution)/shard_map/ppermute | solution.py:600
  187.1 17.8 %collective-permute-start.17 = (bf16[256,2048]{1,0:T(8,128)(2,1)S(1)}, bf16[256,2048]{1,0:T(8,128)(2,1)S(1)}, u32[]{:S(2)}, u32[]{:S(2)}) collective-permute-start(bf16[256,2048]{1,0:T(8,128)(2,1)S(1)} %get-tuple-element.135.refs_1_), channel_id=1, source_target_pairs={{0,4},{3,7},{4,0},{7,3},{8,12},{11,15},{12,8},{15,11},{16,20},{19,... | collective-permute-start | bytes 3145736 | tf_op jit(solution)/shard_map/ppermute | solution.py:600
  190.1 36.1 %collective-permute-start.16 = (bf16[256,2048]{1,0:T(8,128)(2,1)S(1)}, bf16[256,2048]{1,0:T(8,128)(2,1)S(1)}, u32[]{:S(2)}, u32[]{:S(2)}) collective-permute-start(bf16[256,2048]{1,0:T(8,128)(2,1)S(1)} %get-tuple-element.134.refs_0_), channel_id=1, source_target_pairs={{0,4},{3,7},{4,0},{7,3},{8,12},{11,15},{12,8},{15,11},{16,20},{19,... | collective-permute-start | bytes 3145736 | tf_op jit(solution)/shard_map/ppermute | solution.py:600
  193.8 32.5 %collective-permute-start.19 = (bf16[256,2048]{1,0:T(8,128)(2,1)S(1)}, bf16[256,2048]{1,0:T(8,128)(2,1)S(1)}, u32[]{:S(2)}, u32[]{:S(2)}) collective-permute-start(bf16[256,2048]{1,0:T(8,128)(2,1)S(1)} %get-tuple-element.135.refs_1_), channel_id=1, source_target_pairs={{0,2},{3,1},{4,6},{7,5},{8,10},{11,9},{12,14},{15,13},{16,18},{19,... | collective-permute-start | bytes 3145736 | tf_op jit(solution)/shard_map/ppermute | solution.py:600
  199.3 26.9 %collective-permute-start.20 = (bf16[256,2048]{1,0:T(8,128)(2,1)S(1)}, bf16[256,2048]{1,0:T(8,128)(2,1)S(1)}, u32[]{:S(2)}, u32[]{:S(2)}) collective-permute-start(bf16[256,2048]{1,0:T(8,128)(2,1)S(1)} %collective-permute-done.18.refs_4_), channel_id=1, source_target_pairs={{1,5},{2,6},{5,1},{6,2},{9,13},{10,14},{13,9},{14,10},{17,21},{18,... | collective-permute-start | bytes 3145736 | tf_op jit(solution)/shard_map/ppermute | solution.py:600
  204.9 21.4 %collective-permute-start.21 = (bf16[256,2048]{1,0:T(8,128)(2,1)S(1)}, bf16[256,2048]{1,0:T(8,128)(2,1)S(1)}, u32[]{:S(2)}, u32[]{:S(2)}) collective-permute-start(bf16[256,2048]{1,0:T(8,128)(2,1)S(1)} %collective-permute-done.17.refs_3_), channel_id=1, source_target_pairs={{0,2},{3,1},{4,6},{7,5},{8,10},{11,9},{12,14},{15,13},{16,18},{19,... | collective-permute-start | bytes 3145736 | tf_op jit(solution)/shard_map/ppermute | solution.py:600
  230.0 16.8 %collective-permute-start.27 = (bf16[256,2048]{1,0:T(8,128)(2,1)S(1)}, bf16[256,2048]{1,0:T(8,128)(2,1)}, u32[]{:S(2)}, u32[]{:S(2)}) collective-permute-start(bf16[256,2048]{1,0:T(8,128)(2,1)S(1)} %get-tuple-element.142.refs_1_), channel_id=1, source_target_pairs={{0,4},{3,7},{4,0},{7,3},{8,12},{11,15},{12,8},{15,11},{16,20},{19,... | collective-permute-start | bytes 3145736 | tf_op jit(solution)/shard_map/ppermute | solution.py:600
  233.6 35.4 %collective-permute-start.26 = (bf16[256,2048]{1,0:T(8,128)(2,1)S(1)}, bf16[256,2048]{1,0:T(8,128)(2,1)}, u32[]{:S(2)}, u32[]{:S(2)}) collective-permute-start(bf16[256,2048]{1,0:T(8,128)(2,1)S(1)} %get-tuple-element.141.refs_0_), channel_id=1, source_target_pairs={{0,4},{3,7},{4,0},{7,3},{8,12},{11,15},{12,8},{15,11},{16,20},{19,... | collective-permute-start | bytes 3145736 | tf_op jit(solution)/shard_map/ppermute | solution.py:600
  237.1 31.9 %collective-permute-start.29 = (bf16[256,2048]{1,0:T(8,128)(2,1)S(1)}, bf16[256,2048]{1,0:T(8,128)(2,1)}, u32[]{:S(2)}, u32[]{:S(2)}) collective-permute-start(bf16[256,2048]{1,0:T(8,128)(2,1)S(1)} %get-tuple-element.142.refs_1_), channel_id=1, source_target_pairs={{0,2},{3,1},{4,6},{7,5},{8,10},{11,9},{12,14},{15,13},{16,18},{19,... | collective-permute-start | bytes 3145736 | tf_op jit(solution)/shard_map/ppermute | solution.py:600
  242.2 26.8 %collective-permute-start.30 = (bf16[256,2048]{1,0:T(8,128)(2,1)S(1)}, bf16[256,2048]{1,0:T(8,128)(2,1)}, u32[]{:S(2)}, u32[]{:S(2)}) collective-permute-start(bf16[256,2048]{1,0:T(8,128)(2,1)S(1)} %collective-permute-done.28.refs_4_), channel_id=1, source_target_pairs={{1,5},{2,6},{5,1},{6,2},{9,13},{10,14},{13,9},{14,10},{17,21},{18,... | collective-permute-start | bytes 3145736 | tf_op jit(solution)/shard_map/ppermute | solution.py:600
  246.8 22.3 %collective-permute-start.31 = (bf16[256,2048]{1,0:T(8,128)(2,1)}, bf16[256,2048]{1,0:T(8,128)(2,1)}, u32[]{:S(2)}, u32[]{:S(2)}) collective-permute-start(bf16[256,2048]{1,0:T(8,128)(2,1)} %collective-permute-done.27.refs_3_), channel_id=1, source_target_pairs={{0,2},{3,1},{4,6},{7,5},{8,10},{11,9},{12,14},{15,13},{16,18},{19,... | collective-permute-start | bytes 3145736 | tf_op jit(solution)/shard_map/ppermute | solution.py:600
  286.5 195.0 %reduce-scatter.6.cloned.1.call-start = ((), (), s32[]{:S(2)}) async-start(), calls=%async_computation.7 | async-start | bytes 9437184 | tf_op jit(solution)/shard_map/reduce_scatter | solution.py:655
  310.3 28.0 %collective-permute-start.35 = (bf16[256,2048]{1,0:T(8,128)(2,1)S(1)}, bf16[256,2048]{1,0:T(8,128)(2,1)}, u32[]{:S(2)}, u32[]{:S(2)}) collective-permute-start(bf16[256,2048]{1,0:T(8,128)(2,1)S(1)} %get-tuple-element.152), channel_id=1, source_target_pairs={{1,3},{2,0},{5,7},{6,4},{9,11},{10,8},{13,15},{14,12},{17,19},{18,... | collective-permute-start | bytes 3145736 | tf_op jit(solution)/shard_map/ppermute | solution.py:600
  311.6 26.7 %collective-permute-start.36 = (bf16[256,2048]{1,0:T(8,128)(2,1)}, bf16[256,2048]{1,0:T(8,128)(2,1)S(1)}, u32[]{:S(2)}, u32[]{:S(2)}) collective-permute-start(bf16[256,2048]{1,0:T(8,128)(2,1)} %get-tuple-element.153), channel_id=1, source_target_pairs={{0,4},{1,5},{2,6},{3,7},{4,0},{5,1},{6,2},{7,3},{8,12},{9,13},{10,... | collective-permute-start | bytes 3145736 | tf_op jit(solution)/shard_map/ppermute | solution.py:600
  322.1 22.4 %collective-permute-start.38 = (bf16[256,2048]{1,0:T(8,128)(2,1)}, bf16[256,2048]{1,0:T(8,128)(2,1)}, u32[]{:S(2)}, u32[]{:S(2)}) collective-permute-start(bf16[256,2048]{1,0:T(8,128)(2,1)} %get-tuple-element.161.refs_3_), channel_id=1, source_target_pairs={{1,3},{2,0},{5,7},{6,4},{9,11},{10,8},{13,15},{14,12},{17,19},{18,... | collective-permute-start | bytes 3145736 | tf_op jit(solution)/shard_map/ppermute | solution.py:600
  338.3 248.0 %reduce-scatter.8.cloned.1.call-start = ((), (), s32[]{:S(2)}) async-start(), calls=%async_computation.8 | async-start | bytes 9437184 | tf_op jit(solution)/shard_map/reduce_scatter | solution.py:655
  340.0 16.8 %collective-permute-start.39 = (bf16[256,2048]{1,0:T(8,128)(2,1)S(1)}, bf16[256,2048]{1,0:T(8,128)(2,1)S(1)}, u32[]{:S(2)}, u32[]{:S(2)}) collective-permute-start(bf16[256,2048]{1,0:T(8,128)(2,1)S(1)} %add_convert_fusion.4), channel_id=1, source_target_pairs={{0,4},{3,7},{4,0},{7,3},{8,12},{11,15},{12,8},{15,11},{16,20},{19,... | collective-permute-start | bytes 3145736 | tf_op jit(solution)/shard_map/ppermute | solution.py:600
  343.0 16.9 %collective-permute-start.37 = (bf16[256,2048]{1,0:T(8,128)(2,1)S(1)}, bf16[256,2048]{1,0:T(8,128)(2,1)S(1)}, u32[]{:S(2)}, u32[]{:S(2)}) collective-permute-start(bf16[256,2048]{1,0:T(8,128)(2,1)S(1)} %add_convert_fusion.5), channel_id=1, source_target_pairs={{1,3},{2,0},{5,7},{6,4},{9,11},{10,8},{13,15},{14,12},{17,19},{18,... | collective-permute-start | bytes 3145736 | tf_op jit(solution)/shard_map/ppermute | solution.py:600
  369.5 18.2 %collective-permute-start.42 = (bf16[256,2048]{1,0:T(8,128)(2,1)S(1)}, bf16[256,2048]{1,0:T(8,128)(2,1)S(1)}, u32[]{:S(2)}, u32[]{:S(2)}) collective-permute-start(bf16[256,2048]{1,0:T(8,128)(2,1)S(1)} %get-tuple-element.165.refs_0_), channel_id=1, source_target_pairs={{0,2},{3,1},{4,6},{7,5},{8,10},{11,9},{12,14},{15,13},{16,18},{19,... | collective-permute-start | bytes 3145736 | tf_op jit(solution)/shard_map/ppermute | solution.py:600
  371.1 17.4 %collective-permute-start.41 = (bf16[256,2048]{1,0:T(8,128)(2,1)S(1)}, bf16[256,2048]{1,0:T(8,128)(2,1)S(1)}, u32[]{:S(2)}, u32[]{:S(2)}) collective-permute-start(bf16[256,2048]{1,0:T(8,128)(2,1)S(1)} %get-tuple-element.166.refs_1_), channel_id=1, source_target_pairs={{0,4},{3,7},{4,0},{7,3},{8,12},{11,15},{12,8},{15,11},{16,20},{19,... | collective-permute-start | bytes 3145736 | tf_op jit(solution)/shard_map/ppermute | solution.py:600
  374.2 36.0 %collective-permute-start.40 = (bf16[256,2048]{1,0:T(8,128)(2,1)S(1)}, bf16[256,2048]{1,0:T(8,128)(2,1)S(1)}, u32[]{:S(2)}, u32[]{:S(2)}) collective-permute-start(bf16[256,2048]{1,0:T(8,128)(2,1)S(1)} %get-tuple-element.165.refs_0_), channel_id=1, source_target_pairs={{0,4},{3,7},{4,0},{7,3},{8,12},{11,15},{12,8},{15,11},{16,20},{19,... | collective-permute-start | bytes 3145736 | tf_op jit(solution)/shard_map/ppermute | solution.py:600
  376.9 33.3 %collective-permute-start.43 = (bf16[256,2048]{1,0:T(8,128)(2,1)S(1)}, bf16[256,2048]{1,0:T(8,128)(2,1)S(1)}, u32[]{:S(2)}, u32[]{:S(2)}) collective-permute-start(bf16[256,2048]{1,0:T(8,128)(2,1)S(1)} %get-tuple-element.166.refs_1_), channel_id=1, source_target_pairs={{0,2},{3,1},{4,6},{7,5},{8,10},{11,9},{12,14},{15,13},{16,18},{19,... | collective-permute-start | bytes 3145736 | tf_op jit(solution)/shard_map/ppermute | solution.py:600
  387.7 22.5 %collective-permute-start.44 = (bf16[256,2048]{1,0:T(8,128)(2,1)S(1)}, bf16[256,2048]{1,0:T(8,128)(2,1)S(1)}, u32[]{:S(2)}, u32[]{:S(2)}) collective-permute-start(bf16[256,2048]{1,0:T(8,128)(2,1)S(1)} %collective-permute-done.42.refs_4_), channel_id=1, source_target_pairs={{1,5},{2,6},{5,1},{6,2},{9,13},{10,14},{13,9},{14,10},{17,21},{18,... | collective-permute-start | bytes 3145736 | tf_op jit(solution)/shard_map/ppermute | solution.py:600
  388.5 21.8 %collective-permute-start.45 = (bf16[256,2048]{1,0:T(8,128)(2,1)S(1)}, bf16[256,2048]{1,0:T(8,128)(2,1)S(1)}, u32[]{:S(2)}, u32[]{:S(2)}) collective-permute-start(bf16[256,2048]{1,0:T(8,128)(2,1)S(1)} %collective-permute-done.41.refs_3_), channel_id=1, source_target_pairs={{0,2},{3,1},{4,6},{7,5},{8,10},{11,9},{12,14},{15,13},{16,18},{19,... | collective-permute-start | bytes 3145736 | tf_op jit(solution)/shard_map/ppermute | solution.py:600
  412.6 28.8 %collective-permute-start.46 = (bf16[256,2048]{1,0:T(8,128)(2,1)S(1)}, bf16[256,2048]{1,0:T(8,128)(2,1)}, u32[]{:S(2)}, u32[]{:S(2)}) collective-permute-start(bf16[256,2048]{1,0:T(8,128)(2,1)S(1)} %get-tuple-element.176), channel_id=1, source_target_pairs={{1,3},{2,0},{5,7},{6,4},{9,11},{10,8},{13,15},{14,12},{17,19},{18,... | collective-permute-start | bytes 3145736 | tf_op jit(solution)/shard_map/ppermute | solution.py:600
  413.9 27.5 %collective-permute-start.47 = (bf16[256,2048]{1,0:T(8,128)(2,1)}, bf16[256,2048]{1,0:T(8,128)(2,1)}, u32[]{:S(2)}, u32[]{:S(2)}) collective-permute-start(bf16[256,2048]{1,0:T(8,128)(2,1)} %get-tuple-element.177), channel_id=1, source_target_pairs={{0,4},{1,5},{2,6},{3,7},{4,0},{5,1},{6,2},{7,3},{8,12},{9,13},{10,... | collective-permute-start | bytes 3145736 | tf_op jit(solution)/shard_map/ppermute | solution.py:600
  439.0 17.7 %collective-permute-start.48 = (bf16[256,2048]{1,0:T(8,128)(2,1)S(1)}, bf16[256,2048]{1,0:T(8,128)(2,1)S(1)}, u32[]{:S(2)}, u32[]{:S(2)}) collective-permute-start(bf16[256,2048]{1,0:T(8,128)(2,1)S(1)} %get-tuple-element.175), channel_id=1, source_target_pairs={{1,3},{2,0},{5,7},{6,4},{9,11},{10,8},{13,15},{14,12},{17,19},{18,... | collective-permute-start | bytes 3145736 | tf_op jit(solution)/shard_map/ppermute | solution.py:600
  440.5 25.1 %collective-permute-start.49 = (bf16[256,2048]{1,0:T(8,128)(2,1)S(1)}, bf16[256,2048]{1,0:T(8,128)(2,1)S(1)}, u32[]{:S(2)}, u32[]{:S(2)}) collective-permute-start(bf16[256,2048]{1,0:T(8,128)(2,1)S(1)} %get-tuple-element.174), channel_id=1, source_target_pairs={{0,4},{1,5},{2,6},{3,7},{4,0},{5,1},{6,2},{7,3},{8,12},{9,13},{10,... | collective-permute-start | bytes 3145736 | tf_op jit(solution)/shard_map/ppermute | solution.py:600
  481.5 16.9 %collective-permute-start.60 = (bf16[256,2048]{1,0:T(8,128)(2,1)}, bf16[256,2048]{1,0:T(8,128)(2,1)S(1)}, u32[]{:S(2)}, u32[]{:S(2)}) collective-permute-start(bf16[256,2048]{1,0:T(8,128)(2,1)} %copy-done.16), channel_id=1, source_target_pairs={{1,3},{2,0},{5,7},{6,4},{9,11},{10,8},{13,15},{14,12},{17,19},{18,... | collective-permute-start | bytes 3145736 | tf_op jit(solution)/shard_map/ppermute | solution.py:600
  484.7 17.0 %collective-permute-start.61 = (bf16[256,2048]{1,0:T(8,128)(2,1)S(1)}, bf16[256,2048]{1,0:T(8,128)(2,1)S(1)}, u32[]{:S(2)}, u32[]{:S(2)}) collective-permute-start(bf16[256,2048]{1,0:T(8,128)(2,1)S(1)} %add_convert_fusion), channel_id=1, source_target_pairs={{0,4},{3,7},{4,0},{7,3},{8,12},{11,15},{12,8},{15,11},{16,20},{19,... | collective-permute-start | bytes 3145736 | tf_op jit(solution)/shard_map/ppermute | solution.py:600
  489.7 19.9 %collective-permute-start.59 = (bf16[256,2048]{1,0:T(8,128)(2,1)S(1)}, bf16[256,2048]{1,0:T(8,128)(2,1)S(1)}, u32[]{:S(2)}, u32[]{:S(2)}) collective-permute-start(bf16[256,2048]{1,0:T(8,128)(2,1)S(1)} %add_convert_fusion.1), channel_id=1, source_target_pairs={{1,3},{2,0},{5,7},{6,4},{9,11},{10,8},{13,15},{14,12},{17,19},{18,... | collective-permute-start | bytes 3145736 | tf_op jit(solution)/shard_map/ppermute | solution.py:600
  491.0 29.8 %collective-permute-start.54 = (bf16[256,2048]{1,0:T(8,128)(2,1)S(1)}, bf16[256,2048]{1,0:T(8,128)(2,1)S(1)}, u32[]{:S(2)}, u32[]{:S(2)}) collective-permute-start(bf16[256,2048]{1,0:T(8,128)(2,1)S(1)} %copy-done.19), channel_id=1, source_target_pairs={{1,3},{2,0},{5,7},{6,4},{9,11},{10,8},{13,15},{14,12},{17,19},{18,... | collective-permute-start | bytes 3145736 | tf_op jit(solution)/shard_map/ppermute | solution.py:600
  492.8 28.1 %collective-permute-start.55 = (bf16[256,2048]{1,0:T(8,128)(2,1)S(1)}, bf16[256,2048]{1,0:T(8,128)(2,1)S(1)}, u32[]{:S(2)}, u32[]{:S(2)}) collective-permute-start(bf16[256,2048]{1,0:T(8,128)(2,1)S(1)} %add_convert_fusion.2), channel_id=1, source_target_pairs={{0,4},{3,7},{4,0},{7,3},{8,12},{11,15},{12,8},{15,11},{16,20},{19,... | collective-permute-start | bytes 3145736 | tf_op jit(solution)/shard_map/ppermute | solution.py:600
  498.4 33.7 %collective-permute-start.53 = (bf16[256,2048]{1,0:T(8,128)(2,1)S(1)}, bf16[256,2048]{1,0:T(8,128)(2,1)S(1)}, u32[]{:S(2)}, u32[]{:S(2)}) collective-permute-start(bf16[256,2048]{1,0:T(8,128)(2,1)S(1)} %add_convert_fusion.3), channel_id=1, source_target_pairs={{1,3},{2,0},{5,7},{6,4},{9,11},{10,8},{13,15},{14,12},{17,19},{18,... | collective-permute-start | bytes 3145736 | tf_op jit(solution)/shard_map/ppermute | solution.py:600
  515.6 46.5 %collective-permute-start.62 = (bf16[512,2048]{1,0:T(8,128)(2,1)}, bf16[512,2048]{1,0:T(8,128)(2,1)}, u32[]{:S(2)}, u32[]{:S(2)}) collective-permute-start(bf16[512,2048]{1,0:T(8,128)(2,1)} %output.1), channel_id=1, source_target_pairs={{0,1},{3,2},{4,5},{7,6},{8,9},{11,10},{12,13},{15,14},{16,17},{19,... | collective-permute-start | bytes 6291464 | tf_op jit(solution)/shard_map/ppermute | solution.py:600
  539.5 43.6 %collective-permute-start.63 = (bf16[512,2048]{1,0:T(8,128)(2,1)}, bf16[512,2048]{1,0:T(8,128)(2,1)}, u32[]{:S(2)}, u32[]{:S(2)}) collective-permute-start(bf16[512,2048]{1,0:T(8,128)(2,1)} %get-tuple-element.206), channel_id=1, source_target_pairs={{0,1},{3,2},{4,5},{7,6},{8,9},{11,10},{12,13},{15,14},{16,17},{19,... | collective-permute-start | bytes 6291464 | tf_op jit(solution)/shard_map/ppermute | solution.py:600
  562.1 17.2 %collective-permute-start.56 = (bf16[128,1024]{1,0:T(8,128)(2,1)S(1)}, bf16[128,1024]{1,0:T(8,128)(2,1)S(1)}, u32[]{:S(2)}, u32[]{:S(2)}) collective-permute-start(bf16[128,1024]{1,0:T(8,128)(2,1)S(1)} %get-tuple-element.198), channel_id=1, source_target_pairs={{0,2},{1,3},{2,0},{3,1},{4,6},{5,7},{6,4},{7,5},{8,10},{9,11},{10,... | collective-permute-start | bytes 786440 | tf_op jit(solution)/shard_map/ppermute | solution.py:600
  (85 other events, 926.3 us)
Sparse Core Ops, SparseCore 0:
  27.7 82.3 all-gather.3
  112.3 80.5 all-gather.5
  194.5 80.5 all-gather.7
  286.6 89.6 reduce-scatter.3
  378.4 87.9 reduce-scatter.5
  481.6 89.1 reduce-scatter.7

commit v4 on v3

--- a/solution.py
+++ b/solution.py
@@ -151,7 +151,7 @@
         in_specs=[pl.BlockSpec((block, info.shape[1]), lambda b, c: (b, 0)), spec(width)],
         out_specs=[spec(width // 3)] * 2,
         out_shape=[jax.ShapeDtypeStruct((sides, rows, width // 3), t) for t in (BF, F32)],
-        compiler_params=params(),
+        compiler_params=params(16),
         cost_estimate=cost(16 * rows * block * width, 8 * rows * width * 2, rows * block * 4),
         name="attend",
     )(info, projected)
@@ -167,7 +167,7 @@
         out_specs=spec(width),
         out_shape=jax.ShapeDtypeStruct((sides, rows, width), BF),
         scratch_shapes=[pltpu.VMEM((block, width // 3), F32)] * 2,
-        compiler_params=params(),
+        compiler_params=params(20),
         cost_estimate=cost(40 * rows * block * width, 16 * rows * width * 2, rows * block * 4),
         name="attend_back",
     )(info, projected, mixed_back, log_sums)
@@ -175,6 +175,10 @@
 
 def steps(width, step=256):
     return [slice(j, min(j + step, width)) for j in range(0, width, step)]
+
+
+def far_away(v):
+    return pltpu.with_memory_space_constraint(v, pltpu.HBM)
 
 
 def project_kernel(a_ref, w_ref, o_ref):
@@ -191,10 +195,10 @@
         in_specs=[pl.BlockSpec((m, k), lambda c: (0, 0)), pl.BlockSpec((None, k, width), lambda c: (c, 0, column))],
         out_specs=pl.BlockSpec((None, m, width), lambda c: (c, 0, 0)),
         out_shape=jax.ShapeDtypeStruct((sides, m, width), BF),
-        compiler_params=params(),
+        compiler_params=params(24),
         cost_estimate=cost(2 * sides * m * k * width, 2 * (m * k + sides * k * width + sides * m * width)),
         name="project",
-    )(rows, weights)
+    )(far_away(rows), far_away(weights))
 
 
 def expand_kernel(a_ref, w_ref, b_ref, o_ref, d_ref):
@@ -223,10 +227,10 @@
         ],
         out_specs=[out, out],
         out_shape=[jax.ShapeDtypeStruct((sides, m, n), BF), jax.ShapeDtypeStruct((sides, m, n), F32)],
-        compiler_params=params(),
+        compiler_params=params(24),
         cost_estimate=cost(2 * sides * m * k * n, 2 * (m * k + sides * k * n) + 6 * sides * m * n, sides * m * n),
         name="expand",
-    )(rows, weights, bias)
+    )(far_away(rows), far_away(weights), bias)
 
 
 def expand_back_kernel(a_ref, w_ref, d_ref, o_ref, s_ref):
@@ -251,10 +255,10 @@
         ],
         out_specs=[out, pl.BlockSpec((None, 1, tile), lambda c, j: (c, 0, j))],
         out_shape=[jax.ShapeDtypeStruct((sides, m, n), BF), jax.ShapeDtypeStruct((sides, 1, n), F32)],
-        compiler_params=params(),
+        compiler_params=params(24),
         cost_estimate=cost(2 * sides * m * k * n, 2 * (m * k + sides * k * n) + 6 * sides * m * n),
         name="expand_back",
-    )(rows, weights, slope)
+    )(far_away(rows), far_away(weights), far_away(slope))
 
 
 def contract_kernel(a_ref, w_ref, top_ref, low_ref):
@@ -283,10 +287,10 @@
         ],
         out_specs=[half, half],
         out_shape=[out, out],
-        compiler_params=params(),
+        compiler_params=params(16),
         cost_estimate=cost(2 * sides * m * n * d, 2 * (sides * m * n + sides * n * d + m * d)),
         name="contract",
-    )(terms, weights)
+    )(terms, far_away(weights))
 
 
 def outer_kernel(pairs, adds, pick_ref, *refs):
@@ -322,9 +326,9 @@
         grid_spec=pltpu.PrefetchScalarGridSpec(
             num_scalar_prefetch=1, grid=(sides, depth), in_specs=specs, out_specs=place
         ),
-        out_shape=jax.ShapeDtypeStruct((depth, sides, tile, total), BF),
-        compiler_params=params(),
-        cost_estimate=cost(2 * sides * m * d * total, 2 * (m * d + sides * m * total + sides * d * total)),
+        out_shape=pltpu.HBM((depth, sides, tile, total), BF),
+        compiler_params=params(16),
+        cost_estimate=cost(4 * sides * m * d * total, 4 * (m * d + sides * m * total + sides * d * total)),
         name="outer",
     )(pick, *args)
 
@@ -460,7 +464,7 @@
         in_specs=specs,
         out_specs=out_specs,
         out_shape=outs,
-        compiler_params=params(),
+        compiler_params=params(24),
         cost_estimate=cost(20 * m * d, 16 * m * d),
         name=kernel.__name__.replace("_kernel", ""),
     )(*terms, *rows, *vectors)
@@ -492,7 +496,7 @@
         out_specs=pl.BlockSpec(memory_space=pltpu.VMEM),
         out_shape=jax.ShapeDtypeStruct((4 * rows, d), BF),
         scratch_shapes=[pltpu.SemaphoreType.DMA((4,))],
-        compiler_params=params(16),
+        compiler_params=params(10),
         cost_estimate=cost(0, 16 * rows * d),
         name="assemble",
     )(own, *mine, *theirs)
@@ -539,35 +543,39 @@
             out_specs=specs,
         ),
         out_shape=outs,
-        compiler_params=params(),
+        compiler_params=params(12),
         cost_estimate=cost(0, 16 * m * n),
         name="place",
     )(plane, *pieces)
 
 
-def part_kernel(plane_ref, v_ref, *outs):
+def part_kernel(plane_ref, *refs):
+    inputs, outs = refs[:-4], refs[-4:]
     for k in range(4):
 
         @pl.when(pl.program_id(0) == k)
         def _():
-            outs[k][...] = v_ref[...]
-
-
-def part_rows(plane, v):
-    m, n = v.shape[0] // 4, v.shape[1]
+            start = 0
+            for v_ref in inputs:
+                outs[k][:, start : start + v_ref.shape[1]] = v_ref[...]
+                start += v_ref.shape[1]
+
+
+def part_rows(plane, *arrays):
+    m, n = arrays[0].shape[0] // 4, sum(v.shape[1] for v in arrays)
     return pl.pallas_call(
         part_kernel,
         grid_spec=pltpu.PrefetchScalarGridSpec(
             num_scalar_prefetch=1,
             grid=(4,),
-            in_specs=[pl.BlockSpec((m, n), lambda k, p: (p[0] ^ k, 0))],
+            in_specs=[pl.BlockSpec((m, v.shape[1]), lambda k, p: (p[0] ^ k, 0)) for v in arrays],
             out_specs=[pl.BlockSpec((m, n), lambda k, p: (0, 0))] * 4,
         ),
-        out_shape=[jax.ShapeDtypeStruct((m, n), v.dtype)] * 4,
-        compiler_params=params(),
+        out_shape=[jax.ShapeDtypeStruct((m, n), BF)] * 4,
+        compiler_params=params(12),
         cost_estimate=cost(0, 16 * m * n),
         name="part_rows",
-    )(plane, v)
+    )(plane, *arrays)
 
 
 def after(value, *others):
@@ -647,8 +655,11 @@
         width = v.shape[-1] // 4
         return lax.dynamic_slice_in_dim(v, (plane ^ k) * width, width, axis=-1)
 
-    def gather(pieces):
-        full = lax.all_gather(place(plane_flag, pieces, 0, BF)[0], ("c", "z"), axis=0, tiled=True)
+    def placed_rows(pieces):
+        return place(plane_flag, pieces, 0, BF)[0]
+
+    def gather(rows):
+        full = lax.all_gather(rows, ("c", "z"), axis=0, tiled=True)
         return full.reshape(2, full.shape[0] // 2, full.shape[1])
 
     def scatter(terms, axes):
@@ -667,7 +678,7 @@
         return jnp.concatenate([heads[:, 0], heads[:, 1], heads[:, 2], columns(output_weight, k)], axis=1)
 
     heads_got = shuffle([attention_columns(k) for k in range(4)])
-    heads_all = gather(heads_got)
+    heads_all = gather(placed_rows(heads_got))
 
     info, live = bounds_of(group_sizes, prefix_lengths, solution_lengths, block)
     info = jnp.pad(info, ((0, 0), (0, 5)))
@@ -679,9 +690,9 @@
     first = spread_on(spread_out(*first_own))
 
     expand_got = shuffle([columns(expand_weight, k) for k in range(4)], first)
-    expand_all = gather(expand_got)
+    expand_all = gather(placed_rows(expand_got))
     reduce_got = shuffle([columns(reduce_weight, k) for k in range(4)], *expand_got)
-    reduce_all = gather(reduce_got)
+    reduce_rows = placed_rows(reduce_got)
     bias_mine = lax.dynamic_slice_in_dim(expand_bias, plane * inner, inner).reshape(1, 1, inner)
     bias_other = send(bias_mine, lambda y, x, c: (y, x, 1 - c))
     bias = wide(
@@ -691,6 +702,8 @@
     upstream_own = (upstream_own[: block // 2], upstream_own[block // 2 :])
 
     both = jnp.arange(2, dtype=jnp.int32)
+    first, reduce_rows, bias = lax.optimization_barrier((first, reduce_rows, bias))
+    reduce_all = gather(reduce_rows)
     projected = project(first, heads_all, 3 * part, 0)
     mixed, log_sums = attend(info_two, projected, block)
     far = contract(mixed, heads_all, 3, 1)
@@ -729,22 +742,20 @@
 
     mixed_back = project(after(middle_low, reduce_part, *far, *near), heads_all, part, 3)
     projected_back = attend_back(info_two, projected, mixed_back, log_sums, block)
-    far = contract(projected_back, heads_all, 0, 1)
-    near = contract(after(projected_back, *far, *moved), heads_all, 0, 0)
-    first_back, ahead = collect(far, near)
-    heads_terms = outer(both, [(first, after(projected_back, *near, *ahead)), (middle_low, mixed)], depth)
-    heads_part = scatter(after(heads_terms, expand_part), ("z", "c"))
-    reduce_got = shuffle(part_rows(plane_flag, reduce_part), *far, *near)
+    heads_terms = outer(both, [(first, after(projected_back, *moved)), (middle_low, mixed)], depth)
+    heads_part = scatter(heads_terms, ("z", "c"))
+    far = contract(after(projected_back, heads_terms), heads_all, 0, 1)
+    near = contract(after(projected_back, *far), heads_all, 0, 0)
+    first_back, _ = collect(far, near)
     (outputs,) = over_rows(output_kernel, branch, (middle, live_wide), (row(reduce_bias),), (BF,))
     outputs = from_owner(outputs)
-    (reduce_gradient,) = place(plane_flag, reduce_got, 1, F32)
     input_gradient, sums_first = over_rows(
         input_back_kernel, first_back, (inputs, middle_back), (row(gamma_first),), (BF,), sums=True
     )
     input_gradient = from_owner(input_gradient)
 
-    expand_got = shuffle(part_rows(plane_flag, expand_part), *first_back)
-    (expand_gradient,) = place(plane_flag, expand_got, 1, F32)
+    feed_got = shuffle(part_rows(plane_flag, reduce_part, expand_part), *first_back)
+    reduce_gradient, expand_gradient = place(plane_flag, feed_got, 1, F32, (1, 1))
     gamma_first_gradient, beta_first_gradient = sums_first[0], sums_first[1]
     gamma_second_gradient, beta_second_gradient = sums_second[0], sums_second[1]
     output_bias_gradient, reduce_bias_gradient = sums_second[2], sums_second[3]

time: 621 us -> 603 us (0.971)
  Pallas kernels: 207 us -> 187 us
  waiting for transfers between devices: 218 us -> 231 us
  starting transfers between devices: 126 us -> 116 us
    ppermute x70 -> x67, starting transfers between devices: 124 us -> 111 us  [body(): send = lambda v, route: lax.ppermute(v, ALL, pairs_of(depth, route))]
    ppermute x70 -> x67, waiting for transfers between devices: 214 us -> 225 us  [body(): send = lambda v, route: lax.ppermute(v, ALL, pairs_of(depth, route))]
    pallas_call x5, Pallas kernels: 32.1 us -> 22.7 us  [over_rows(): pl.pallas_call(functools.partial(kernel, m // 2 // TILE), grid=(m // TILE...]
    pallas_call x3, Pallas kernels: 46.3 us -> 39 us  [outer(): pl.pallas_call(functools.partial(outer_kernel, len(pairs), extra is not N...]
    unnamed x109 -> x111, local copies, waits for them, and re-layouts: 20.4 us -> 16.1 us
  transfers between devices with their start and end apart: 78 -> 75, of which waited for: 37 -> 39; matrix products, arithmetic and copies ran while one was open for 3% -> 4% of each run, Pallas kernels for 33% -> 31%
where the time goes in v4:
time: 603 us; the launch traced here: 593 us
  waiting for transfers between devices  231 us (38%)
  Pallas kernels  187 us (31%)
  starting transfers between devices  116 us (19%)
  local copies, waits for them, and re-layouts  24.3 us (4%)
  other arithmetic  18.3 us (3%)
  between operations  16.1 us (3%)
    ppermute x67, waiting for transfers between devices, body(): send = lambda v, route: lax.ppermute(v, ALL, pairs_of(depth, route))  225 us
    ppermute x67, starting transfers between devices, body(): send = lambda v, route: lax.ppermute(v, ALL, pairs_of(depth, route))  111 us
    pallas_call x8, Pallas kernels, contract(): pl.pallas_call(contract_kernel, grid=(d // tile,), in_specs=[pl.BlockSpec...  52.1 us
    pallas_call x3, Pallas kernels, outer(): pl.pallas_call(functools.partial(outer_kernel, len(pairs), extra is not N...  39 us
    pallas_call x5, Pallas kernels, over_rows(): pl.pallas_call(functools.partial(kernel, m // 2 // TILE), grid=(m // TILE...  22.7 us
    pallas_call x1, Pallas kernels, expand(): pl.pallas_call(expand_kernel, grid=(sides, n // tile), in_specs=[pl.Block...  16.8 us
    unnamed x111, local copies, waits for them, and re-layouts  16.1 us
    pallas_call x2, Pallas kernels, project(): pl.pallas_call(project_kernel, grid=(sides,), in_specs=[pl.BlockSpec((m,...  15.3 us
  transfers between devices with their start and end apart: 75, of which 39 were waited for; matrix products, arithmetic and copies ran while one was open for 4% of the time, Pallas kernels for 31%

profile of v4, /device:TPU:0, one launch (start us, length us, event | category | flops | bytes accessed | tf_op | source)
XLA Modules:
  0.0 592.5 jit_solution(17382290197703599447)
XLA Ops:
  14.2 5.6 collective-permute-done.refs_1_
  19.8 6.2 %collective-permute-done.1.refs_2_ = bf16[128,1024]{1,0:T(8,128)(2,1)S(1)} collective-permute-done((bf16[128,1024]{1,0:T(8,128)(2,1)S(1)}, bf16[128,1024]{1,0:T(8,128)(2,1)S(1)}, u32[]{:S(2)}, u32[]{:S(2)}) %collective-permute-start.1) | collective-permute-done | bytes 262176 | tf_op jit(solution)/shard_map/ppermute | solution.py:608
  30.2 4.2 collective-permute-start.5
  47.3 5.7 collective-permute-done.4.refs_3_
  56.6 17.3 %collective-permute-done.3.refs_2_ = bf16[256,2048]{1,0:T(8,128)(2,1)} collective-permute-done((bf16[256,2048]{1,0:T(8,128)(2,1)S(1)}, bf16[256,2048]{1,0:T(8,128)(2,1)}, u32[]{:S(2)}, u32[]{:S(2)}) %collective-permute-start.3) | collective-permute-done | bytes 1048608 | tf_op jit(solution)/shard_map/ppermute | solution.py:608
  81.6 9.1 %collective-permute-done.10.refs_2_ = bf16[128,1024]{1,0:T(8,128)(2,1)S(1)} collective-permute-done((bf16[128,1024]{1,0:T(8,128)(2,1)S(1)}, bf16[128,1024]{1,0:T(8,128)(2,1)S(1)}, u32[]{:S(2)}, u32[]{:S(2)}) %collective-permute-start.10) | collective-permute-done | bytes 262176 | tf_op jit(solution)/shard_map/ppermute | solution.py:608
  101.7 9.9 %collective-permute-done.17 = s32[512,8]{0,1:T(8,128)S(1)} collective-permute-done((s32[512,8]{0,1:T(8,128)S(1)}, s32[512,8]{0,1:T(8,128)S(1)}, u32[]{:S(2)}, u32[]{:S(2)}) %collective-permute-start.17) | collective-permute-done | bytes 16416 | tf_op jit(solution)/shard_map/ppermute | solution.py:608
  114.2 10.0 %project.2.p_ref = bf16[2,1024,768]{2,1,0:T(8,128)(2,1)S(1)} custom-call(bf16[1024,2048]{1,0:T(8,128)(2,1)} %copy-done.7, bf16[2,2048,1024]{2,1,0:T(8,128)(2,1)} %bitcast.85), custom_call_target="tpu_custom_call" | custom-call | flops 25769803776 | bytes 54525952 | tf_op jit(solution)/shard_map/project/pallas_call | solution.py:192
  124.2 4.3 attend.1
  128.5 5.0 contract.8
  137.0 3.7 contract.9
  142.0 8.5 %collective-permute-done.18 = bf16[256,2048]{1,0:T(8,128)(2,1)} collective-permute-done((bf16[256,2048]{1,0:T(8,128)(2,1)}, bf16[256,2048]{1,0:T(8,128)(2,1)}, u32[]{:S(2)}, u32[]{:S(2)}) %collective-permute-start.18) | collective-permute-done | bytes 1048608 | tf_op jit(solution)/shard_map/ppermute | solution.py:608
  150.5 8.9 %collective-permute-done.19.refs_2_ = bf16[256,2048]{1,0:T(8,128)(2,1)S(1)} collective-permute-done((bf16[256,2048]{1,0:T(8,128)(2,1)}, bf16[256,2048]{1,0:T(8,128)(2,1)S(1)}, u32[]{:S(2)}, u32[]{:S(2)}) %collective-permute-start.19) | collective-permute-done | bytes 1048608 | tf_op jit(solution)/shard_map/ppermute | solution.py:608
  166.5 11.8 %collective-permute-done.22.refs_5_ = bf16[256,2048]{1,0:T(8,128)(2,1)S(1)} collective-permute-done((bf16[256,2048]{1,0:T(8,128)(2,1)S(1)}, bf16[256,2048]{1,0:T(8,128)(2,1)S(1)}, u32[]{:S(2)}, u32[]{:S(2)}) %collective-permute-start.22) | collective-permute-done | bytes 1048608 | tf_op jit(solution)/shard_map/ppermute | solution.py:608
  178.3 3.5 collective-permute-done.20.refs_1_
  194.2 4.2 collective-permute-done.25.refs_4_
  199.1 5.5 collective-permute-done.24.refs_3_
  207.6 17.7 %collective-permute-done.23.refs_2_ = bf16[256,2048]{1,0:T(8,128)(2,1)S(1)} collective-permute-done((bf16[256,2048]{1,0:T(8,128)(2,1)S(1)}, bf16[256,2048]{1,0:T(8,128)(2,1)S(1)}, u32[]{:S(2)}, u32[]{:S(2)}) %collective-permute-start.23) | collective-permute-done | bytes 1048608 | tf_op jit(solution)/shard_map/ppermute | solution.py:608
  249.7 16.8 %expand.1 = (bf16[2,1024,1024]{2,1,0:T(8,128)(2,1)S(1)}, f32[2,1024,1024]{2,1,0:T(8,128)S(1)}) custom-call(bf16[1024,2048]{1,0:T(8,128)(2,1)} %copy-done.9, bf16[2,2048,1024]{2,1,0:T(8,128)(2,1)} %bitcast.91, f32[2,1,1024]{2,1,0:T(1,128)S(1)} %fusion.b_ref), custom_call_target="tpu_custom_call" | custom-call | flops 34359738368 | bytes 100663296 | tf_op jit(solution)/shard_map/expand/pallas_call | solution.py:220
  268.8 3.8 assemble.6.refs_0_.a_ref
  272.7 12.8 %outer.3 = bf16[4,2,512,1024]{3,2,1,0:T(8,128)(2,1)} custom-call(s32[2]{0:T(128)S(1)} %iota.48.pick_ref, bf16[1024,2048]{1,0:T(8,128)(2,1)S(1)} %assemble.6.refs_0_.a_ref, bf16[2,1024,1024]{2,1,0:T(8,128)(2,1)S(1)} %get-tuple-element.167.refs_1_.a_ref), custom_call_target="tpu_custom_call" | custom-call | flops 68719476736 | bytes 134217728 | tf_op jit(solution)/shard_map/outer/pallas_call | solution.py:324
  285.6 13.3 %expand_back.1 = (bf16[2,1024,1024]{2,1,0:T(8,128)(2,1)S(1)}, f32[2,1,1024]{2,1,0:T(1,128)S(1)}) custom-call(bf16[1024,2048]{1,0:T(8,128)(2,1)} %copy-done.13, bf16[2,2048,1024]{2,1,0:T(8,128)(2,1)} %bitcast.94, f32[2,1024,1024]{2,1,0:T(8,128)} %copy-done.38), custom_call_target="tpu_custom_call" | custom-call | flops 34359738368 | bytes 100663296 | tf_op jit(solution)/shard_map/expand_back/pallas_call | solution.py:248
  298.9 7.3 %contract.11 = (bf16[256,2048]{1,0:T(8,128)(2,1)S(1)}, bf16[256,2048]{1,0:T(8,128)(2,1)S(1)}) custom-call(bf16[2,1024,1024]{2,1,0:T(8,128)(2,1)S(1)} %get-tuple-element.155.a_ref.refs_1_, bf16[2,2048,1024]{2,1,0:T(8,128)(2,1)} %bitcast.92), custom_call_target="tpu_custom_call" | custom-call | flops 17179869184 | bytes 50331648 | tf_op jit(solution)/shard_map/contract/pallas_call | solution.py:281
  309.2 8.0 %contract.10 = (bf16[256,2048]{1,0:T(8,128)(2,1)S(1)}, bf16[256,2048]{1,0:T(8,128)(2,1)}) custom-call(bf16[2,1024,1024]{2,1,0:T(8,128)(2,1)S(1)} %get-tuple-element.155.a_ref.refs_1_, bf16[2,2048,1024]{2,1,0:T(8,128)(2,1)} %bitcast.93), custom_call_target="tpu_custom_call" | custom-call | flops 17179869184 | bytes 50331648 | tf_op jit(solution)/shard_map/contract/pallas_call | solution.py:281
  318.5 12.8 %outer.4 = bf16[4,2,512,1024]{3,2,1,0:T(8,128)(2,1)} custom-call(s32[2]{0:T(128)S(1)} %iota.49.pick_ref, bf16[1024,2048]{1,0:T(8,128)(2,1)S(1)} %copy-done.10, bf16[2,1024,1024]{2,1,0:T(8,128)(2,1)S(1)} %get-tuple-element.155.a_ref.refs_1_), custom_call_target="tpu_custom_call" | custom-call | flops 68719476736 | bytes 134217728 | tf_op jit(solution)/shard_map/outer/pallas_call | solution.py:324
  339.7 10.9 %collective-permute-done.39.refs_5_ = bf16[256,2048]{1,0:T(8,128)(2,1)} collective-permute-done((bf16[256,2048]{1,0:T(8,128)(2,1)}, bf16[256,2048]{1,0:T(8,128)(2,1)}, u32[]{:S(2)}, u32[]{:S(2)}) %collective-permute-start.39) | collective-permute-done | bytes 1048608 | tf_op jit(solution)/shard_map/ppermute | solution.py:608
  350.6 4.5 collective-permute-done.37.refs_1_
  360.4 7.4 %middle_back.1 = (f32[512,2048]{1,0:T(8,128)S(1)}, f32[8,2048]{1,0:T(8,128)S(1)}, bf16[256,2048]{1,0:T(8,128)(2,1)S(1)}, bf16[256,2048]{1,0:T(8,128)(2,1)S(1)}) custom-call(bf16[256,2048]{1,0:T(8,128)(2,1)S(1)} %copy-done.17, bf16[256,2048]{1,0:T(8,128)(2,1)} %collective-permute-done.37.refs_1_, bf16[256,2048]{1,0:T(8,128)(2,1)S(1)} %collective-permute-done.36.refs_2_, ...), custom_call_target="tpu_custom_call" | custom-call | flops 83886080 | bytes 67108864 | tf_op jit(solution)/shard_map/middle_back/pallas_call | solution.py:461
  376.4 7.7 %contract.13 = (bf16[256,2048]{1,0:T(8,128)(2,1)S(1)}, bf16[256,2048]{1,0:T(8,128)(2,1)S(1)}) custom-call(bf16[2,1024,1024]{2,1,0:T(8,128)(2,1)S(1)} %copy-done.37, bf16[2,2048,1024]{2,1,0:T(8,128)(2,1)} %bitcast.95), custom_call_target="tpu_custom_call" | custom-call | flops 17179869184 | bytes 50331648 | tf_op jit(solution)/shard_map/contract/pallas_call | solution.py:281
  384.9 4.6 collective-permute-done.41.refs_3_
  390.9 8.1 %contract.12 = (bf16[256,2048]{1,0:T(8,128)(2,1)}, bf16[256,2048]{1,0:T(8,128)(2,1)}) custom-call(bf16[2,1024,1024]{2,1,0:T(8,128)(2,1)S(1)} %copy-done.37, bf16[2,2048,1024]{2,1,0:T(8,128)(2,1)} %bitcast.96), custom_call_target="tpu_custom_call" | custom-call | flops 17179869184 | bytes 50331648 | tf_op jit(solution)/shard_map/contract/pallas_call | solution.py:281
  398.9 9.4 %collective-permute-done.40.refs_2_ = bf16[256,2048]{1,0:T(8,128)(2,1)S(1)} collective-permute-done((bf16[256,2048]{1,0:T(8,128)(2,1)S(1)}, bf16[256,2048]{1,0:T(8,128)(2,1)S(1)}, u32[]{:S(2)}, u32[]{:S(2)}) %collective-permute-start.40) | collective-permute-done | bytes 1048608 | tf_op jit(solution)/shard_map/ppermute | solution.py:608
  413.1 5.3 project.3.g_ref
  418.4 7.3 %attend_back.1.refs_1_.a_ref = bf16[2,1024,768]{2,1,0:T(8,128)(2,1)S(1)} custom-call(s32[1024,8]{1,0:T(8,128)S(1)} %copy-done.26, bf16[2,1024,768]{2,1,0:T(8,128)(2,1)S(1)} %copy-done.40, bf16[2,1024,256]{2,1,0:T(8,128)(2,1)S(1)} %project.3.g_ref, f32[2,1024,256]{2,1,0:T(8,128)S(1)} %copy-done.42), custom_call_target="tpu_custom_call" | custom-call | flops 64424509440 | bytes 100663296 | tf_op jit(solution)/shard_map/attend_back/pallas_call | solution.py:163
  427.7 7.2 %collective-permute-done.47.refs_2_ = bf16[256,2048]{1,0:T(8,128)(2,1)} collective-permute-done((bf16[256,2048]{1,0:T(8,128)(2,1)}, bf16[256,2048]{1,0:T(8,128)(2,1)}, u32[]{:S(2)}, u32[]{:S(2)}) %collective-permute-start.47) | collective-permute-done | bytes 1048608 | tf_op jit(solution)/shard_map/ppermute | solution.py:608
  435.0 13.4 %outer.5 = bf16[4,2,512,1024]{3,2,1,0:T(8,128)(2,1)} custom-call(s32[2]{0:T(128)S(1)} %iota.42.pick_ref, bf16[1024,2048]{1,0:T(8,128)(2,1)S(1)} %copy-done.8, bf16[2,1024,768]{2,1,0:T(8,128)(2,1)S(1)} %attend_back.1.refs_1_.a_ref, bf16[1024,2048]{1,0:T(8,128)(2,1)S(1)} %copy-done.12, bf16[2,1024,256]{2,1,0:T(8,128)(2,1)S(1)} %copy-done.33), custom_call_target="tpu_custom_call" | custom-call | flops 68719476736 | bytes 134217728 | tf_op jit(solution)/shard_map/outer/pallas_call | solution.py:324
  458.1 6.2 %contract.14 = (bf16[256,2048]{1,0:T(8,128)(2,1)S(1)}, bf16[256,2048]{1,0:T(8,128)(2,1)S(1)}) custom-call(bf16[2,1024,768]{2,1,0:T(8,128)(2,1)S(1)} %copy-done.35, bf16[2,2048,1024]{2,1,0:T(8,128)(2,1)} %bitcast.89), custom_call_target="tpu_custom_call" | custom-call | flops 12884901888 | bytes 39845888 | tf_op jit(solution)/shard_map/contract/pallas_call | solution.py:281
  466.6 6.1 %contract.15 = (bf16[256,2048]{1,0:T(8,128)(2,1)S(1)}, bf16[256,2048]{1,0:T(8,128)(2,1)S(1)}) custom-call(bf16[2,1024,768]{2,1,0:T(8,128)(2,1)S(1)} %copy-done.35, bf16[2,2048,1024]{2,1,0:T(8,128)(2,1)} %bitcast.90), custom_call_target="tpu_custom_call" | custom-call | flops 12884901888 | bytes 39845888 | tf_op jit(solution)/shard_map/contract/pallas_call | solution.py:281
  472.7 15.1 %collective-permute-done.48 = bf16[256,2048]{1,0:T(8,128)(2,1)S(1)} collective-permute-done((bf16[256,2048]{1,0:T(8,128)(2,1)S(1)}, bf16[256,2048]{1,0:T(8,128)(2,1)S(1)}, u32[]{:S(2)}, u32[]{:S(2)}) %collective-permute-start.48) | collective-permute-done | bytes 1048608 | tf_op jit(solution)/shard_map/ppermute | solution.py:608
  496.6 4.8 output.1
  504.5 4.0 collective-permute-done.52.refs_5_
  508.5 7.2 %collective-permute-done.50.refs_1_ = bf16[256,2048]{1,0:T(8,128)(2,1)S(1)} collective-permute-done((bf16[256,2048]{1,0:T(8,128)(2,1)S(1)}, bf16[256,2048]{1,0:T(8,128)(2,1)S(1)}, u32[]{:S(2)}, u32[]{:S(2)}) %collective-permute-start.50) | collective-permute-done | bytes 1048608 | tf_op jit(solution)/shard_map/ppermute | solution.py:608
  515.7 5.1 input_back.1
  526.2 4.7 collective-permute-done.62
  549.0 4.0 collective-permute-done.65
  554.7 9.3 %collective-permute-done.55.refs_3_ = bf16[128,2048]{1,0:T(8,128)(2,1)S(1)} collective-permute-done((bf16[128,2048]{1,0:T(8,128)(2,1)}, bf16[128,2048]{1,0:T(8,128)(2,1)S(1)}, u32[]{:S(2)}, u32[]{:S(2)}) %collective-permute-start.55) | collective-permute-done | bytes 524320 | tf_op jit(solution)/shard_map/ppermute | solution.py:608
  575.1 4.7 collective-permute-done.66.refs_1_
  579.8 3.6 collective-permute-done.67.refs_2_
  (321 shorter events, 199.9 us)
Async XLA Ops:
  7.2 107.0 %all-gather.4.cloned.1.call-start = ((), (), s32[]{:S(2)}) async-start(), calls=%async_computation.3 | async-start | bytes 9437184 | tf_op jit(solution)/shard_map/all_gather | solution.py:662
  27.6 222.1 %all-gather.6.cloned.1.call-start = ((), (), s32[]{:S(2)}) async-start(), calls=%async_computation.4 | async-start | bytes 9437184 | tf_op jit(solution)/shard_map/all_gather | solution.py:662
  34.4 18.6 %collective-permute-start.4 = (bf16[256,2048]{1,0:T(8,128)(2,1)}, bf16[256,2048]{1,0:T(8,128)(2,1)}, u32[]{:S(2)}, u32[]{:S(2)}) collective-permute-start(bf16[256,2048]{1,0:T(8,128)(2,1)} %get-tuple-element.122.refs_1_), channel_id=1, source_target_pairs={{0,4},{3,7},{4,0},{7,3},{8,12},{11,15},{12,8},{15,11},{16,20},{19,... | collective-permute-start | bytes 3145736 | tf_op jit(solution)/shard_map/ppermute | solution.py:608
  37.1 36.7 %collective-permute-start.3 = (bf16[256,2048]{1,0:T(8,128)(2,1)S(1)}, bf16[256,2048]{1,0:T(8,128)(2,1)}, u32[]{:S(2)}, u32[]{:S(2)}) collective-permute-start(bf16[256,2048]{1,0:T(8,128)(2,1)S(1)} %get-tuple-element.121.refs_0_), channel_id=1, source_target_pairs={{0,4},{3,7},{4,0},{7,3},{8,12},{11,15},{12,8},{15,11},{16,20},{19,... | collective-permute-start | bytes 3145736 | tf_op jit(solution)/shard_map/ppermute | solution.py:608
  40.3 33.6 %collective-permute-start.6 = (bf16[256,2048]{1,0:T(8,128)(2,1)}, bf16[256,2048]{1,0:T(8,128)(2,1)}, u32[]{:S(2)}, u32[]{:S(2)}) collective-permute-start(bf16[256,2048]{1,0:T(8,128)(2,1)} %get-tuple-element.122.refs_1_), channel_id=1, source_target_pairs={{0,2},{3,1},{4,6},{7,5},{8,10},{11,9},{12,14},{15,13},{16,18},{19,... | collective-permute-start | bytes 3145736 | tf_op jit(solution)/shard_map/ppermute | solution.py:608
  45.7 28.2 %collective-permute-start.7 = (bf16[256,2048]{1,0:T(8,128)(2,1)}, bf16[256,2048]{1,0:T(8,128)(2,1)}, u32[]{:S(2)}, u32[]{:S(2)}) collective-permute-start(bf16[256,2048]{1,0:T(8,128)(2,1)} %collective-permute-done.5.refs_4_), channel_id=1, source_target_pairs={{1,5},{2,6},{5,1},{6,2},{9,13},{10,14},{13,9},{14,10},{17,21},{18,... | collective-permute-start | bytes 3145736 | tf_op jit(solution)/shard_map/ppermute | solution.py:608
  53.0 20.9 %collective-permute-start.8 = (bf16[256,2048]{1,0:T(8,128)(2,1)}, bf16[256,2048]{1,0:T(8,128)(2,1)}, u32[]{:S(2)}, u32[]{:S(2)}) collective-permute-start(bf16[256,2048]{1,0:T(8,128)(2,1)} %collective-permute-done.4.refs_3_), channel_id=1, source_target_pairs={{0,2},{3,1},{4,6},{7,5},{8,10},{11,9},{12,14},{15,13},{16,18},{19,... | collective-permute-start | bytes 3145736 | tf_op jit(solution)/shard_map/ppermute | solution.py:608
  93.4 192.1 %all-gather.8.cloned.1.call-start = ((), (), s32[]{:S(2)}) async-start(), calls=%async_computation.5 | async-start | bytes 9437184 | tf_op jit(solution)/shard_map/all_gather | solution.py:662
  133.5 17.0 %collective-permute-start.18 = (bf16[256,2048]{1,0:T(8,128)(2,1)}, bf16[256,2048]{1,0:T(8,128)(2,1)}, u32[]{:S(2)}, u32[]{:S(2)}) collective-permute-start(bf16[256,2048]{1,0:T(8,128)(2,1)} %get-tuple-element.134), channel_id=1, source_target_pairs={{1,3},{2,0},{5,7},{6,4},{9,11},{10,8},{13,15},{14,12},{17,19},{18,... | collective-permute-start | bytes 3145736 | tf_op jit(solution)/shard_map/ppermute | solution.py:608
  134.8 24.6 %collective-permute-start.19 = (bf16[256,2048]{1,0:T(8,128)(2,1)}, bf16[256,2048]{1,0:T(8,128)(2,1)S(1)}, u32[]{:S(2)}, u32[]{:S(2)}) collective-permute-start(bf16[256,2048]{1,0:T(8,128)(2,1)} %get-tuple-element.133), channel_id=1, source_target_pairs={{0,4},{1,5},{2,6},{3,7},{4,0},{5,1},{6,2},{7,3},{8,12},{9,13},{10,... | collective-permute-start | bytes 3145736 | tf_op jit(solution)/shard_map/ppermute | solution.py:608
  135.7 277.3 %reduce-scatter.4.cloned.1.call-start = ((), (), s32[]{:S(2)}) async-start(), calls=%async_computation.6 | async-start | bytes 9437184 | tf_op jit(solution)/shard_map/reduce_scatter | solution.py:666
  140.7 25.7 %collective-permute-start.21 = (bf16[256,2048]{1,0:T(8,128)(2,1)S(1)}, bf16[256,2048]{1,0:T(8,128)(2,1)S(1)}, u32[]{:S(2)}, u32[]{:S(2)}) collective-permute-start(bf16[256,2048]{1,0:T(8,128)(2,1)S(1)} %get-tuple-element.138.refs_3_), channel_id=1, source_target_pairs={{1,3},{2,0},{5,7},{6,4},{9,11},{10,8},{13,15},{14,12},{17,19},{18,... | collective-permute-start | bytes 3145736 | tf_op jit(solution)/shard_map/ppermute | solution.py:608
  161.4 16.8 %collective-permute-start.22 = (bf16[256,2048]{1,0:T(8,128)(2,1)S(1)}, bf16[256,2048]{1,0:T(8,128)(2,1)S(1)}, u32[]{:S(2)}, u32[]{:S(2)}) collective-permute-start(bf16[256,2048]{1,0:T(8,128)(2,1)S(1)} %add_convert_fusion.6), channel_id=1, source_target_pairs={{0,4},{3,7},{4,0},{7,3},{8,12},{11,15},{12,8},{15,11},{16,20},{19,... | collective-permute-start | bytes 3145736 | tf_op jit(solution)/shard_map/ppermute | solution.py:608
  165.1 16.7 %collective-permute-start.20 = (bf16[256,2048]{1,0:T(8,128)(2,1)S(1)}, bf16[256,2048]{1,0:T(8,128)(2,1)S(1)}, u32[]{:S(2)}, u32[]{:S(2)}) collective-permute-start(bf16[256,2048]{1,0:T(8,128)(2,1)S(1)} %add_convert_fusion.7), channel_id=1, source_target_pairs={{1,3},{2,0},{5,7},{6,4},{9,11},{10,8},{13,15},{14,12},{17,19},{18,... | collective-permute-start | bytes 3145736 | tf_op jit(solution)/shard_map/ppermute | solution.py:608
  186.1 18.5 %collective-permute-start.24 = (bf16[256,2048]{1,0:T(8,128)(2,1)S(1)}, bf16[256,2048]{1,0:T(8,128)(2,1)S(1)}, u32[]{:S(2)}, u32[]{:S(2)}) collective-permute-start(bf16[256,2048]{1,0:T(8,128)(2,1)S(1)} %get-tuple-element.141.refs_1_), channel_id=1, source_target_pairs={{0,4},{3,7},{4,0},{7,3},{8,12},{11,15},{12,8},{15,11},{16,20},{19,... | collective-permute-start | bytes 3145736 | tf_op jit(solution)/shard_map/ppermute | solution.py:608
  189.5 35.8 %collective-permute-start.23 = (bf16[256,2048]{1,0:T(8,128)(2,1)S(1)}, bf16[256,2048]{1,0:T(8,128)(2,1)S(1)}, u32[]{:S(2)}, u32[]{:S(2)}) collective-permute-start(bf16[256,2048]{1,0:T(8,128)(2,1)S(1)} %get-tuple-element.140.refs_0_), channel_id=1, source_target_pairs={{0,4},{3,7},{4,0},{7,3},{8,12},{11,15},{12,8},{15,11},{16,20},{19,... | collective-permute-start | bytes 3145736 | tf_op jit(solution)/shard_map/ppermute | solution.py:608
  192.7 32.6 %collective-permute-start.26 = (bf16[256,2048]{1,0:T(8,128)(2,1)S(1)}, bf16[256,2048]{1,0:T(8,128)(2,1)S(1)}, u32[]{:S(2)}, u32[]{:S(2)}) collective-permute-start(bf16[256,2048]{1,0:T(8,128)(2,1)S(1)} %get-tuple-element.141.refs_1_), channel_id=1, source_target_pairs={{0,2},{3,1},{4,6},{7,5},{8,10},{11,9},{12,14},{15,13},{16,18},{19,... | collective-permute-start | bytes 3145736 | tf_op jit(solution)/shard_map/ppermute | solution.py:608
  198.4 26.9 %collective-permute-start.27 = (bf16[256,2048]{1,0:T(8,128)(2,1)S(1)}, bf16[256,2048]{1,0:T(8,128)(2,1)S(1)}, u32[]{:S(2)}, u32[]{:S(2)}) collective-permute-start(bf16[256,2048]{1,0:T(8,128)(2,1)S(1)} %collective-permute-done.25.refs_4_), channel_id=1, source_target_pairs={{1,5},{2,6},{5,1},{6,2},{9,13},{10,14},{13,9},{14,10},{17,21},{18,... | collective-permute-start | bytes 3145736 | tf_op jit(solution)/shard_map/ppermute | solution.py:608
  204.6 20.7 %collective-permute-start.28 = (bf16[256,2048]{1,0:T(8,128)(2,1)S(1)}, bf16[256,2048]{1,0:T(8,128)(2,1)S(1)}, u32[]{:S(2)}, u32[]{:S(2)}) collective-permute-start(bf16[256,2048]{1,0:T(8,128)(2,1)S(1)} %collective-permute-done.24.refs_3_), channel_id=1, source_target_pairs={{0,2},{3,1},{4,6},{7,5},{8,10},{11,9},{12,14},{15,13},{16,18},{19,... | collective-permute-start | bytes 3145736 | tf_op jit(solution)/shard_map/ppermute | solution.py:608
  229.9 16.8 %collective-permute-start.30 = (bf16[256,2048]{1,0:T(8,128)(2,1)S(1)}, bf16[256,2048]{1,0:T(8,128)(2,1)}, u32[]{:S(2)}, u32[]{:S(2)}) collective-permute-start(bf16[256,2048]{1,0:T(8,128)(2,1)S(1)} %get-tuple-element.145.refs_1_), channel_id=1, source_target_pairs={{0,4},{3,7},{4,0},{7,3},{8,12},{11,15},{12,8},{15,11},{16,20},{19,... | collective-permute-start | bytes 3145736 | tf_op jit(solution)/shard_map/ppermute | solution.py:608
  232.7 36.1 %collective-permute-start.29 = (bf16[256,2048]{1,0:T(8,128)(2,1)}, bf16[256,2048]{1,0:T(8,128)(2,1)}, u32[]{:S(2)}, u32[]{:S(2)}) collective-permute-start(bf16[256,2048]{1,0:T(8,128)(2,1)} %get-tuple-element.144.refs_0_), channel_id=1, source_target_pairs={{0,4},{3,7},{4,0},{7,3},{8,12},{11,15},{12,8},{15,11},{16,20},{19,... | collective-permute-start | bytes 3145736 | tf_op jit(solution)/shard_map/ppermute | solution.py:608
  235.8 33.0 %collective-permute-start.32 = (bf16[256,2048]{1,0:T(8,128)(2,1)S(1)}, bf16[256,2048]{1,0:T(8,128)(2,1)}, u32[]{:S(2)}, u32[]{:S(2)}) collective-permute-start(bf16[256,2048]{1,0:T(8,128)(2,1)S(1)} %get-tuple-element.145.refs_1_), channel_id=1, source_target_pairs={{0,2},{3,1},{4,6},{7,5},{8,10},{11,9},{12,14},{15,13},{16,18},{19,... | collective-permute-start | bytes 3145736 | tf_op jit(solution)/shard_map/ppermute | solution.py:608
  241.6 27.2 %collective-permute-start.33 = (bf16[256,2048]{1,0:T(8,128)(2,1)}, bf16[256,2048]{1,0:T(8,128)(2,1)}, u32[]{:S(2)}, u32[]{:S(2)}) collective-permute-start(bf16[256,2048]{1,0:T(8,128)(2,1)} %collective-permute-done.31.refs_4_), channel_id=1, source_target_pairs={{1,5},{2,6},{5,1},{6,2},{9,13},{10,14},{13,9},{14,10},{17,21},{18,... | collective-permute-start | bytes 3145736 | tf_op jit(solution)/shard_map/ppermute | solution.py:608
  246.7 22.1 %collective-permute-start.34 = (bf16[256,2048]{1,0:T(8,128)(2,1)}, bf16[256,2048]{1,0:T(8,128)(2,1)}, u32[]{:S(2)}, u32[]{:S(2)}) collective-permute-start(bf16[256,2048]{1,0:T(8,128)(2,1)} %collective-permute-done.30.refs_3_), channel_id=1, source_target_pairs={{0,2},{3,1},{4,6},{7,5},{8,10},{11,9},{12,14},{15,13},{16,18},{19,... | collective-permute-start | bytes 3145736 | tf_op jit(solution)/shard_map/ppermute | solution.py:608
  285.5 251.5 %reduce-scatter.8.cloned.1.call-start = ((), (), s32[]{:S(2)}) async-start(), calls=%async_computation.8 | async-start | bytes 9437184 | tf_op jit(solution)/shard_map/reduce_scatter | solution.py:666
  306.2 25.0 %collective-permute-start.35 = (bf16[256,2048]{1,0:T(8,128)(2,1)S(1)}, bf16[256,2048]{1,0:T(8,128)(2,1)S(1)}, u32[]{:S(2)}, u32[]{:S(2)}) collective-permute-start(bf16[256,2048]{1,0:T(8,128)(2,1)S(1)} %get-tuple-element.152), channel_id=1, source_target_pairs={{1,3},{2,0},{5,7},{6,4},{9,11},{10,8},{13,15},{14,12},{17,19},{18,... | collective-permute-start | bytes 3145736 | tf_op jit(solution)/shard_map/ppermute | solution.py:608
  307.5 24.7 %collective-permute-start.36 = (bf16[256,2048]{1,0:T(8,128)(2,1)S(1)}, bf16[256,2048]{1,0:T(8,128)(2,1)S(1)}, u32[]{:S(2)}, u32[]{:S(2)}) collective-permute-start(bf16[256,2048]{1,0:T(8,128)(2,1)S(1)} %get-tuple-element.153), channel_id=1, source_target_pairs={{0,4},{1,5},{2,6},{3,7},{4,0},{5,1},{6,2},{7,3},{8,12},{9,13},{10,... | collective-permute-start | bytes 3145736 | tf_op jit(solution)/shard_map/ppermute | solution.py:608
  317.2 22.5 %collective-permute-start.38 = (bf16[256,2048]{1,0:T(8,128)(2,1)}, bf16[256,2048]{1,0:T(8,128)(2,1)}, u32[]{:S(2)}, u32[]{:S(2)}) collective-permute-start(bf16[256,2048]{1,0:T(8,128)(2,1)} %get-tuple-element.161.refs_3_), channel_id=1, source_target_pairs={{1,3},{2,0},{5,7},{6,4},{9,11},{10,8},{13,15},{14,12},{17,19},{18,... | collective-permute-start | bytes 3145736 | tf_op jit(solution)/shard_map/ppermute | solution.py:608
  333.6 17.0 %collective-permute-start.39 = (bf16[256,2048]{1,0:T(8,128)(2,1)}, bf16[256,2048]{1,0:T(8,128)(2,1)}, u32[]{:S(2)}, u32[]{:S(2)}) collective-permute-start(bf16[256,2048]{1,0:T(8,128)(2,1)} %add_convert_fusion.4), channel_id=1, source_target_pairs={{0,4},{3,7},{4,0},{7,3},{8,12},{11,15},{12,8},{15,11},{16,20},{19,... | collective-permute-start | bytes 3145736 | tf_op jit(solution)/shard_map/ppermute | solution.py:608
  338.1 17.0 %collective-permute-start.37 = (bf16[256,2048]{1,0:T(8,128)(2,1)}, bf16[256,2048]{1,0:T(8,128)(2,1)}, u32[]{:S(2)}, u32[]{:S(2)}) collective-permute-start(bf16[256,2048]{1,0:T(8,128)(2,1)} %add_convert_fusion.5), channel_id=1, source_target_pairs={{1,3},{2,0},{5,7},{6,4},{9,11},{10,8},{13,15},{14,12},{17,19},{18,... | collective-permute-start | bytes 3145736 | tf_op jit(solution)/shard_map/ppermute | solution.py:608
  339.4 230.1 %reduce-scatter.6.cloned.1.call-start = ((), (), s32[]{:S(2)}) async-start(), calls=%async_computation.7 | async-start | bytes 9437184 | tf_op jit(solution)/shard_map/reduce_scatter | solution.py:666
  369.2 20.3 %collective-permute-start.41 = (bf16[256,2048]{1,0:T(8,128)(2,1)S(1)}, bf16[256,2048]{1,0:T(8,128)(2,1)S(1)}, u32[]{:S(2)}, u32[]{:S(2)}) collective-permute-start(bf16[256,2048]{1,0:T(8,128)(2,1)S(1)} %get-tuple-element.166.refs_1_), channel_id=1, source_target_pairs={{0,4},{3,7},{4,0},{7,3},{8,12},{11,15},{12,8},{15,11},{16,20},{19,... | collective-permute-start | bytes 3145736 | tf_op jit(solution)/shard_map/ppermute | solution.py:608
  372.1 36.3 %collective-permute-start.40 = (bf16[256,2048]{1,0:T(8,128)(2,1)S(1)}, bf16[256,2048]{1,0:T(8,128)(2,1)S(1)}, u32[]{:S(2)}, u32[]{:S(2)}) collective-permute-start(bf16[256,2048]{1,0:T(8,128)(2,1)S(1)} %get-tuple-element.165.refs_0_), channel_id=1, source_target_pairs={{0,4},{3,7},{4,0},{7,3},{8,12},{11,15},{12,8},{15,11},{16,20},{19,... | collective-permute-start | bytes 3145736 | tf_op jit(solution)/shard_map/ppermute | solution.py:608
  375.1 33.3 %collective-permute-start.43 = (bf16[256,2048]{1,0:T(8,128)(2,1)S(1)}, bf16[256,2048]{1,0:T(8,128)(2,1)S(1)}, u32[]{:S(2)}, u32[]{:S(2)}) collective-permute-start(bf16[256,2048]{1,0:T(8,128)(2,1)S(1)} %get-tuple-element.166.refs_1_), channel_id=1, source_target_pairs={{0,2},{3,1},{4,6},{7,5},{8,10},{11,9},{12,14},{15,13},{16,18},{19,... | collective-permute-start | bytes 3145736 | tf_op jit(solution)/shard_map/ppermute | solution.py:608
  384.2 24.2 %collective-permute-start.44 = (bf16[256,2048]{1,0:T(8,128)(2,1)S(1)}, bf16[256,2048]{1,0:T(8,128)(2,1)S(1)}, u32[]{:S(2)}, u32[]{:S(2)}) collective-permute-start(bf16[256,2048]{1,0:T(8,128)(2,1)S(1)} %collective-permute-done.42.refs_4_), channel_id=1, source_target_pairs={{1,5},{2,6},{5,1},{6,2},{9,13},{10,14},{13,9},{14,10},{17,21},{18,... | collective-permute-start | bytes 3145736 | tf_op jit(solution)/shard_map/ppermute | solution.py:608
  389.5 18.9 %collective-permute-start.45 = (bf16[256,2048]{1,0:T(8,128)(2,1)S(1)}, bf16[256,2048]{1,0:T(8,128)(2,1)S(1)}, u32[]{:S(2)}, u32[]{:S(2)}) collective-permute-start(bf16[256,2048]{1,0:T(8,128)(2,1)S(1)} %collective-permute-done.41.refs_3_), channel_id=1, source_target_pairs={{0,2},{3,1},{4,6},{7,5},{8,10},{11,9},{12,14},{15,13},{16,18},{19,... | collective-permute-start | bytes 3145736 | tf_op jit(solution)/shard_map/ppermute | solution.py:608
  410.7 17.0 %collective-permute-start.46 = (bf16[256,2048]{1,0:T(8,128)(2,1)}, bf16[256,2048]{1,0:T(8,128)(2,1)}, u32[]{:S(2)}, u32[]{:S(2)}) collective-permute-start(bf16[256,2048]{1,0:T(8,128)(2,1)} %get-tuple-element.174), channel_id=1, source_target_pairs={{1,3},{2,0},{5,7},{6,4},{9,11},{10,8},{13,15},{14,12},{17,19},{18,... | collective-permute-start | bytes 3145736 | tf_op jit(solution)/shard_map/ppermute | solution.py:608
  412.0 22.9 %collective-permute-start.47 = (bf16[256,2048]{1,0:T(8,128)(2,1)}, bf16[256,2048]{1,0:T(8,128)(2,1)}, u32[]{:S(2)}, u32[]{:S(2)}) collective-permute-start(bf16[256,2048]{1,0:T(8,128)(2,1)} %get-tuple-element.175), channel_id=1, source_target_pairs={{0,4},{1,5},{2,6},{3,7},{4,0},{5,1},{6,2},{7,3},{8,12},{9,13},{10,... | collective-permute-start | bytes 3145736 | tf_op jit(solution)/shard_map/ppermute | solution.py:608
  448.4 46.7 %collective-permute-start.57 = (bf16[256,2048]{1,0:T(8,128)(2,1)}, bf16[256,2048]{1,0:T(8,128)(2,1)S(1)}, u32[]{:S(2)}, u32[]{:S(2)}) collective-permute-start(bf16[256,2048]{1,0:T(8,128)(2,1)} %copy-done.23), channel_id=1, source_target_pairs={{1,3},{2,0},{5,7},{6,4},{9,11},{10,8},{13,15},{14,12},{17,19},{18,... | collective-permute-start | bytes 3145736 | tf_op jit(solution)/shard_map/ppermute | solution.py:608
  451.7 44.8 %collective-permute-start.58 = (bf16[256,2048]{1,0:T(8,128)(2,1)S(1)}, bf16[256,2048]{1,0:T(8,128)(2,1)S(1)}, u32[]{:S(2)}, u32[]{:S(2)}) collective-permute-start(bf16[256,2048]{1,0:T(8,128)(2,1)S(1)} %add_convert_fusion), channel_id=1, source_target_pairs={{0,4},{3,7},{4,0},{7,3},{8,12},{11,15},{12,8},{15,11},{16,20},{19,... | collective-permute-start | bytes 3145736 | tf_op jit(solution)/shard_map/ppermute | solution.py:608
  456.8 39.7 %collective-permute-start.56 = (bf16[256,2048]{1,0:T(8,128)(2,1)S(1)}, bf16[256,2048]{1,0:T(8,128)(2,1)S(1)}, u32[]{:S(2)}, u32[]{:S(2)}) collective-permute-start(bf16[256,2048]{1,0:T(8,128)(2,1)S(1)} %add_convert_fusion.1), channel_id=1, source_target_pairs={{1,3},{2,0},{5,7},{6,4},{9,11},{10,8},{13,15},{14,12},{17,19},{18,... | collective-permute-start | bytes 3145736 | tf_op jit(solution)/shard_map/ppermute | solution.py:608
  464.3 23.5 %collective-permute-start.48 = (bf16[256,2048]{1,0:T(8,128)(2,1)S(1)}, bf16[256,2048]{1,0:T(8,128)(2,1)S(1)}, u32[]{:S(2)}, u32[]{:S(2)}) collective-permute-start(bf16[256,2048]{1,0:T(8,128)(2,1)S(1)} %get-tuple-element.183), channel_id=1, source_target_pairs={{1,3},{2,0},{5,7},{6,4},{9,11},{10,8},{13,15},{14,12},{17,19},{18,... | collective-permute-start | bytes 3145736 | tf_op jit(solution)/shard_map/ppermute | solution.py:608
  465.6 25.5 %collective-permute-start.49 = (bf16[256,2048]{1,0:T(8,128)(2,1)S(1)}, bf16[256,2048]{1,0:T(8,128)(2,1)S(1)}, u32[]{:S(2)}, u32[]{:S(2)}) collective-permute-start(bf16[256,2048]{1,0:T(8,128)(2,1)S(1)} %get-tuple-element.182), channel_id=1, source_target_pairs={{0,4},{1,5},{2,6},{3,7},{4,0},{5,1},{6,2},{7,3},{8,12},{9,13},{10,... | collective-permute-start | bytes 3145736 | tf_op jit(solution)/shard_map/ppermute | solution.py:608
  491.5 17.0 %collective-permute-start.52 = (bf16[256,2048]{1,0:T(8,128)(2,1)S(1)}, bf16[256,2048]{1,0:T(8,128)(2,1)S(1)}, u32[]{:S(2)}, u32[]{:S(2)}) collective-permute-start(bf16[256,2048]{1,0:T(8,128)(2,1)S(1)} %add_convert_fusion.2), channel_id=1, source_target_pairs={{0,4},{3,7},{4,0},{7,3},{8,12},{11,15},{12,8},{15,11},{16,20},{19,... | collective-permute-start | bytes 3145736 | tf_op jit(solution)/shard_map/ppermute | solution.py:608
  495.2 20.6 %collective-permute-start.50 = (bf16[256,2048]{1,0:T(8,128)(2,1)S(1)}, bf16[256,2048]{1,0:T(8,128)(2,1)S(1)}, u32[]{:S(2)}, u32[]{:S(2)}) collective-permute-start(bf16[256,2048]{1,0:T(8,128)(2,1)S(1)} %add_convert_fusion.3), channel_id=1, source_target_pairs={{1,3},{2,0},{5,7},{6,4},{9,11},{10,8},{13,15},{14,12},{17,19},{18,... | collective-permute-start | bytes 3145736 | tf_op jit(solution)/shard_map/ppermute | solution.py:608
  501.4 41.8 %collective-permute-start.59 = (bf16[512,2048]{1,0:T(8,128)(2,1)}, bf16[512,2048]{1,0:T(8,128)(2,1)}, u32[]{:S(2)}, u32[]{:S(2)}) collective-permute-start(bf16[512,2048]{1,0:T(8,128)(2,1)} %output.1), channel_id=1, source_target_pairs={{0,1},{3,2},{4,5},{7,6},{8,9},{11,10},{12,13},{15,14},{16,17},{19,... | collective-permute-start | bytes 6291464 | tf_op jit(solution)/shard_map/ppermute | solution.py:608
  520.8 45.6 %collective-permute-start.60 = (bf16[512,2048]{1,0:T(8,128)(2,1)}, bf16[512,2048]{1,0:T(8,128)(2,1)}, u32[]{:S(2)}, u32[]{:S(2)}) collective-permute-start(bf16[512,2048]{1,0:T(8,128)(2,1)} %get-tuple-element.200), channel_id=1, source_target_pairs={{0,1},{3,2},{4,5},{7,6},{8,9},{11,10},{12,13},{15,14},{16,17},{19,... | collective-permute-start | bytes 6291464 | tf_op jit(solution)/shard_map/ppermute | solution.py:608
  542.4 21.6 %collective-permute-start.55 = (bf16[128,2048]{1,0:T(8,128)(2,1)}, bf16[128,2048]{1,0:T(8,128)(2,1)S(1)}, u32[]{:S(2)}, u32[]{:S(2)}) collective-permute-start(bf16[128,2048]{1,0:T(8,128)(2,1)} %get-tuple-element.192), channel_id=1, source_target_pairs={{0,6},{1,7},{2,4},{3,5},{4,2},{5,3},{6,0},{7,1},{8,14},{9,15},{10,... | collective-permute-start | bytes 1572872 | tf_op jit(solution)/shard_map/ppermute | solution.py:608
  (83 other events, 908.4 us)
Sparse Core Ops, SparseCore 0:
  27.7 82.3 all-gather.3
  112.3 80.5 all-gather.5
  194.5 80.5 all-gather.7
  285.6 89.7 reduce-scatter.3
  377.5 87.9 reduce-scatter.7
  467.7 91.4 reduce-scatter.5

commit v5 on v4

--- a/solution.py
+++ b/solution.py
@@ -789,10 +789,8 @@
     placed = flat[6 * model :].reshape(2, 4 * inner)
     count = 4 * inner // (4 * depth)
     expand_bias_gradient = lax.dynamic_slice(placed, (ci, index * count), (1, count))
-    heads_part, reduce_gradient, expand_gradient, outputs, input_gradient, vectors, expand_bias_gradient = (
-        lax.optimization_barrier(
-            (heads_part, reduce_gradient, expand_gradient, outputs, input_gradient, vectors, expand_bias_gradient)
-        )
+    heads_part, reduce_gradient, expand_gradient, outputs = lax.optimization_barrier(
+        (heads_part, reduce_gradient, expand_gradient, outputs)
     )
     heads_got = shuffle(part_rows(plane_flag, heads_part))
     heads_gradient, output_gradient = place(plane_flag, heads_got, 1, F32, (3, 1))

time: 603 us -> 600 us (level)
  no operation moved by 1% of the time
where the time goes in v5:
time: 600 us; the launch traced here: 589 us
  waiting for transfers between devices  228 us (38%)
  Pallas kernels  187 us (31%)
  starting transfers between devices  116 us (19%)
  local copies, waits for them, and re-layouts  24.3 us (4%)
  other arithmetic  18.3 us (3%)
  between operations  16.1 us (3%)
    ppermute x67, waiting for transfers between devices, body(): send = lambda v, route: lax.ppermute(v, ALL, pairs_of(depth, route))  222 us
    ppermute x67, starting transfers between devices, body(): send = lambda v, route: lax.ppermute(v, ALL, pairs_of(depth, route))  111 us
    pallas_call x8, Pallas kernels, contract(): pl.pallas_call(contract_kernel, grid=(d // tile,), in_specs=[pl.BlockSpec...  52.1 us
    pallas_call x3, Pallas kernels, outer(): pl.pallas_call(functools.partial(outer_kernel, len(pairs), extra is not N...  39 us
    pallas_call x5, Pallas kernels, over_rows(): pl.pallas_call(functools.partial(kernel, m // 2 // TILE), grid=(m // TILE...  22.7 us
    pallas_call x1, Pallas kernels, expand(): pl.pallas_call(expand_kernel, grid=(sides, n // tile), in_specs=[pl.Block...  16.8 us
    unnamed x111, local copies, waits for them, and re-layouts  16.1 us
    pallas_call x2, Pallas kernels, project(): pl.pallas_call(project_kernel, grid=(sides,), in_specs=[pl.BlockSpec((m,...  15.3 us
  transfers between devices with their start and end apart: 75, of which 39 were waited for; matrix products, arithmetic and copies ran while one was open for 4% of the time, Pallas kernels for 31%

profile of v5, /device:TPU:0, one launch (start us, length us, event | category | flops | bytes accessed | tf_op | source)
XLA Modules:
  0.0 589.4 jit_solution(16504394830763545472)
XLA Ops:
  14.2 5.6 collective-permute-done.refs_1_
  19.8 6.2 %collective-permute-done.1.refs_2_ = bf16[128,1024]{1,0:T(8,128)(2,1)S(1)} collective-permute-done((bf16[128,1024]{1,0:T(8,128)(2,1)S(1)}, bf16[128,1024]{1,0:T(8,128)(2,1)S(1)}, u32[]{:S(2)}, u32[]{:S(2)}) %collective-permute-start.1) | collective-permute-done | bytes 262176 | tf_op jit(solution)/shard_map/ppermute | solution.py:608
  30.2 4.2 collective-permute-start.5
  47.3 5.7 collective-permute-done.4.refs_3_
  56.6 17.3 %collective-permute-done.3.refs_2_ = bf16[256,2048]{1,0:T(8,128)(2,1)} collective-permute-done((bf16[256,2048]{1,0:T(8,128)(2,1)S(1)}, bf16[256,2048]{1,0:T(8,128)(2,1)}, u32[]{:S(2)}, u32[]{:S(2)}) %collective-permute-start.3) | collective-permute-done | bytes 1048608 | tf_op jit(solution)/shard_map/ppermute | solution.py:608
  81.6 9.1 %collective-permute-done.10.refs_2_ = bf16[128,1024]{1,0:T(8,128)(2,1)S(1)} collective-permute-done((bf16[128,1024]{1,0:T(8,128)(2,1)S(1)}, bf16[128,1024]{1,0:T(8,128)(2,1)S(1)}, u32[]{:S(2)}, u32[]{:S(2)}) %collective-permute-start.10) | collective-permute-done | bytes 262176 | tf_op jit(solution)/shard_map/ppermute | solution.py:608
  101.7 9.9 %collective-permute-done.17 = s32[512,8]{0,1:T(8,128)S(1)} collective-permute-done((s32[512,8]{0,1:T(8,128)S(1)}, s32[512,8]{0,1:T(8,128)S(1)}, u32[]{:S(2)}, u32[]{:S(2)}) %collective-permute-start.17) | collective-permute-done | bytes 16416 | tf_op jit(solution)/shard_map/ppermute | solution.py:608
  114.2 10.0 %project.2.p_ref = bf16[2,1024,768]{2,1,0:T(8,128)(2,1)S(1)} custom-call(bf16[1024,2048]{1,0:T(8,128)(2,1)} %copy-done.7, bf16[2,2048,1024]{2,1,0:T(8,128)(2,1)} %bitcast.85), custom_call_target="tpu_custom_call" | custom-call | flops 25769803776 | bytes 54525952 | tf_op jit(solution)/shard_map/project/pallas_call | solution.py:192
  124.2 4.3 attend.1
  128.5 5.0 contract.8
  137.0 3.7 contract.9
  142.0 8.5 %collective-permute-done.18 = bf16[256,2048]{1,0:T(8,128)(2,1)} collective-permute-done((bf16[256,2048]{1,0:T(8,128)(2,1)}, bf16[256,2048]{1,0:T(8,128)(2,1)}, u32[]{:S(2)}, u32[]{:S(2)}) %collective-permute-start.18) | collective-permute-done | bytes 1048608 | tf_op jit(solution)/shard_map/ppermute | solution.py:608
  150.5 8.9 %collective-permute-done.19.refs_2_ = bf16[256,2048]{1,0:T(8,128)(2,1)S(1)} collective-permute-done((bf16[256,2048]{1,0:T(8,128)(2,1)}, bf16[256,2048]{1,0:T(8,128)(2,1)S(1)}, u32[]{:S(2)}, u32[]{:S(2)}) %collective-permute-start.19) | collective-permute-done | bytes 1048608 | tf_op jit(solution)/shard_map/ppermute | solution.py:608
  166.5 11.8 %collective-permute-done.22.refs_5_ = bf16[256,2048]{1,0:T(8,128)(2,1)S(1)} collective-permute-done((bf16[256,2048]{1,0:T(8,128)(2,1)S(1)}, bf16[256,2048]{1,0:T(8,128)(2,1)S(1)}, u32[]{:S(2)}, u32[]{:S(2)}) %collective-permute-start.22) | collective-permute-done | bytes 1048608 | tf_op jit(solution)/shard_map/ppermute | solution.py:608
  178.3 3.5 collective-permute-done.20.refs_1_
  194.2 4.2 collective-permute-done.25.refs_4_
  199.1 5.5 collective-permute-done.24.refs_3_
  207.6 17.7 %collective-permute-done.23.refs_2_ = bf16[256,2048]{1,0:T(8,128)(2,1)S(1)} collective-permute-done((bf16[256,2048]{1,0:T(8,128)(2,1)S(1)}, bf16[256,2048]{1,0:T(8,128)(2,1)S(1)}, u32[]{:S(2)}, u32[]{:S(2)}) %collective-permute-start.23) | collective-permute-done | bytes 1048608 | tf_op jit(solution)/shard_map/ppermute | solution.py:608
  238.1 3.5 collective-permute-done.31.refs_4_
  249.7 16.8 %expand.1 = (bf16[2,1024,1024]{2,1,0:T(8,128)(2,1)S(1)}, f32[2,1024,1024]{2,1,0:T(8,128)S(1)}) custom-call(bf16[1024,2048]{1,0:T(8,128)(2,1)} %copy-done.9, bf16[2,2048,1024]{2,1,0:T(8,128)(2,1)} %bitcast.91, f32[2,1,1024]{2,1,0:T(1,128)S(1)} %fusion.b_ref), custom_call_target="tpu_custom_call" | custom-call | flops 34359738368 | bytes 100663296 | tf_op jit(solution)/shard_map/expand/pallas_call | solution.py:220
  268.8 3.8 assemble.6.refs_0_.a_ref
  272.7 12.8 %outer.3 = bf16[4,2,512,1024]{3,2,1,0:T(8,128)(2,1)} custom-call(s32[2]{0:T(128)S(1)} %iota.48.pick_ref, bf16[1024,2048]{1,0:T(8,128)(2,1)S(1)} %assemble.6.refs_0_.a_ref, bf16[2,1024,1024]{2,1,0:T(8,128)(2,1)S(1)} %get-tuple-element.164.refs_1_.a_ref), custom_call_target="tpu_custom_call" | custom-call | flops 68719476736 | bytes 134217728 | tf_op jit(solution)/shard_map/outer/pallas_call | solution.py:324
  285.6 13.3 %expand_back.1 = (bf16[2,1024,1024]{2,1,0:T(8,128)(2,1)S(1)}, f32[2,1,1024]{2,1,0:T(1,128)S(1)}) custom-call(bf16[1024,2048]{1,0:T(8,128)(2,1)} %copy-done.13, bf16[2,2048,1024]{2,1,0:T(8,128)(2,1)} %bitcast.94, f32[2,1024,1024]{2,1,0:T(8,128)} %copy-done.38), custom_call_target="tpu_custom_call" | custom-call | flops 34359738368 | bytes 100663296 | tf_op jit(solution)/shard_map/expand_back/pallas_call | solution.py:248
  298.9 7.3 %contract.11 = (bf16[256,2048]{1,0:T(8,128)(2,1)S(1)}, bf16[256,2048]{1,0:T(8,128)(2,1)S(1)}) custom-call(bf16[2,1024,1024]{2,1,0:T(8,128)(2,1)S(1)} %get-tuple-element.152.a_ref.refs_1_, bf16[2,2048,1024]{2,1,0:T(8,128)(2,1)} %bitcast.92), custom_call_target="tpu_custom_call" | custom-call | flops 17179869184 | bytes 50331648 | tf_op jit(solution)/shard_map/contract/pallas_call | solution.py:281
  309.2 8.0 %contract.10 = (bf16[256,2048]{1,0:T(8,128)(2,1)S(1)}, bf16[256,2048]{1,0:T(8,128)(2,1)}) custom-call(bf16[2,1024,1024]{2,1,0:T(8,128)(2,1)S(1)} %get-tuple-element.152.a_ref.refs_1_, bf16[2,2048,1024]{2,1,0:T(8,128)(2,1)} %bitcast.93), custom_call_target="tpu_custom_call" | custom-call | flops 17179869184 | bytes 50331648 | tf_op jit(solution)/shard_map/contract/pallas_call | solution.py:281
  318.5 12.8 %outer.4 = bf16[4,2,512,1024]{3,2,1,0:T(8,128)(2,1)} custom-call(s32[2]{0:T(128)S(1)} %iota.49.pick_ref, bf16[1024,2048]{1,0:T(8,128)(2,1)S(1)} %copy-done.10, bf16[2,1024,1024]{2,1,0:T(8,128)(2,1)S(1)} %get-tuple-element.152.a_ref.refs_1_), custom_call_target="tpu_custom_call" | custom-call | flops 68719476736 | bytes 134217728 | tf_op jit(solution)/shard_map/outer/pallas_call | solution.py:324
  339.7 10.9 %collective-permute-done.39.refs_5_ = bf16[256,2048]{1,0:T(8,128)(2,1)} collective-permute-done((bf16[256,2048]{1,0:T(8,128)(2,1)}, bf16[256,2048]{1,0:T(8,128)(2,1)}, u32[]{:S(2)}, u32[]{:S(2)}) %collective-permute-start.39) | collective-permute-done | bytes 1048608 | tf_op jit(solution)/shard_map/ppermute | solution.py:608
  350.6 4.5 collective-permute-done.37.refs_1_
  360.4 7.4 %middle_back.1 = (f32[512,2048]{1,0:T(8,128)S(1)}, f32[8,2048]{1,0:T(8,128)S(1)}, bf16[256,2048]{1,0:T(8,128)(2,1)S(1)}, bf16[256,2048]{1,0:T(8,128)(2,1)S(1)}) custom-call(bf16[256,2048]{1,0:T(8,128)(2,1)S(1)} %copy-done.17, bf16[256,2048]{1,0:T(8,128)(2,1)} %collective-permute-done.37.refs_1_, bf16[256,2048]{1,0:T(8,128)(2,1)S(1)} %collective-permute-done.36.refs_2_, ...), custom_call_target="tpu_custom_call" | custom-call | flops 83886080 | bytes 67108864 | tf_op jit(solution)/shard_map/middle_back/pallas_call | solution.py:461
  376.4 7.7 %contract.13 = (bf16[256,2048]{1,0:T(8,128)(2,1)S(1)}, bf16[256,2048]{1,0:T(8,128)(2,1)S(1)}) custom-call(bf16[2,1024,1024]{2,1,0:T(8,128)(2,1)S(1)} %copy-done.37, bf16[2,2048,1024]{2,1,0:T(8,128)(2,1)} %bitcast.95), custom_call_target="tpu_custom_call" | custom-call | flops 17179869184 | bytes 50331648 | tf_op jit(solution)/shard_map/contract/pallas_call | solution.py:281
  384.9 4.6 collective-permute-done.41.refs_3_
  390.9 8.1 %contract.12 = (bf16[256,2048]{1,0:T(8,128)(2,1)}, bf16[256,2048]{1,0:T(8,128)(2,1)}) custom-call(bf16[2,1024,1024]{2,1,0:T(8,128)(2,1)S(1)} %copy-done.37, bf16[2,2048,1024]{2,1,0:T(8,128)(2,1)} %bitcast.96), custom_call_target="tpu_custom_call" | custom-call | flops 17179869184 | bytes 50331648 | tf_op jit(solution)/shard_map/contract/pallas_call | solution.py:281
  398.9 9.4 %collective-permute-done.40.refs_2_ = bf16[256,2048]{1,0:T(8,128)(2,1)S(1)} collective-permute-done((bf16[256,2048]{1,0:T(8,128)(2,1)S(1)}, bf16[256,2048]{1,0:T(8,128)(2,1)S(1)}, u32[]{:S(2)}, u32[]{:S(2)}) %collective-permute-start.40) | collective-permute-done | bytes 1048608 | tf_op jit(solution)/shard_map/ppermute | solution.py:608
  413.1 5.3 project.3.g_ref
  418.4 7.3 %attend_back.1.refs_1_.a_ref = bf16[2,1024,768]{2,1,0:T(8,128)(2,1)S(1)} custom-call(s32[1024,8]{1,0:T(8,128)S(1)} %copy-done.26, bf16[2,1024,768]{2,1,0:T(8,128)(2,1)S(1)} %copy-done.40, bf16[2,1024,256]{2,1,0:T(8,128)(2,1)S(1)} %project.3.g_ref, f32[2,1024,256]{2,1,0:T(8,128)S(1)} %copy-done.42), custom_call_target="tpu_custom_call" | custom-call | flops 64424509440 | bytes 100663296 | tf_op jit(solution)/shard_map/attend_back/pallas_call | solution.py:163
  427.7 7.2 %collective-permute-done.47.refs_2_ = bf16[256,2048]{1,0:T(8,128)(2,1)} collective-permute-done((bf16[256,2048]{1,0:T(8,128)(2,1)}, bf16[256,2048]{1,0:T(8,128)(2,1)}, u32[]{:S(2)}, u32[]{:S(2)}) %collective-permute-start.47) | collective-permute-done | bytes 1048608 | tf_op jit(solution)/shard_map/ppermute | solution.py:608
  435.0 13.4 %outer.5 = bf16[4,2,512,1024]{3,2,1,0:T(8,128)(2,1)} custom-call(s32[2]{0:T(128)S(1)} %iota.42.pick_ref, bf16[1024,2048]{1,0:T(8,128)(2,1)S(1)} %copy-done.8, bf16[2,1024,768]{2,1,0:T(8,128)(2,1)S(1)} %attend_back.1.refs_1_.a_ref, bf16[1024,2048]{1,0:T(8,128)(2,1)S(1)} %copy-done.12, bf16[2,1024,256]{2,1,0:T(8,128)(2,1)S(1)} %copy-done.33), custom_call_target="tpu_custom_call" | custom-call | flops 68719476736 | bytes 134217728 | tf_op jit(solution)/shard_map/outer/pallas_call | solution.py:324
  458.1 6.2 %contract.14 = (bf16[256,2048]{1,0:T(8,128)(2,1)S(1)}, bf16[256,2048]{1,0:T(8,128)(2,1)S(1)}) custom-call(bf16[2,1024,768]{2,1,0:T(8,128)(2,1)S(1)} %copy-done.35, bf16[2,2048,1024]{2,1,0:T(8,128)(2,1)} %bitcast.89), custom_call_target="tpu_custom_call" | custom-call | flops 12884901888 | bytes 39845888 | tf_op jit(solution)/shard_map/contract/pallas_call | solution.py:281
  466.6 6.1 %contract.15 = (bf16[256,2048]{1,0:T(8,128)(2,1)S(1)}, bf16[256,2048]{1,0:T(8,128)(2,1)S(1)}) custom-call(bf16[2,1024,768]{2,1,0:T(8,128)(2,1)S(1)} %copy-done.35, bf16[2,2048,1024]{2,1,0:T(8,128)(2,1)} %bitcast.90), custom_call_target="tpu_custom_call" | custom-call | flops 12884901888 | bytes 39845888 | tf_op jit(solution)/shard_map/contract/pallas_call | solution.py:281
  472.7 15.1 %collective-permute-done.48 = bf16[256,2048]{1,0:T(8,128)(2,1)S(1)} collective-permute-done((bf16[256,2048]{1,0:T(8,128)(2,1)S(1)}, bf16[256,2048]{1,0:T(8,128)(2,1)S(1)}, u32[]{:S(2)}, u32[]{:S(2)}) %collective-permute-start.48) | collective-permute-done | bytes 1048608 | tf_op jit(solution)/shard_map/ppermute | solution.py:608
  496.6 4.8 output.1
  504.5 4.0 collective-permute-done.52.refs_5_
  508.5 7.2 %collective-permute-done.50.refs_1_ = bf16[256,2048]{1,0:T(8,128)(2,1)S(1)} collective-permute-done((bf16[256,2048]{1,0:T(8,128)(2,1)S(1)}, bf16[256,2048]{1,0:T(8,128)(2,1)S(1)}, u32[]{:S(2)}, u32[]{:S(2)}) %collective-permute-start.50) | collective-permute-done | bytes 1048608 | tf_op jit(solution)/shard_map/ppermute | solution.py:608
  515.7 5.1 input_back.1
  526.2 4.7 collective-permute-done.62
  549.0 4.0 collective-permute-done.65
  554.7 9.3 %collective-permute-done.55.refs_3_ = bf16[128,2048]{1,0:T(8,128)(2,1)S(1)} collective-permute-done((bf16[128,2048]{1,0:T(8,128)(2,1)}, bf16[128,2048]{1,0:T(8,128)(2,1)S(1)}, u32[]{:S(2)}, u32[]{:S(2)}) %collective-permute-start.55) | collective-permute-done | bytes 524320 | tf_op jit(solution)/shard_map/ppermute | solution.py:608
  576.7 3.6 collective-permute-done.67.refs_2_
  (321 shorter events, 197.9 us)
Async XLA Ops:
  7.2 107.0 %all-gather.4.cloned.1.call-start = ((), (), s32[]{:S(2)}) async-start(), calls=%async_computation.3 | async-start | bytes 9437184 | tf_op jit(solution)/shard_map/all_gather | solution.py:662
  27.6 222.1 %all-gather.6.cloned.1.call-start = ((), (), s32[]{:S(2)}) async-start(), calls=%async_computation.4 | async-start | bytes 9437184 | tf_op jit(solution)/shard_map/all_gather | solution.py:662
  34.4 18.6 %collective-permute-start.4 = (bf16[256,2048]{1,0:T(8,128)(2,1)}, bf16[256,2048]{1,0:T(8,128)(2,1)}, u32[]{:S(2)}, u32[]{:S(2)}) collective-permute-start(bf16[256,2048]{1,0:T(8,128)(2,1)} %get-tuple-element.119.refs_1_), channel_id=1, source_target_pairs={{0,4},{3,7},{4,0},{7,3},{8,12},{11,15},{12,8},{15,11},{16,20},{19,... | collective-permute-start | bytes 3145736 | tf_op jit(solution)/shard_map/ppermute | solution.py:608
  37.1 36.7 %collective-permute-start.3 = (bf16[256,2048]{1,0:T(8,128)(2,1)S(1)}, bf16[256,2048]{1,0:T(8,128)(2,1)}, u32[]{:S(2)}, u32[]{:S(2)}) collective-permute-start(bf16[256,2048]{1,0:T(8,128)(2,1)S(1)} %get-tuple-element.118.refs_0_), channel_id=1, source_target_pairs={{0,4},{3,7},{4,0},{7,3},{8,12},{11,15},{12,8},{15,11},{16,20},{19,... | collective-permute-start | bytes 3145736 | tf_op jit(solution)/shard_map/ppermute | solution.py:608
  40.3 33.6 %collective-permute-start.6 = (bf16[256,2048]{1,0:T(8,128)(2,1)}, bf16[256,2048]{1,0:T(8,128)(2,1)}, u32[]{:S(2)}, u32[]{:S(2)}) collective-permute-start(bf16[256,2048]{1,0:T(8,128)(2,1)} %get-tuple-element.119.refs_1_), channel_id=1, source_target_pairs={{0,2},{3,1},{4,6},{7,5},{8,10},{11,9},{12,14},{15,13},{16,18},{19,... | collective-permute-start | bytes 3145736 | tf_op jit(solution)/shard_map/ppermute | solution.py:608
  45.7 28.2 %collective-permute-start.7 = (bf16[256,2048]{1,0:T(8,128)(2,1)}, bf16[256,2048]{1,0:T(8,128)(2,1)}, u32[]{:S(2)}, u32[]{:S(2)}) collective-permute-start(bf16[256,2048]{1,0:T(8,128)(2,1)} %collective-permute-done.5.refs_4_), channel_id=1, source_target_pairs={{1,5},{2,6},{5,1},{6,2},{9,13},{10,14},{13,9},{14,10},{17,21},{18,... | collective-permute-start | bytes 3145736 | tf_op jit(solution)/shard_map/ppermute | solution.py:608
  53.0 20.9 %collective-permute-start.8 = (bf16[256,2048]{1,0:T(8,128)(2,1)}, bf16[256,2048]{1,0:T(8,128)(2,1)}, u32[]{:S(2)}, u32[]{:S(2)}) collective-permute-start(bf16[256,2048]{1,0:T(8,128)(2,1)} %collective-permute-done.4.refs_3_), channel_id=1, source_target_pairs={{0,2},{3,1},{4,6},{7,5},{8,10},{11,9},{12,14},{15,13},{16,18},{19,... | collective-permute-start | bytes 3145736 | tf_op jit(solution)/shard_map/ppermute | solution.py:608
  93.4 192.1 %all-gather.8.cloned.1.call-start = ((), (), s32[]{:S(2)}) async-start(), calls=%async_computation.5 | async-start | bytes 9437184 | tf_op jit(solution)/shard_map/all_gather | solution.py:662
  133.5 17.0 %collective-permute-start.18 = (bf16[256,2048]{1,0:T(8,128)(2,1)}, bf16[256,2048]{1,0:T(8,128)(2,1)}, u32[]{:S(2)}, u32[]{:S(2)}) collective-permute-start(bf16[256,2048]{1,0:T(8,128)(2,1)} %get-tuple-element.131), channel_id=1, source_target_pairs={{1,3},{2,0},{5,7},{6,4},{9,11},{10,8},{13,15},{14,12},{17,19},{18,... | collective-permute-start | bytes 3145736 | tf_op jit(solution)/shard_map/ppermute | solution.py:608
  134.8 24.6 %collective-permute-start.19 = (bf16[256,2048]{1,0:T(8,128)(2,1)}, bf16[256,2048]{1,0:T(8,128)(2,1)S(1)}, u32[]{:S(2)}, u32[]{:S(2)}) collective-permute-start(bf16[256,2048]{1,0:T(8,128)(2,1)} %get-tuple-element.130), channel_id=1, source_target_pairs={{0,4},{1,5},{2,6},{3,7},{4,0},{5,1},{6,2},{7,3},{8,12},{9,13},{10,... | collective-permute-start | bytes 3145736 | tf_op jit(solution)/shard_map/ppermute | solution.py:608
  135.7 277.3 %reduce-scatter.4.cloned.1.call-start = ((), (), s32[]{:S(2)}) async-start(), calls=%async_computation.6 | async-start | bytes 9437184 | tf_op jit(solution)/shard_map/reduce_scatter | solution.py:666
  140.7 25.7 %collective-permute-start.21 = (bf16[256,2048]{1,0:T(8,128)(2,1)S(1)}, bf16[256,2048]{1,0:T(8,128)(2,1)S(1)}, u32[]{:S(2)}, u32[]{:S(2)}) collective-permute-start(bf16[256,2048]{1,0:T(8,128)(2,1)S(1)} %get-tuple-element.135.refs_3_), channel_id=1, source_target_pairs={{1,3},{2,0},{5,7},{6,4},{9,11},{10,8},{13,15},{14,12},{17,19},{18,... | collective-permute-start | bytes 3145736 | tf_op jit(solution)/shard_map/ppermute | solution.py:608
  161.4 16.8 %collective-permute-start.22 = (bf16[256,2048]{1,0:T(8,128)(2,1)S(1)}, bf16[256,2048]{1,0:T(8,128)(2,1)S(1)}, u32[]{:S(2)}, u32[]{:S(2)}) collective-permute-start(bf16[256,2048]{1,0:T(8,128)(2,1)S(1)} %add_convert_fusion.6), channel_id=1, source_target_pairs={{0,4},{3,7},{4,0},{7,3},{8,12},{11,15},{12,8},{15,11},{16,20},{19,... | collective-permute-start | bytes 3145736 | tf_op jit(solution)/shard_map/ppermute | solution.py:608
  165.1 16.7 %collective-permute-start.20 = (bf16[256,2048]{1,0:T(8,128)(2,1)S(1)}, bf16[256,2048]{1,0:T(8,128)(2,1)S(1)}, u32[]{:S(2)}, u32[]{:S(2)}) collective-permute-start(bf16[256,2048]{1,0:T(8,128)(2,1)S(1)} %add_convert_fusion.7), channel_id=1, source_target_pairs={{1,3},{2,0},{5,7},{6,4},{9,11},{10,8},{13,15},{14,12},{17,19},{18,... | collective-permute-start | bytes 3145736 | tf_op jit(solution)/shard_map/ppermute | solution.py:608
  186.1 18.5 %collective-permute-start.24 = (bf16[256,2048]{1,0:T(8,128)(2,1)S(1)}, bf16[256,2048]{1,0:T(8,128)(2,1)S(1)}, u32[]{:S(2)}, u32[]{:S(2)}) collective-permute-start(bf16[256,2048]{1,0:T(8,128)(2,1)S(1)} %get-tuple-element.138.refs_1_), channel_id=1, source_target_pairs={{0,4},{3,7},{4,0},{7,3},{8,12},{11,15},{12,8},{15,11},{16,20},{19,... | collective-permute-start | bytes 3145736 | tf_op jit(solution)/shard_map/ppermute | solution.py:608
  189.5 35.8 %collective-permute-start.23 = (bf16[256,2048]{1,0:T(8,128)(2,1)S(1)}, bf16[256,2048]{1,0:T(8,128)(2,1)S(1)}, u32[]{:S(2)}, u32[]{:S(2)}) collective-permute-start(bf16[256,2048]{1,0:T(8,128)(2,1)S(1)} %get-tuple-element.137.refs_0_), channel_id=1, source_target_pairs={{0,4},{3,7},{4,0},{7,3},{8,12},{11,15},{12,8},{15,11},{16,20},{19,... | collective-permute-start | bytes 3145736 | tf_op jit(solution)/shard_map/ppermute | solution.py:608
  192.7 32.6 %collective-permute-start.26 = (bf16[256,2048]{1,0:T(8,128)(2,1)S(1)}, bf16[256,2048]{1,0:T(8,128)(2,1)S(1)}, u32[]{:S(2)}, u32[]{:S(2)}) collective-permute-start(bf16[256,2048]{1,0:T(8,128)(2,1)S(1)} %get-tuple-element.138.refs_1_), channel_id=1, source_target_pairs={{0,2},{3,1},{4,6},{7,5},{8,10},{11,9},{12,14},{15,13},{16,18},{19,... | collective-permute-start | bytes 3145736 | tf_op jit(solution)/shard_map/ppermute | solution.py:608
  198.4 26.9 %collective-permute-start.27 = (bf16[256,2048]{1,0:T(8,128)(2,1)S(1)}, bf16[256,2048]{1,0:T(8,128)(2,1)S(1)}, u32[]{:S(2)}, u32[]{:S(2)}) collective-permute-start(bf16[256,2048]{1,0:T(8,128)(2,1)S(1)} %collective-permute-done.25.refs_4_), channel_id=1, source_target_pairs={{1,5},{2,6},{5,1},{6,2},{9,13},{10,14},{13,9},{14,10},{17,21},{18,... | collective-permute-start | bytes 3145736 | tf_op jit(solution)/shard_map/ppermute | solution.py:608
  204.6 20.7 %collective-permute-start.28 = (bf16[256,2048]{1,0:T(8,128)(2,1)S(1)}, bf16[256,2048]{1,0:T(8,128)(2,1)S(1)}, u32[]{:S(2)}, u32[]{:S(2)}) collective-permute-start(bf16[256,2048]{1,0:T(8,128)(2,1)S(1)} %collective-permute-done.24.refs_3_), channel_id=1, source_target_pairs={{0,2},{3,1},{4,6},{7,5},{8,10},{11,9},{12,14},{15,13},{16,18},{19,... | collective-permute-start | bytes 3145736 | tf_op jit(solution)/shard_map/ppermute | solution.py:608
  229.9 16.8 %collective-permute-start.30 = (bf16[256,2048]{1,0:T(8,128)(2,1)S(1)}, bf16[256,2048]{1,0:T(8,128)(2,1)}, u32[]{:S(2)}, u32[]{:S(2)}) collective-permute-start(bf16[256,2048]{1,0:T(8,128)(2,1)S(1)} %get-tuple-element.142.refs_1_), channel_id=1, source_target_pairs={{0,4},{3,7},{4,0},{7,3},{8,12},{11,15},{12,8},{15,11},{16,20},{19,... | collective-permute-start | bytes 3145736 | tf_op jit(solution)/shard_map/ppermute | solution.py:608
  232.7 36.1 %collective-permute-start.29 = (bf16[256,2048]{1,0:T(8,128)(2,1)}, bf16[256,2048]{1,0:T(8,128)(2,1)}, u32[]{:S(2)}, u32[]{:S(2)}) collective-permute-start(bf16[256,2048]{1,0:T(8,128)(2,1)} %get-tuple-element.141.refs_0_), channel_id=1, source_target_pairs={{0,4},{3,7},{4,0},{7,3},{8,12},{11,15},{12,8},{15,11},{16,20},{19,... | collective-permute-start | bytes 3145736 | tf_op jit(solution)/shard_map/ppermute | solution.py:608
  235.8 33.0 %collective-permute-start.32 = (bf16[256,2048]{1,0:T(8,128)(2,1)S(1)}, bf16[256,2048]{1,0:T(8,128)(2,1)}, u32[]{:S(2)}, u32[]{:S(2)}) collective-permute-start(bf16[256,2048]{1,0:T(8,128)(2,1)S(1)} %get-tuple-element.142.refs_1_), channel_id=1, source_target_pairs={{0,2},{3,1},{4,6},{7,5},{8,10},{11,9},{12,14},{15,13},{16,18},{19,... | collective-permute-start | bytes 3145736 | tf_op jit(solution)/shard_map/ppermute | solution.py:608
  241.6 27.2 %collective-permute-start.33 = (bf16[256,2048]{1,0:T(8,128)(2,1)}, bf16[256,2048]{1,0:T(8,128)(2,1)}, u32[]{:S(2)}, u32[]{:S(2)}) collective-permute-start(bf16[256,2048]{1,0:T(8,128)(2,1)} %collective-permute-done.31.refs_4_), channel_id=1, source_target_pairs={{1,5},{2,6},{5,1},{6,2},{9,13},{10,14},{13,9},{14,10},{17,21},{18,... | collective-permute-start | bytes 3145736 | tf_op jit(solution)/shard_map/ppermute | solution.py:608
  246.7 22.1 %collective-permute-start.34 = (bf16[256,2048]{1,0:T(8,128)(2,1)}, bf16[256,2048]{1,0:T(8,128)(2,1)}, u32[]{:S(2)}, u32[]{:S(2)}) collective-permute-start(bf16[256,2048]{1,0:T(8,128)(2,1)} %collective-permute-done.30.refs_3_), channel_id=1, source_target_pairs={{0,2},{3,1},{4,6},{7,5},{8,10},{11,9},{12,14},{15,13},{16,18},{19,... | collective-permute-start | bytes 3145736 | tf_op jit(solution)/shard_map/ppermute | solution.py:608
  285.5 251.5 %reduce-scatter.8.cloned.1.call-start = ((), (), s32[]{:S(2)}) async-start(), calls=%async_computation.8 | async-start | bytes 9437184 | tf_op jit(solution)/shard_map/reduce_scatter | solution.py:666
  306.2 25.0 %collective-permute-start.35 = (bf16[256,2048]{1,0:T(8,128)(2,1)S(1)}, bf16[256,2048]{1,0:T(8,128)(2,1)S(1)}, u32[]{:S(2)}, u32[]{:S(2)}) collective-permute-start(bf16[256,2048]{1,0:T(8,128)(2,1)S(1)} %get-tuple-element.149), channel_id=1, source_target_pairs={{1,3},{2,0},{5,7},{6,4},{9,11},{10,8},{13,15},{14,12},{17,19},{18,... | collective-permute-start | bytes 3145736 | tf_op jit(solution)/shard_map/ppermute | solution.py:608
  307.5 24.7 %collective-permute-start.36 = (bf16[256,2048]{1,0:T(8,128)(2,1)S(1)}, bf16[256,2048]{1,0:T(8,128)(2,1)S(1)}, u32[]{:S(2)}, u32[]{:S(2)}) collective-permute-start(bf16[256,2048]{1,0:T(8,128)(2,1)S(1)} %get-tuple-element.150), channel_id=1, source_target_pairs={{0,4},{1,5},{2,6},{3,7},{4,0},{5,1},{6,2},{7,3},{8,12},{9,13},{10,... | collective-permute-start | bytes 3145736 | tf_op jit(solution)/shard_map/ppermute | solution.py:608
  317.2 22.5 %collective-permute-start.38 = (bf16[256,2048]{1,0:T(8,128)(2,1)}, bf16[256,2048]{1,0:T(8,128)(2,1)}, u32[]{:S(2)}, u32[]{:S(2)}) collective-permute-start(bf16[256,2048]{1,0:T(8,128)(2,1)} %get-tuple-element.158.refs_3_), channel_id=1, source_target_pairs={{1,3},{2,0},{5,7},{6,4},{9,11},{10,8},{13,15},{14,12},{17,19},{18,... | collective-permute-start | bytes 3145736 | tf_op jit(solution)/shard_map/ppermute | solution.py:608
  333.6 17.0 %collective-permute-start.39 = (bf16[256,2048]{1,0:T(8,128)(2,1)}, bf16[256,2048]{1,0:T(8,128)(2,1)}, u32[]{:S(2)}, u32[]{:S(2)}) collective-permute-start(bf16[256,2048]{1,0:T(8,128)(2,1)} %add_convert_fusion.4), channel_id=1, source_target_pairs={{0,4},{3,7},{4,0},{7,3},{8,12},{11,15},{12,8},{15,11},{16,20},{19,... | collective-permute-start | bytes 3145736 | tf_op jit(solution)/shard_map/ppermute | solution.py:608
  338.1 17.0 %collective-permute-start.37 = (bf16[256,2048]{1,0:T(8,128)(2,1)}, bf16[256,2048]{1,0:T(8,128)(2,1)}, u32[]{:S(2)}, u32[]{:S(2)}) collective-permute-start(bf16[256,2048]{1,0:T(8,128)(2,1)} %add_convert_fusion.5), channel_id=1, source_target_pairs={{1,3},{2,0},{5,7},{6,4},{9,11},{10,8},{13,15},{14,12},{17,19},{18,... | collective-permute-start | bytes 3145736 | tf_op jit(solution)/shard_map/ppermute | solution.py:608
  339.4 227.0 %reduce-scatter.6.cloned.1.call-start = ((), (), s32[]{:S(2)}) async-start(), calls=%async_computation.7 | async-start | bytes 9437184 | tf_op jit(solution)/shard_map/reduce_scatter | solution.py:666
  369.2 20.3 %collective-permute-start.41 = (bf16[256,2048]{1,0:T(8,128)(2,1)S(1)}, bf16[256,2048]{1,0:T(8,128)(2,1)S(1)}, u32[]{:S(2)}, u32[]{:S(2)}) collective-permute-start(bf16[256,2048]{1,0:T(8,128)(2,1)S(1)} %get-tuple-element.163.refs_1_), channel_id=1, source_target_pairs={{0,4},{3,7},{4,0},{7,3},{8,12},{11,15},{12,8},{15,11},{16,20},{19,... | collective-permute-start | bytes 3145736 | tf_op jit(solution)/shard_map/ppermute | solution.py:608
  372.1 36.3 %collective-permute-start.40 = (bf16[256,2048]{1,0:T(8,128)(2,1)S(1)}, bf16[256,2048]{1,0:T(8,128)(2,1)S(1)}, u32[]{:S(2)}, u32[]{:S(2)}) collective-permute-start(bf16[256,2048]{1,0:T(8,128)(2,1)S(1)} %get-tuple-element.162.refs_0_), channel_id=1, source_target_pairs={{0,4},{3,7},{4,0},{7,3},{8,12},{11,15},{12,8},{15,11},{16,20},{19,... | collective-permute-start | bytes 3145736 | tf_op jit(solution)/shard_map/ppermute | solution.py:608
  375.1 33.3 %collective-permute-start.43 = (bf16[256,2048]{1,0:T(8,128)(2,1)S(1)}, bf16[256,2048]{1,0:T(8,128)(2,1)S(1)}, u32[]{:S(2)}, u32[]{:S(2)}) collective-permute-start(bf16[256,2048]{1,0:T(8,128)(2,1)S(1)} %get-tuple-element.163.refs_1_), channel_id=1, source_target_pairs={{0,2},{3,1},{4,6},{7,5},{8,10},{11,9},{12,14},{15,13},{16,18},{19,... | collective-permute-start | bytes 3145736 | tf_op jit(solution)/shard_map/ppermute | solution.py:608
  384.2 24.2 %collective-permute-start.44 = (bf16[256,2048]{1,0:T(8,128)(2,1)S(1)}, bf16[256,2048]{1,0:T(8,128)(2,1)S(1)}, u32[]{:S(2)}, u32[]{:S(2)}) collective-permute-start(bf16[256,2048]{1,0:T(8,128)(2,1)S(1)} %collective-permute-done.42.refs_4_), channel_id=1, source_target_pairs={{1,5},{2,6},{5,1},{6,2},{9,13},{10,14},{13,9},{14,10},{17,21},{18,... | collective-permute-start | bytes 3145736 | tf_op jit(solution)/shard_map/ppermute | solution.py:608
  389.5 18.9 %collective-permute-start.45 = (bf16[256,2048]{1,0:T(8,128)(2,1)S(1)}, bf16[256,2048]{1,0:T(8,128)(2,1)S(1)}, u32[]{:S(2)}, u32[]{:S(2)}) collective-permute-start(bf16[256,2048]{1,0:T(8,128)(2,1)S(1)} %collective-permute-done.41.refs_3_), channel_id=1, source_target_pairs={{0,2},{3,1},{4,6},{7,5},{8,10},{11,9},{12,14},{15,13},{16,18},{19,... | collective-permute-start | bytes 3145736 | tf_op jit(solution)/shard_map/ppermute | solution.py:608
  410.7 17.0 %collective-permute-start.46 = (bf16[256,2048]{1,0:T(8,128)(2,1)}, bf16[256,2048]{1,0:T(8,128)(2,1)}, u32[]{:S(2)}, u32[]{:S(2)}) collective-permute-start(bf16[256,2048]{1,0:T(8,128)(2,1)} %get-tuple-element.171), channel_id=1, source_target_pairs={{1,3},{2,0},{5,7},{6,4},{9,11},{10,8},{13,15},{14,12},{17,19},{18,... | collective-permute-start | bytes 3145736 | tf_op jit(solution)/shard_map/ppermute | solution.py:608
  412.0 22.9 %collective-permute-start.47 = (bf16[256,2048]{1,0:T(8,128)(2,1)}, bf16[256,2048]{1,0:T(8,128)(2,1)}, u32[]{:S(2)}, u32[]{:S(2)}) collective-permute-start(bf16[256,2048]{1,0:T(8,128)(2,1)} %get-tuple-element.172), channel_id=1, source_target_pairs={{0,4},{1,5},{2,6},{3,7},{4,0},{5,1},{6,2},{7,3},{8,12},{9,13},{10,... | collective-permute-start | bytes 3145736 | tf_op jit(solution)/shard_map/ppermute | solution.py:608
  448.4 46.7 %collective-permute-start.57 = (bf16[256,2048]{1,0:T(8,128)(2,1)}, bf16[256,2048]{1,0:T(8,128)(2,1)S(1)}, u32[]{:S(2)}, u32[]{:S(2)}) collective-permute-start(bf16[256,2048]{1,0:T(8,128)(2,1)} %copy-done.23), channel_id=1, source_target_pairs={{1,3},{2,0},{5,7},{6,4},{9,11},{10,8},{13,15},{14,12},{17,19},{18,... | collective-permute-start | bytes 3145736 | tf_op jit(solution)/shard_map/ppermute | solution.py:608
  451.7 44.8 %collective-permute-start.58 = (bf16[256,2048]{1,0:T(8,128)(2,1)S(1)}, bf16[256,2048]{1,0:T(8,128)(2,1)S(1)}, u32[]{:S(2)}, u32[]{:S(2)}) collective-permute-start(bf16[256,2048]{1,0:T(8,128)(2,1)S(1)} %add_convert_fusion), channel_id=1, source_target_pairs={{0,4},{3,7},{4,0},{7,3},{8,12},{11,15},{12,8},{15,11},{16,20},{19,... | collective-permute-start | bytes 3145736 | tf_op jit(solution)/shard_map/ppermute | solution.py:608
  456.8 39.7 %collective-permute-start.56 = (bf16[256,2048]{1,0:T(8,128)(2,1)S(1)}, bf16[256,2048]{1,0:T(8,128)(2,1)S(1)}, u32[]{:S(2)}, u32[]{:S(2)}) collective-permute-start(bf16[256,2048]{1,0:T(8,128)(2,1)S(1)} %add_convert_fusion.1), channel_id=1, source_target_pairs={{1,3},{2,0},{5,7},{6,4},{9,11},{10,8},{13,15},{14,12},{17,19},{18,... | collective-permute-start | bytes 3145736 | tf_op jit(solution)/shard_map/ppermute | solution.py:608
  464.3 23.5 %collective-permute-start.48 = (bf16[256,2048]{1,0:T(8,128)(2,1)S(1)}, bf16[256,2048]{1,0:T(8,128)(2,1)S(1)}, u32[]{:S(2)}, u32[]{:S(2)}) collective-permute-start(bf16[256,2048]{1,0:T(8,128)(2,1)S(1)} %get-tuple-element.180), channel_id=1, source_target_pairs={{1,3},{2,0},{5,7},{6,4},{9,11},{10,8},{13,15},{14,12},{17,19},{18,... | collective-permute-start | bytes 3145736 | tf_op jit(solution)/shard_map/ppermute | solution.py:608
  465.6 25.5 %collective-permute-start.49 = (bf16[256,2048]{1,0:T(8,128)(2,1)S(1)}, bf16[256,2048]{1,0:T(8,128)(2,1)S(1)}, u32[]{:S(2)}, u32[]{:S(2)}) collective-permute-start(bf16[256,2048]{1,0:T(8,128)(2,1)S(1)} %get-tuple-element.179), channel_id=1, source_target_pairs={{0,4},{1,5},{2,6},{3,7},{4,0},{5,1},{6,2},{7,3},{8,12},{9,13},{10,... | collective-permute-start | bytes 3145736 | tf_op jit(solution)/shard_map/ppermute | solution.py:608
  491.5 17.0 %collective-permute-start.52 = (bf16[256,2048]{1,0:T(8,128)(2,1)S(1)}, bf16[256,2048]{1,0:T(8,128)(2,1)S(1)}, u32[]{:S(2)}, u32[]{:S(2)}) collective-permute-start(bf16[256,2048]{1,0:T(8,128)(2,1)S(1)} %add_convert_fusion.2), channel_id=1, source_target_pairs={{0,4},{3,7},{4,0},{7,3},{8,12},{11,15},{12,8},{15,11},{16,20},{19,... | collective-permute-start | bytes 3145736 | tf_op jit(solution)/shard_map/ppermute | solution.py:608
  495.2 20.6 %collective-permute-start.50 = (bf16[256,2048]{1,0:T(8,128)(2,1)S(1)}, bf16[256,2048]{1,0:T(8,128)(2,1)S(1)}, u32[]{:S(2)}, u32[]{:S(2)}) collective-permute-start(bf16[256,2048]{1,0:T(8,128)(2,1)S(1)} %add_convert_fusion.3), channel_id=1, source_target_pairs={{1,3},{2,0},{5,7},{6,4},{9,11},{10,8},{13,15},{14,12},{17,19},{18,... | collective-permute-start | bytes 3145736 | tf_op jit(solution)/shard_map/ppermute | solution.py:608
  501.4 41.8 %collective-permute-start.59 = (bf16[512,2048]{1,0:T(8,128)(2,1)}, bf16[512,2048]{1,0:T(8,128)(2,1)}, u32[]{:S(2)}, u32[]{:S(2)}) collective-permute-start(bf16[512,2048]{1,0:T(8,128)(2,1)} %output.1), channel_id=1, source_target_pairs={{0,1},{3,2},{4,5},{7,6},{8,9},{11,10},{12,13},{15,14},{16,17},{19,... | collective-permute-start | bytes 6291464 | tf_op jit(solution)/shard_map/ppermute | solution.py:608
  520.8 50.6 %collective-permute-start.60 = (bf16[512,2048]{1,0:T(8,128)(2,1)}, bf16[512,2048]{1,0:T(8,128)(2,1)}, u32[]{:S(2)}, u32[]{:S(2)}) collective-permute-start(bf16[512,2048]{1,0:T(8,128)(2,1)} %get-tuple-element.198), channel_id=1, source_target_pairs={{0,1},{3,2},{4,5},{7,6},{8,9},{11,10},{12,13},{15,14},{16,17},{19,... | collective-permute-start | bytes 6291464 | tf_op jit(solution)/shard_map/ppermute | solution.py:608
  542.4 21.6 %collective-permute-start.55 = (bf16[128,2048]{1,0:T(8,128)(2,1)}, bf16[128,2048]{1,0:T(8,128)(2,1)S(1)}, u32[]{:S(2)}, u32[]{:S(2)}) collective-permute-start(bf16[128,2048]{1,0:T(8,128)(2,1)} %get-tuple-element.189), channel_id=1, source_target_pairs={{0,6},{1,7},{2,4},{3,5},{4,2},{5,3},{6,0},{7,1},{8,14},{9,15},{10,... | collective-permute-start | bytes 1572872 | tf_op jit(solution)/shard_map/ppermute | solution.py:608
  (83 other events, 908.4 us)
Sparse Core Ops, SparseCore 0:
  27.7 82.3 all-gather.3
  112.3 80.5 all-gather.5
  194.5 80.5 all-gather.7
  285.6 89.7 reduce-scatter.3
  377.5 87.9 reduce-scatter.7
  467.7 91.4 reduce-scatter.5
